TPU v7x, 512 devices: a whole 4x8x8 slice. The times are simulated.
512 devices in a mesh: dp: 4 (over z_hi, core), row: 4 (over z_lo), col: 32 (over x, y).
Axes of the slice: x: 4, y: 8, z: 8 (z_hi: 2, z_lo: 4; z = z_hi * 4 + z_lo), core: 2. Of those that a mesh axis runs over, the one named last changes fastest.
Arguments:
- tokens: bfloat16 [4, 128, 256, 256], P('dp', 'row', 'col'), may hold values from -6 to 6
- timesteps: int32 [4], P('dp'), may hold values from 0 to 999
- cotangent: bfloat16 [4, 128, 256, 256], P('dp', 'row', 'col'), may hold values from -6 to 6
- qkv_weight: bfloat16 [256, 768], replicated, may hold values from -0.375 to 0.375
- output_weight: bfloat16 [256, 256], replicated, may hold values from -0.375 to 0.375
- time_weight: bfloat16 [256, 256], replicated, may hold values from -0.375 to 0.375
Outputs:
- result: bfloat16 [4, 128, 256, 256], P('dp', 'row', 'col')
- grad_tokens: bfloat16 [4, 128, 256, 256], P('dp', 'row', 'col')
- grad_qkv: float32 [256, 768], replicated
- grad_output: float32 [256, 256], replicated
- grad_time: float32 [256, 256], replicated
All inputs are finite; a program needn't handle non-finite values.
Results may differ from a plain program's by a relative error of at most 0.0084.
Values may be sent and summed in bfloat16 or wider, within the bound.
No kernel may reach another device: no remote copies, remote signals or barrier semaphores. Data moves between devices by JAX's collectives and lax.ppermute only.
A program may use at most 64 MiB of HBM per device.

v0:
```python
import math

import jax
import jax.numpy as jnp
from jax import lax
from jax.sharding import PartitionSpec as P

HEAD_DIM = 64
CF = 256
RADIUS = 3
TILE_ROWS = 16


score_scale = 6.0
epsilon = 1e-06


def extended(block, sides, width):
    for axis, dim in sides:
        count = lax.axis_size(axis)
        forward = [(i, i + 1) for i in range(count - 1)]
        backward = [(target, source) for source, target in forward]
        low = lax.ppermute(
            lax.slice_in_dim(block, block.shape[dim] - width, None, axis=dim), axis, forward
        )
        high = lax.ppermute(lax.slice_in_dim(block, 0, width, axis=dim), axis, backward)
        block = jnp.concatenate([low, block, high], axis=dim)
    return block


def fourier(step_value):
    half_count = CF // 2
    ladder = jnp.arange(half_count, dtype=jnp.float32)
    frequency = jnp.exp(ladder * (-math.log(1000.0) / half_count))
    phase_angle = step_value.astype(jnp.float32) * frequency
    return jnp.concatenate([jnp.cos(phase_angle), jnp.sin(phase_angle)])


def norm_back(values, inverse, grad_normed, factor):
    inner_mean = jnp.mean(grad_normed * values, axis=-1, keepdims=True)
    return factor * inverse * (grad_normed - values * inverse * inverse * inner_mean)


def tile_mask(tile_start, row_first, col_first, tile_rows, breadth, total_rows, total_cols):
    padded_cols = breadth + 2 * RADIUS
    query_place = jnp.arange(tile_rows * breadth, dtype=jnp.int32)
    key_place = jnp.arange((tile_rows + 2 * RADIUS) * padded_cols, dtype=jnp.int32)
    query_row = (query_place // breadth)[:, None]
    query_col = (query_place % breadth)[:, None]
    key_row = (key_place // padded_cols)[None, :]
    key_col = (key_place % padded_cols)[None, :]
    nearby = (
        (key_row - query_row >= 0)
        & (key_row - query_row <= 2 * RADIUS)
        & (key_col - query_col >= 0)
        & (key_col - query_col <= 2 * RADIUS)
    )
    global_row = row_first + tile_start + key_row - RADIUS
    global_col = col_first + key_col - RADIUS
    inside = (
        (global_row >= 0)
        & (global_row < total_rows)
        & (global_col >= 0)
        & (global_col < total_cols)
    )
    return jnp.where(nearby & inside, 1.0, 0.0).astype(jnp.float32)


def tile_weights(query_tile, key_block, key_mask):
    scores = jnp.einsum("qhe,khe->hqk", query_tile, key_block, preferred_element_type=jnp.float32)
    exponent = jnp.exp(scores - score_scale) * key_mask[None]
    denominator = jnp.sum(exponent, axis=2, keepdims=True)
    return (exponent / denominator).astype(jnp.bfloat16)


def on_device(tokens, timesteps, cotangent, qkv_weight, output_weight, time_weight):
    picture = tokens[0]
    height, breadth, model_width = picture.shape
    head_count = model_width // HEAD_DIM
    tile_rows = TILE_ROWS
    tile_count = height // tile_rows
    query_count = tile_rows * breadth
    key_rows = tile_rows + 2 * RADIUS
    padded_cols = breadth + 2 * RADIUS
    key_count = key_rows * padded_cols
    row_first = lax.axis_index("row") * height
    col_first = lax.axis_index("col") * breadth
    total_rows = height * lax.axis_size("row")
    total_cols = breadth * lax.axis_size("col")
    features = fourier(timesteps[0])
    adaptive = 1.0 + jnp.dot(
        features, time_weight.astype(jnp.float32), precision=lax.Precision.HIGHEST
    )
    pixels = picture.astype(jnp.float32)
    inverse = lax.rsqrt(jnp.mean(pixels * pixels, axis=-1, keepdims=True) + epsilon)
    normed = (pixels * inverse * adaptive).astype(jnp.bfloat16)
    flat_normed = normed.reshape(height * breadth, model_width)
    project = jnp.dot(flat_normed, qkv_weight, preferred_element_type=jnp.float32)
    project = project.reshape(height, breadth, 3, head_count, HEAD_DIM)
    query_raw = project[:, :, 0]
    key_raw = project[:, :, 1]
    value_raw = project[:, :, 2]
    query_inv = lax.rsqrt(jnp.mean(query_raw * query_raw, axis=-1, keepdims=True) + epsilon)
    key_inv = lax.rsqrt(jnp.mean(key_raw * key_raw, axis=-1, keepdims=True) + epsilon)
    query_factor = score_scale / HEAD_DIM
    query_unit = (query_raw * query_inv * query_factor).astype(jnp.bfloat16)
    key_unit = (key_raw * key_inv).astype(jnp.bfloat16)
    value_unit = value_raw.astype(jnp.bfloat16)
    key_value = jnp.concatenate(
        [
            key_unit.reshape(height, breadth, model_width),
            value_unit.reshape(height, breadth, model_width),
        ],
        axis=-1,
    )
    key_value_pad = extended(key_value, (("row", 0), ("col", 1)), RADIUS)
    query_tiles = query_unit.reshape(tile_count, query_count, head_count, HEAD_DIM)

    def tile_inputs(tile_index):
        pair_block = lax.dynamic_slice_in_dim(key_value_pad, tile_index * tile_rows, key_rows, 0)
        pair_block = pair_block.reshape(key_count, 2, head_count, HEAD_DIM)
        key_mask = tile_mask(
            tile_index * tile_rows, row_first, col_first, tile_rows, breadth, total_rows, total_cols
        )
        return (pair_block[:, 0], pair_block[:, 1], key_mask)

    def forward_tile(tile_index):
        key_block, value_block, key_mask = tile_inputs(tile_index)
        weights = tile_weights(query_tiles[tile_index], key_block, key_mask)
        attended_tile = jnp.einsum(
            "hqk,khe->qhe", weights, value_block, preferred_element_type=jnp.float32
        )
        return attended_tile.astype(jnp.bfloat16).reshape(query_count, model_width)

    attended = lax.map(forward_tile, jnp.arange(tile_count, dtype=jnp.int32)).reshape(
        height * breadth, model_width
    )
    mixed_out = jnp.dot(attended, output_weight, preferred_element_type=jnp.float32)
    result = (pixels + mixed_out.reshape(height, breadth, model_width)).astype(jnp.bfloat16)
    flat_cotan = cotangent[0].reshape(height * breadth, model_width)
    grad_output = jnp.dot(attended.T, flat_cotan, preferred_element_type=jnp.float32)
    grad_attended = jnp.dot(flat_cotan, output_weight.T, preferred_element_type=jnp.float32).astype(
        jnp.bfloat16
    )
    grad_tiles = grad_attended.reshape(tile_count, query_count, head_count, HEAD_DIM)

    def backward_tile(grad_pad, tile_index):
        key_block, value_block, key_mask = tile_inputs(tile_index)
        query_tile = query_tiles[tile_index]
        grad_tile = grad_tiles[tile_index]
        weights = tile_weights(query_tile, key_block, key_mask)
        weight_wide = weights.astype(jnp.float32)
        slope_term = jnp.einsum(
            "qhe,khe->hqk", grad_tile, value_block, preferred_element_type=jnp.float32
        )
        middle = jnp.sum(weight_wide * slope_term, axis=2, keepdims=True)
        grad_score = (weight_wide * (slope_term - middle)).astype(jnp.bfloat16)
        grad_query = jnp.einsum(
            "hqk,khe->qhe", grad_score, key_block, preferred_element_type=jnp.float32
        )
        grad_key = jnp.einsum(
            "hqk,qhe->khe", grad_score, query_tile, preferred_element_type=jnp.float32
        )
        grad_value = jnp.einsum(
            "hqk,qhe->khe", weights, grad_tile, preferred_element_type=jnp.float32
        )
        tile_piece = jnp.concatenate(
            [grad_key.reshape(key_count, model_width), grad_value.reshape(key_count, model_width)],
            axis=-1,
        )
        tile_piece = tile_piece.reshape(key_rows, padded_cols, 2 * model_width)
        row_start = tile_index * tile_rows
        previous = lax.dynamic_slice_in_dim(grad_pad, row_start, key_rows, 0)
        grad_pad = lax.dynamic_update_slice_in_dim(grad_pad, previous + tile_piece, row_start, 0)
        return (grad_pad, grad_query)

    empty_pad = jnp.zeros((height + 2 * RADIUS, padded_cols, 2 * model_width), jnp.float32)
    grad_pad, grad_query_tiles = lax.scan(
        backward_tile, empty_pad, jnp.arange(tile_count, dtype=jnp.int32)
    )
    edge_rows = jnp.concatenate([grad_pad[:RADIUS], grad_pad[height + RADIUS :]], axis=0)
    received_rows = extended(edge_rows.astype(jnp.bfloat16), (("row", 0),), RADIUS).astype(
        edge_rows.dtype
    )
    inner_rows = grad_pad[RADIUS : height + RADIUS]
    inner_rows = inner_rows.at[:RADIUS].add(received_rows[:RADIUS])
    inner_rows = inner_rows.at[height - RADIUS :].add(received_rows[3 * RADIUS :])
    edge_cols = jnp.concatenate([inner_rows[:, :RADIUS], inner_rows[:, breadth + RADIUS :]], axis=1)
    received_cols = extended(edge_cols.astype(jnp.bfloat16), (("col", 1),), RADIUS).astype(
        edge_cols.dtype
    )
    own_cells = inner_rows[:, RADIUS : breadth + RADIUS]
    own_cells = own_cells.at[:, :RADIUS].add(received_cols[:, :RADIUS])
    own_cells = own_cells.at[:, breadth - RADIUS :].add(received_cols[:, 3 * RADIUS :])
    grad_key = own_cells[..., :model_width].reshape(height, breadth, head_count, HEAD_DIM)
    grad_value = own_cells[..., model_width:].reshape(height, breadth, head_count, HEAD_DIM)
    grad_query = grad_query_tiles.reshape(height, breadth, head_count, HEAD_DIM)
    grad_query_raw = norm_back(query_raw, query_inv, grad_query, query_factor)
    grad_key_raw = norm_back(key_raw, key_inv, grad_key, 1.0)
    grad_project = (
        jnp.stack([grad_query_raw, grad_key_raw, grad_value], axis=2)
        .reshape(height * breadth, 3 * model_width)
        .astype(jnp.bfloat16)
    )
    grad_qkv = jnp.dot(flat_normed.T, grad_project, preferred_element_type=jnp.float32)
    grad_normed = jnp.dot(grad_project, qkv_weight.T, preferred_element_type=jnp.float32).reshape(
        height, breadth, model_width
    )
    scaled = grad_normed * adaptive
    grad_pixels = norm_back(pixels, inverse, scaled, 1.0)
    grad_tokens = (cotangent[0].astype(jnp.float32) + grad_pixels).astype(jnp.bfloat16)
    grad_adaptive = jnp.sum(grad_normed * pixels * inverse, axis=(0, 1))
    grad_time = features[:, None] * grad_adaptive[None, :]
    reduced = lax.psum((grad_qkv, grad_output, grad_time), ("dp", "row", "col"))
    total_qkv, total_output, total_time = reduced
    return (result[None], grad_tokens[None], total_qkv, total_output, total_time)


def solution(mesh):
    in_specs = (P("dp", "row", "col", None), P("dp"), P("dp", "row", "col", None), P(), P(), P())
    out_specs = (P("dp", "row", "col", None), P("dp", "row", "col", None), P(), P(), P())
    return jax.shard_map(
        on_device, mesh=mesh, in_specs=in_specs, out_specs=out_specs, check_vma=False
    )
```

profile of v0, /device:TPU:1, one launch (start us, length us, event | category | flops | bytes accessed | tf_op | source)
XLA Modules:
  0.0 410.9 jit_solution(10312437559333469425)
XLA Ops:
  8.0 1.0 fusion.108
  9.1 1.0 fusion.76
  10.1 1.2 copy.77
  11.3 1.3 fusion.89
  15.6 4.8 %collective-permute-start = (bf16[3,8,512]{2,1,0:T(8,128)(2,1)S(1)}, bf16[3,8,512]{2,1,0:T(8,128)(2,1)S(1)}, u32[]{:S(2)}, u32[]{:S(2)}) collective-permute-start(bf16[3,8,512]{2,1,0:T(8,128)(2,1)S(1)} %get-tuple-element.476), channel_id=1, source_target_pairs={{0,32},{32,64},{64,96},{1,33},{33,65},{65,97},{2,34},{34,66},{66,9... | collective-permute-start | bytes 73736 | tf_op jit(solution)/shard_map/ppermute | solution.py:23
  20.4 1.3 collective-permute-start.1
  23.1 2.6 collective-permute-done.1
  25.8 3.2 collective-permute-start.2
  29.0 1.3 collective-permute-start.3
  33.2 1.8 collective-permute-done.3
  35.0 1.2 pad_maximum_fusion
  36.3 28.6 %while.33 = (s32[]{:T(128)}, f32[38,14,512]{2,1,0:T(8,128)S(1)}, f32[2,128,4,64]{1,3,2,0:T(8,128)}, s32[2]{0:T(128)S(1)}, bf16[2,128,4,64]{1,3,2,0:T(8,128)(2,1)...) while((s32[]{:T(128)}, f32[38,14,512]{2,1,0:T(8,128)S(1)}, ...), condition=%wide.region_9.10_spmd, body=%wide.region_6.9_spmd.sunk | while | flops 124238480 | bytes 19322752 | solution.py:178
  37.7 1.0 constant_dynamic-slice_fusion.5
  43.0 1.1 convolution_bitcast_fusion.6
  44.8 1.2 fusion.168
  46.0 1.1 convolution_bitcast_fusion.5
  47.1 1.3 copy.132
  52.0 1.0 constant_dynamic-slice_fusion.5
  57.3 1.1 convolution_bitcast_fusion.6
  59.1 1.2 fusion.168
  60.3 1.1 convolution_bitcast_fusion.5
  61.4 1.3 copy.132
  65.6 4.6 %collective-permute-start.4 = (bf16[3,14,512]{2,1,0:T(8,128)(2,1)S(1)}, bf16[3,14,512]{2,1,0:T(8,128)(2,1)}, u32[]{:S(2)}, u32[]{:S(2)}) collective-permute-start(bf16[3,14,512]{2,1,0:T(8,128)(2,1)S(1)} %get-tuple-element.470), channel_id=1, source_target_pairs={{0,32},{32,64},{64,96},{1,33},{33,65},{65,97},{2,34},{34,66},{66,9... | collective-permute-start | bytes 129032 | tf_op jit(solution)/shard_map/ppermute | solution.py:23
  70.2 1.3 collective-permute-start.5
  71.5 1.0 copy.91
  73.0 16.4 %while.32 = (s32[]{:T(128)}, bf16[2,128,256]{2,1,0:T(8,128)(2,1)}, s32[2]{0:T(128)}, bf16[38,14,512]{2,1,0:T(8,128)(2,1)}, bf16[2,128,4,64]{1,3,2,0:T(8,128)(2,1...) while((s32[]{:T(128)}, bf16[2,128,256]{2,1,0:T(8,128)(2,1)}, ...), condition=%wide.region_5.6_spmd, body=%wide.region_3.5_spmd.sunk | while | flops 41480536 | bytes 5906129 | solution.py:135
  73.0 1.3 dynamic_slice.97
  75.0 1.0 constant_dynamic-slice_fusion.4
  81.3 1.2 dynamic_slice.97
  83.2 1.0 constant_dynamic-slice_fusion.4
  89.4 1.9 fusion.93
  91.3 1.3 multiply_reduce_fusion
  92.7 0.8 fusion.98
  93.5 0.8 fusion.97
  94.6 3.2 collective-permute-start.6
  97.8 1.5 collective-permute-start.7
  100.1 4.2 %collective-permute-done.7 = bf16[32,3,512]{2,1,0:T(4,128)(2,1)S(1)} collective-permute-done((bf16[32,3,512]{2,1,0:T(4,128)(2,1)S(1)}, bf16[32,3,512]{2,1,0:T(4,128)(2,1)S(1)}, u32[]{:S(2)}, u32[]{:S(2)}) %collective-permute-start.7) | collective-permute-done | bytes 98336 | tf_op jit(solution)/shard_map/ppermute | solution.py:26
  104.6 1.1 scatter-add.16
  106.0 1.1 scatter-add.19
  107.4 1.0 reshape.608
  109.6 1.1 stack_reshape.3
  110.7 1.7 fusion.69
  113.9 1.3 fusion.91
  115.6 0.8 broadcast_multiply_fusion
  116.4 0.8 fusion.65
  117.3 0.8 fusion.88
  118.1 282.4 %all-reduce.3.cloned.1.call-done = (f32[256,768]{1,0:T(8,128)}, f32[256,256]{1,0:T(8,128)}, f32[256,256]{1,0:T(8,128)}) async-done(((f32[256,768]{1,0:T(8,128)}, f32[256,256]{1,0:T(8,128)}, f32[256,256]{1,0:T(8,128)}), (f32[256,768]{1,0:T(8,128)}, f32[256,256]{1,0:T(8,128)}, f32[256,256]{1,0:T(8,128)})) %all-reduce.3.cloned.1.call-update) | async-done | bytes 1310736 | tf_op jit(solution)/shard_map/psum | solution.py:214
  400.5 2.1 copy.161
  (206 shorter events, 32.9 us)
Async XLA Ops:
  7.2 23.1 %copy-start = (bf16[256,256]{1,0:T(8,128)(2,1)S(1)}, bf16[256,256]{1,0:T(8,128)(2,1)}, u32[]{:S(2)}) copy-start(bf16[256,256]{1,0:T(8,128)(2,1)} %param.22) | copy-start | bytes 393220
  7.2 393.3 %all-reduce.3.cloned.1.call-start = ((), (), s32[]{:S(2)}) async-start(), calls=%async_computation | async-start | bytes 2621440 | tf_op jit(solution)/shard_map/psum | solution.py:214
  8.0 1.1 copy-start.27
  9.1 3.5 copy-start.25
  12.6 1.2 copy-start.1
  15.6 7.5 %collective-permute-start = (bf16[3,8,512]{2,1,0:T(8,128)(2,1)S(1)}, bf16[3,8,512]{2,1,0:T(8,128)(2,1)S(1)}, u32[]{:S(2)}, u32[]{:S(2)}) collective-permute-start(bf16[3,8,512]{2,1,0:T(8,128)(2,1)S(1)} %get-tuple-element.476), channel_id=1, source_target_pairs={{0,32},{32,64},{64,96},{1,33},{33,65},{65,97},{2,34},{34,66},{66,9... | collective-permute-start | bytes 73736 | tf_op jit(solution)/shard_map/ppermute | solution.py:23
  20.4 5.2 %collective-permute-start.1 = (bf16[3,8,512]{2,1,0:T(8,128)(2,1)S(1)}, bf16[3,8,512]{2,1,0:T(8,128)(2,1)S(1)}, u32[]{:S(2)}, u32[]{:S(2)}) collective-permute-start(bf16[3,8,512]{2,1,0:T(8,128)(2,1)S(1)} %get-tuple-element.477), channel_id=1, source_target_pairs={{32,0},{64,32},{96,64},{33,1},{65,33},{97,65},{34,2},{66,34},{98,6... | collective-permute-start | bytes 73736 | tf_op jit(solution)/shard_map/ppermute | solution.py:26
  22.1 0.8 copy-start.5
  22.1 8.2 %copy-start.14 = (bf16[1,32,8,256]{3,2,1,0:T(8,128)(2,1)S(1)}, bf16[1,32,8,256]{3,2,1,0:T(8,128)(2,1)}, u32[]{:S(2)}) copy-start(bf16[1,32,8,256]{3,2,1,0:T(8,128)(2,1)} %param.20) | copy-start | bytes 393220
  25.8 7.4 %collective-permute-start.2 = (bf16[38,3,512]{2,1,0:T(4,128)(2,1)S(1)}, bf16[38,3,512]{2,1,0:T(4,128)(2,1)S(1)}, u32[]{:S(2)}, u32[]{:S(2)}) collective-permute-start(bf16[38,3,512]{2,1,0:T(4,128)(2,1)S(1)} %get-tuple-element.474), channel_id=1, source_target_pairs={{0,1},{1,2},{2,3},{3,4},{4,5},{5,6},{6,7},{7,8},{8,9},{9,10},{10,1... | collective-permute-start | bytes 350216 | tf_op jit(solution)/shard_map/ppermute | solution.py:23
  29.0 6.0 %collective-permute-start.3 = (bf16[38,3,512]{2,1,0:T(4,128)(2,1)S(1)}, bf16[38,3,512]{2,1,0:T(4,128)(2,1)S(1)}, u32[]{:S(2)}, u32[]{:S(2)}) collective-permute-start(bf16[38,3,512]{2,1,0:T(4,128)(2,1)S(1)} %get-tuple-element.475), channel_id=1, source_target_pairs={{1,0},{2,1},{3,2},{4,3},{5,4},{6,5},{7,6},{8,7},{9,8},{10,9},{11,1... | collective-permute-start | bytes 350216 | tf_op jit(solution)/shard_map/ppermute | solution.py:26
  36.3 6.2 %copy-start.10 = (bf16[2,128,4,64]{1,3,2,0:T(8,128)(2,1)}, bf16[2,128,4,64]{1,3,2,0:T(8,128)(2,1)S(1)}, u32[]{:S(2)}) copy-start(bf16[2,128,4,64]{1,3,2,0:T(8,128)(2,1)S(1)} %get-tuple-element.681) | copy-start | bytes 393220 | tf_op jit(solution)/shard_map/while
  36.3 6.6 %copy-start.3 = (bf16[2,128,4,64]{1,3,2,0:T(8,128)(2,1)}, bf16[2,128,4,64]{1,3,2,0:T(8,128)(2,1)S(1)}, u32[]{:S(2)}) copy-start(bf16[2,128,4,64]{1,3,2,0:T(8,128)(2,1)S(1)} %get-tuple-element.677) | copy-start | bytes 393220 | tf_op jit(solution)/shard_map/while
  44.4 1.6 copy-start.11
  48.7 1.0 copy-start.19
  48.8 1.9 copy-start.4
  48.8 1.8 copy-start.12
  49.9 0.7 copy-start.20
  50.6 6.2 %copy-start.10 = (bf16[2,128,4,64]{1,3,2,0:T(8,128)(2,1)}, bf16[2,128,4,64]{1,3,2,0:T(8,128)(2,1)S(1)}, u32[]{:S(2)}) copy-start(bf16[2,128,4,64]{1,3,2,0:T(8,128)(2,1)S(1)} %get-tuple-element.681) | copy-start | bytes 393220 | tf_op jit(solution)/shard_map/while
  50.6 6.6 %copy-start.3 = (bf16[2,128,4,64]{1,3,2,0:T(8,128)(2,1)}, bf16[2,128,4,64]{1,3,2,0:T(8,128)(2,1)S(1)}, u32[]{:S(2)}) copy-start(bf16[2,128,4,64]{1,3,2,0:T(8,128)(2,1)S(1)} %get-tuple-element.677) | copy-start | bytes 393220 | tf_op jit(solution)/shard_map/while
  58.7 1.6 copy-start.11
  63.0 1.0 copy-start.19
  63.0 1.9 copy-start.4
  63.0 1.8 copy-start.12
  64.2 0.7 copy-start.20
  64.9 6.6 %copy-start.21 = (f32[2,128,4,64]{1,3,2,0:T(8,128)S(1)}, f32[2,128,4,64]{1,3,2,0:T(8,128)}, u32[]{:S(2)}) copy-start(f32[2,128,4,64]{1,3,2,0:T(8,128)} %get-tuple-element.355) | copy-start | bytes 786436
  65.6 27.1 %collective-permute-start.4 = (bf16[3,14,512]{2,1,0:T(8,128)(2,1)S(1)}, bf16[3,14,512]{2,1,0:T(8,128)(2,1)}, u32[]{:S(2)}, u32[]{:S(2)}) collective-permute-start(bf16[3,14,512]{2,1,0:T(8,128)(2,1)S(1)} %get-tuple-element.470), channel_id=1, source_target_pairs={{0,32},{32,64},{64,96},{1,33},{33,65},{65,97},{2,34},{34,66},{66,9... | collective-permute-start | bytes 129032 | tf_op jit(solution)/shard_map/ppermute | solution.py:23
  70.2 22.5 %collective-permute-start.5 = (bf16[3,14,512]{2,1,0:T(8,128)(2,1)}, bf16[3,14,512]{2,1,0:T(8,128)(2,1)}, u32[]{:S(2)}, u32[]{:S(2)}) collective-permute-start(bf16[3,14,512]{2,1,0:T(8,128)(2,1)} %get-tuple-element.471), channel_id=1, source_target_pairs={{32,0},{64,32},{96,64},{33,1},{65,33},{97,65},{34,2},{66,34},{98,6... | collective-permute-start | bytes 129032 | tf_op jit(solution)/shard_map/ppermute | solution.py:26
  73.0 18.3 %copy-start.6 = (f32[32,8,1,4,64]{4,1,0,3,2:T(8,128)S(1)}, f32[32,8,1,4,64]{4,1,0,3,2:T(8,128)}, u32[]{:S(2)}) copy-start(f32[32,8,1,4,64]{4,1,0,3,2:T(8,128)} %copy-done.5) | copy-start | bytes 786436
  79.7 0.9 copy-start.16
  80.6 0.7 copy-start.17
  87.8 0.9 copy-start.16
  88.8 0.7 copy-start.17
  94.6 5.6 %collective-permute-start.6 = (bf16[32,3,512]{2,1,0:T(4,128)(2,1)S(1)}, bf16[32,3,512]{2,1,0:T(4,128)(2,1)S(1)}, u32[]{:S(2)}, u32[]{:S(2)}) collective-permute-start(bf16[32,3,512]{2,1,0:T(4,128)(2,1)S(1)} %get-tuple-element.472), channel_id=1, source_target_pairs={{0,1},{1,2},{2,3},{3,4},{4,5},{5,6},{6,7},{7,8},{8,9},{9,10},{10,1... | collective-permute-start | bytes 294920 | tf_op jit(solution)/shard_map/ppermute | solution.py:23
  97.8 6.6 %collective-permute-start.7 = (bf16[32,3,512]{2,1,0:T(4,128)(2,1)S(1)}, bf16[32,3,512]{2,1,0:T(4,128)(2,1)S(1)}, u32[]{:S(2)}, u32[]{:S(2)}) collective-permute-start(bf16[32,3,512]{2,1,0:T(4,128)(2,1)S(1)} %get-tuple-element.473), channel_id=1, source_target_pairs={{1,0},{2,1},{3,2},{4,3},{5,4},{6,5},{7,6},{8,7},{9,8},{10,9},{11,1... | collective-permute-start | bytes 294920 | tf_op jit(solution)/shard_map/ppermute | solution.py:26
  107.1 2.0 copy-start.2
  108.4 2.3 copy-start.7
  108.4 2.3 copy-start.22
  109.1 1.6 copy-start.9
  112.9 1.0 copy-start.8
  112.9 1.0 copy-start.26
  113.4 1.8 copy-start.13
  113.9 1.7 copy-start.28
  115.1 1.3 copy-start.18
  115.6 1.7 copy-start.15
  400.5 2.1 copy-start.24
  400.5 2.8 copy-start.23
Sparse Core Ops, SparseCore 0:
  116.5 283.9 all-reduce.2
where the time goes:
time: 414 us; the launch traced here: 411 us
  waiting for transfers between devices  291 us (70%)
  local copies, waits for them, and re-layouts  43.1 us (10%)
  starting transfers between devices  21.2 us (5%)
  matrix products  17.1 us (4%)
  between operations  15.4 us (4%)
  other arithmetic  11.9 us (3%)
  loops' own time  11.2 us (3%)
    psum x1, waiting for transfers between devices, on_device(): reduced = lax.psum((grad_qkv, grad_output, grad_time), ('dp', 'row', 'col'))  282 us
    ppermute x4, starting transfers between devices, extended(): lax.ppermute(lax.slice_in_dim(block, block.shape[dim] - width, None, axis...  15.8 us
    ppermute x4, waiting for transfers between devices, extended(): lax.ppermute(lax.slice_in_dim(block, 0, width, axis=dim), axis, backward)  8.58 us
  transfers between devices with their start and end apart: 9, of which 4 were waited for; matrix products, arithmetic and copies ran while one was open for 5% of the time, Pallas kernels for 0%

commit v1 on v0

--- a/solution.py
+++ b/solution.py
@@ -210,10 +210,43 @@
     grad_pixels = norm_back(pixels, inverse, scaled, 1.0)
     grad_tokens = (cotangent[0].astype(jnp.float32) + grad_pixels).astype(jnp.bfloat16)
     grad_adaptive = jnp.sum(grad_normed * pixels * inverse, axis=(0, 1))
-    grad_time = features[:, None] * grad_adaptive[None, :]
-    reduced = lax.psum((grad_qkv, grad_output, grad_time), ("dp", "row", "col"))
-    total_qkv, total_output, total_time = reduced
+    total_qkv, total_output, total_time = summed(grad_qkv, grad_output, grad_adaptive, timesteps[0])
     return (result[None], grad_tokens[None], total_qkv, total_output, total_time)
+
+
+def swap(pieces, axes):
+    return lax.all_to_all(pieces, axes, 0, 0, tiled=True)
+
+
+def summed(grad_qkv, grad_output, grad_adaptive, step_value):
+    width = grad_qkv.shape[1] + grad_output.shape[1]
+    rows = grad_qkv.shape[0]
+    images = lax.axis_size("dp")
+    parts = lax.axis_size("col")
+    others = lax.axis_size("dp") * lax.axis_size("row")
+    block = rows // parts
+    lanes = grad_adaptive.shape[0] * images // block
+    mine = (jnp.arange(images) == lax.axis_index("dp"))[:, None]
+    side = jnp.where(mine, grad_adaptive[None], 0.0).reshape(1, block, lanes)
+    high = (step_value // 32).astype(jnp.float32)
+    low = (step_value % 32).astype(jnp.float32)
+    steps = jnp.where(mine, jnp.stack([high, low])[None], 0.0).reshape(1, 1, 2 * images)
+    steps = jnp.pad(steps, ((0, 0), (0, block - 1), (0, lanes - 2 * images)))
+    side = jnp.pad(jnp.concatenate([side, steps], axis=0), ((0, parts - 2), (0, 0), (0, 0)))
+    whole = jnp.concatenate([grad_qkv, grad_output, side.reshape(rows, lanes)], axis=1)
+    pieces = whole.astype(jnp.bfloat16).reshape(parts, block, width + lanes)
+    piece = jnp.sum(swap(pieces, "col").astype(jnp.float32), axis=0).astype(jnp.bfloat16)
+    copies = lax.optimization_barrier(jnp.broadcast_to(piece[None], (others,) + piece.shape))
+    piece = jnp.sum(swap(copies, ("dp", "row")).astype(jnp.float32), axis=0).astype(jnp.bfloat16)
+    copies = lax.optimization_barrier(jnp.broadcast_to(piece[None], (parts,) + piece.shape))
+    whole = swap(copies, "col").astype(jnp.float32)
+    side = whole[:2, :, width:]
+    whole = whole.reshape(rows, width + lanes)
+    adaptives = side[0].reshape(images, grad_adaptive.shape[0])
+    steps = side[1, 0, : 2 * images].reshape(images, 2) / (parts * lax.axis_size("row"))
+    features = jax.vmap(fourier)(steps[:, 0] * 32.0 + steps[:, 1])
+    total_time = jnp.sum(features[:, :, None] * adaptives[:, None, :], axis=0)
+    return whole[:, : grad_qkv.shape[1]], whole[:, grad_qkv.shape[1] : width], total_time
 
 
 def solution(mesh):

time: 414 us -> 188 us (0.45)
  the two profiles are of different devices: /device:TPU:1 before, /device:TPU:72 now
where the time goes in v1:
time: 188 us; the launch traced here: 187 us
  local copies, waits for them, and re-layouts  44.6 us (24%)
  blocking collectives  43.6 us (23%)
  starting transfers between devices  29.9 us (16%)
  waiting for transfers between devices  27.2 us (14%)
  matrix products  15.9 us (8%)
  other arithmetic  13 us (7%)
  loops' own time  10.5 us (6%)
  between operations  2.14 us (1%)
    all_to_all x2, blocking collectives, swap(): return lax.all_to_all(pieces, axes, 0, 0, tiled=True)  43.6 us
    all_to_all x1, waiting for transfers between devices, swap(): return lax.all_to_all(pieces, axes, 0, 0, tiled=True)  18.2 us
    ppermute x4, starting transfers between devices, extended(): lax.ppermute(lax.slice_in_dim(block, block.shape[dim] - width, None, axis...  16.7 us
    ppermute x4, starting transfers between devices, extended(): lax.ppermute(lax.slice_in_dim(block, 0, width, axis=dim), axis, backward)  8.53 us
    ppermute x4, waiting for transfers between devices, extended(): lax.ppermute(lax.slice_in_dim(block, 0, width, axis=dim), axis, backward)  8.08 us
    while x44, local copies, waits for them, and re-layouts  7.26 us
    another operation x1, loops' own time, on_device(): lax.map(forward_tile, jnp.arange(tile_count, dtype=jnp.int32))  5.6 us
    another operation x1, loops' own time, on_device(): lax.scan(backward_tile, empty_pad, jnp.arange(tile_count, dtype=jnp.int32))  4.91 us
  transfers between devices with their start and end apart: 9, of which 4 were waited for; matrix products, arithmetic and copies ran while one was open for 12% of the time, Pallas kernels for 0%

profile of v1, /device:TPU:72, one launch (start us, length us, event | category | flops | bytes accessed | tf_op | source)
XLA Modules:
  0.0 186.8 jit_solution(15666256381549667959)
XLA Ops:
  1.4 1.0 fusion.112
  2.5 1.0 fusion.78
  3.5 1.2 copy.143
  4.7 1.3 fusion.92
  9.0 4.4 %collective-permute-start = (bf16[3,8,512]{2,1,0:T(8,128)(2,1)S(1)}, bf16[3,8,512]{2,1,0:T(8,128)(2,1)S(1)}, u32[]{:S(2)}, u32[]{:S(2)}) collective-permute-start(bf16[3,8,512]{2,1,0:T(8,128)(2,1)S(1)} %get-tuple-element.507), channel_id=1, source_target_pairs={{0,32},{32,64},{64,96},{1,33},{33,65},{65,97},{2,34},{34,66},{66,9... | collective-permute-start | bytes 73736 | tf_op jit(solution)/shard_map/ppermute | solution.py:23
  13.5 1.9 %collective-permute-start.1 = (bf16[3,8,512]{2,1,0:T(8,128)(2,1)S(1)}, bf16[3,8,512]{2,1,0:T(8,128)(2,1)S(1)}, u32[]{:S(2)}, u32[]{:S(2)}) collective-permute-start(bf16[3,8,512]{2,1,0:T(8,128)(2,1)S(1)} %get-tuple-element.508), channel_id=1, source_target_pairs={{32,0},{64,32},{96,64},{33,1},{65,33},{97,65},{34,2},{66,34},{98,6... | collective-permute-start | bytes 73736 | tf_op jit(solution)/shard_map/ppermute | solution.py:26
  20.7 3.5 %collective-permute-start.2 = (bf16[38,3,512]{2,1,0:T(4,128)(2,1)S(1)}, bf16[38,3,512]{2,1,0:T(4,128)(2,1)S(1)}, u32[]{:S(2)}, u32[]{:S(2)}) collective-permute-start(bf16[38,3,512]{2,1,0:T(4,128)(2,1)S(1)} %get-tuple-element.505), channel_id=1, source_target_pairs={{0,1},{1,2},{2,3},{3,4},{4,5},{5,6},{6,7},{7,8},{8,9},{9,10},{10,1... | collective-permute-start | bytes 350216 | tf_op jit(solution)/shard_map/ppermute | solution.py:23
  24.2 2.4 %collective-permute-start.3 = (bf16[38,3,512]{2,1,0:T(4,128)(2,1)S(1)}, bf16[38,3,512]{2,1,0:T(4,128)(2,1)S(1)}, u32[]{:S(2)}, u32[]{:S(2)}) collective-permute-start(bf16[38,3,512]{2,1,0:T(4,128)(2,1)S(1)} %get-tuple-element.506), channel_id=1, source_target_pairs={{1,0},{2,1},{3,2},{4,3},{5,4},{6,5},{7,6},{8,7},{9,8},{10,9},{11,1... | collective-permute-start | bytes 350216 | tf_op jit(solution)/shard_map/ppermute | solution.py:26
  27.2 0.9 collective-permute-done.2
  28.0 3.2 %collective-permute-done.3 = bf16[38,3,512]{2,1,0:T(4,128)(2,1)S(1)} collective-permute-done((bf16[38,3,512]{2,1,0:T(4,128)(2,1)S(1)}, bf16[38,3,512]{2,1,0:T(4,128)(2,1)S(1)}, u32[]{:S(2)}, u32[]{:S(2)}) %collective-permute-start.3) | collective-permute-done | bytes 116768 | tf_op jit(solution)/shard_map/ppermute | solution.py:26
  31.3 1.2 pad_maximum_fusion
  32.6 27.5 %while.33 = (s32[]{:T(128)}, f32[38,14,512]{2,1,0:T(8,128)S(1)}, f32[2,128,4,64]{1,3,2,0:T(8,128)}, s32[2]{0:T(128)S(1)}, bf16[2,128,4,64]{1,3,2,0:T(8,128)(2,1)...) while((s32[]{:T(128)}, f32[38,14,512]{2,1,0:T(8,128)S(1)}, ...), condition=%wide.region_9.10_spmd, body=%wide.region_6.9_spmd.sunk | while | flops 124238480 | bytes 19322752 | solution.py:178
  33.8 1.0 constant_dynamic-slice_fusion.5
  38.8 1.1 convolution_bitcast_fusion.6
  40.6 1.2 fusion.171
  41.8 1.0 convolution_bitcast_fusion.5
  42.8 1.3 copy.204
  47.6 1.0 constant_dynamic-slice_fusion.5
  52.6 1.1 convolution_bitcast_fusion.6
  54.3 1.2 fusion.171
  55.5 1.0 convolution_bitcast_fusion.5
  56.6 1.3 copy.204
  60.8 4.3 %collective-permute-start.4 = (bf16[3,14,512]{2,1,0:T(8,128)(2,1)S(1)}, bf16[3,14,512]{2,1,0:T(8,128)(2,1)}, u32[]{:S(2)}, u32[]{:S(2)}) collective-permute-start(bf16[3,14,512]{2,1,0:T(8,128)(2,1)S(1)} %get-tuple-element.499), channel_id=1, source_target_pairs={{0,32},{32,64},{64,96},{1,33},{33,65},{65,97},{2,34},{34,66},{66,9... | collective-permute-start | bytes 129032 | tf_op jit(solution)/shard_map/ppermute | solution.py:23
  65.1 2.1 %collective-permute-start.5 = (bf16[3,14,512]{2,1,0:T(8,128)(2,1)}, bf16[3,14,512]{2,1,0:T(8,128)(2,1)}, u32[]{:S(2)}, u32[]{:S(2)}) collective-permute-start(bf16[3,14,512]{2,1,0:T(8,128)(2,1)} %get-tuple-element.500), channel_id=1, source_target_pairs={{32,0},{64,32},{96,64},{33,1},{65,33},{97,65},{34,2},{66,34},{98,6... | collective-permute-start | bytes 129032 | tf_op jit(solution)/shard_map/ppermute | solution.py:26
  67.3 1.0 copy.157
  68.8 16.7 %while.32 = (s32[]{:T(128)}, bf16[2,128,256]{2,1,0:T(8,128)(2,1)}, s32[2]{0:T(128)}, bf16[38,14,512]{2,1,0:T(8,128)(2,1)}, bf16[2,128,4,64]{1,3,2,0:T(8,128)(2,1...) while((s32[]{:T(128)}, bf16[2,128,256]{2,1,0:T(8,128)(2,1)}, ...), condition=%wide.region_5.6_spmd, body=%wide.region_3.5_spmd.sunk | while | flops 41480536 | bytes 5906129 | solution.py:135
  68.8 1.4 dynamic_slice.97
  70.9 1.0 constant_dynamic-slice_fusion.4
  77.2 1.3 dynamic_slice.97
  79.2 1.0 constant_dynamic-slice_fusion.4
  85.5 1.0 copy.172
  86.5 1.8 convolution_convert_fusion.2
  88.3 1.3 multiply_reduce_fusion.1
  91.5 4.5 %collective-permute-start.6 = (bf16[32,3,512]{2,1,0:T(4,128)(2,1)S(1)}, bf16[32,3,512]{2,1,0:T(4,128)(2,1)S(1)}, u32[]{:S(2)}, u32[]{:S(2)}) collective-permute-start(bf16[32,3,512]{2,1,0:T(4,128)(2,1)S(1)} %get-tuple-element.503), channel_id=1, source_target_pairs={{0,1},{1,2},{2,3},{3,4},{4,5},{5,6},{6,7},{7,8},{8,9},{9,10},{10,1... | collective-permute-start | bytes 294920 | tf_op jit(solution)/shard_map/ppermute | solution.py:23
  96.0 2.1 %collective-permute-start.7 = (bf16[32,3,512]{2,1,0:T(4,128)(2,1)S(1)}, bf16[32,3,512]{2,1,0:T(4,128)(2,1)S(1)}, u32[]{:S(2)}, u32[]{:S(2)}) collective-permute-start(bf16[32,3,512]{2,1,0:T(4,128)(2,1)S(1)} %get-tuple-element.504), channel_id=1, source_target_pairs={{1,0},{2,1},{3,2},{4,3},{5,4},{6,5},{7,6},{8,7},{9,8},{10,9},{11,1... | collective-permute-start | bytes 294920 | tf_op jit(solution)/shard_map/ppermute | solution.py:26
  99.0 4.8 %collective-permute-done.7 = bf16[32,3,512]{2,1,0:T(4,128)(2,1)S(1)} collective-permute-done((bf16[32,3,512]{2,1,0:T(4,128)(2,1)S(1)}, bf16[32,3,512]{2,1,0:T(4,128)(2,1)S(1)}, u32[]{:S(2)}, u32[]{:S(2)}) %collective-permute-start.7) | collective-permute-done | bytes 98336 | tf_op jit(solution)/shard_map/ppermute | solution.py:26
  104.1 1.1 scatter-add.16
  105.5 1.1 scatter-add.19
  106.9 1.0 reshape.702
  109.0 1.1 stack_reshape.3
  110.2 1.7 fusion.71
  114.4 23.6 %all_to_all.15 = bf16[32,8,1152]{2,1,0:T(8,128)(2,1)S(1)} all-to-all(bf16[32,8,1152]{2,1,0:T(8,128)(2,1)S(1)} %fusion.67), channel_id=1, replica_groups=mesh['dp'=4,'row'=4,'col'=32] {'col'}, dimensions={0} | all-to-all | bytes 1179648 | tf_op jit(solution)/shard_map/all_to_all | solution.py:218
  138.1 20.0 %all_to_all.16 = bf16[16,8,1152]{2,1,0:T(8,128)(2,1)S(1)} all-to-all(bf16[16,8,1152]{2,1,0:T(8,128)(2,1)S(1)} %broadcast_in_dim.144), channel_id=1, replica_groups=mesh['dp'=4,'row'=4,'col'=32] {'dp','row'}, dimensions={0} | all-to-all | bytes 589824 | tf_op jit(solution)/shard_map/all_to_all | solution.py:218
  158.2 0.9 broadcast_in_dim.145
  159.1 4.7 %all-to-all-start.2 = ((bf16[32,8,1152]{2,1,0:T(8,128)(2,1)}), bf16[32,8,1152]{2,1,0:T(8,128)(2,1)S(1)}, u32[]{:S(2)}, u32[]{:S(2)}) async-start(bf16[32,8,1152]{2,1,0:T(8,128)(2,1)} %broadcast_in_dim.145), calls=%async_computation.2 | async-start | bytes 1179648 | tf_op jit(solution)/shard_map/all_to_all | solution.py:218
  165.5 18.2 %all-to-all-done.2 = bf16[32,8,1152]{2,1,0:T(8,128)(2,1)S(1)} async-done(((bf16[32,8,1152]{2,1,0:T(8,128)(2,1)}), bf16[32,8,1152]{2,1,0:T(8,128)(2,1)S(1)}, u32[]{:S(2)}, u32[]{:S(2)}) %all-to-all-start.2) | async-done | bytes 589856 | tf_op jit(solution)/shard_map/all_to_all | solution.py:218
  183.8 0.9 slice.261
  185.9 0.9 multiply_reduce_fusion
  (234 shorter events, 38.1 us)
Async XLA Ops:
  0.6 15.5 %copy-start = (bf16[256,256]{1,0:T(8,128)(2,1)S(1)}, bf16[256,256]{1,0:T(8,128)(2,1)}, u32[]{:S(2)}) copy-start(bf16[256,256]{1,0:T(8,128)(2,1)} %param.22) | copy-start | bytes 393220
  2.4 13.0 %copy-start.26 = (f32[256]{0:T(256)}, f32[256]{0:T(256)S(1)}, u32[]{:S(2)}) copy-start(f32[256]{0:T(256)S(1)} %broadcast_add_fusion) | copy-start | bytes 3076
  6.0 1.2 copy-start.1
  8.3 7.1 %copy-start.8 = (bf16[1,32,8,256]{3,2,1,0:T(8,128)(2,1)S(1)}, bf16[1,32,8,256]{3,2,1,0:T(8,128)(2,1)}, u32[]{:S(2)}) copy-start(bf16[1,32,8,256]{3,2,1,0:T(8,128)(2,1)} %param.18) | copy-start | bytes 393220
  9.0 7.1 %copy-start.15 = (bf16[1,32,8,256]{3,2,1,0:T(8,128)(2,1)S(1)}, bf16[1,32,8,256]{3,2,1,0:T(8,128)(2,1)}, u32[]{:S(2)}) copy-start(bf16[1,32,8,256]{3,2,1,0:T(8,128)(2,1)} %param.20) | copy-start | bytes 393220
  9.0 11.5 %collective-permute-start = (bf16[3,8,512]{2,1,0:T(8,128)(2,1)S(1)}, bf16[3,8,512]{2,1,0:T(8,128)(2,1)S(1)}, u32[]{:S(2)}, u32[]{:S(2)}) collective-permute-start(bf16[3,8,512]{2,1,0:T(8,128)(2,1)S(1)} %get-tuple-element.507), channel_id=1, source_target_pairs={{0,32},{32,64},{64,96},{1,33},{33,65},{65,97},{2,34},{34,66},{66,9... | collective-permute-start | bytes 73736 | tf_op jit(solution)/shard_map/ppermute | solution.py:23
  13.5 7.1 %collective-permute-start.1 = (bf16[3,8,512]{2,1,0:T(8,128)(2,1)S(1)}, bf16[3,8,512]{2,1,0:T(8,128)(2,1)S(1)}, u32[]{:S(2)}, u32[]{:S(2)}) collective-permute-start(bf16[3,8,512]{2,1,0:T(8,128)(2,1)S(1)} %get-tuple-element.508), channel_id=1, source_target_pairs={{32,0},{64,32},{96,64},{33,1},{65,33},{97,65},{34,2},{66,34},{98,6... | collective-permute-start | bytes 73736 | tf_op jit(solution)/shard_map/ppermute | solution.py:26
  15.9 2.5 %copy-start.5 = (f32[32,8,1,4,64]{4,1,0,3,2:T(8,128)}, f32[32,8,1,4,64]{4,1,0,3,2:T(8,128)S(1)}, u32[]{:S(2)}) copy-start(f32[32,8,1,4,64]{4,1,0,3,2:T(8,128)S(1)} %copy.148) | copy-start | bytes 786436
  20.7 7.4 %collective-permute-start.2 = (bf16[38,3,512]{2,1,0:T(4,128)(2,1)S(1)}, bf16[38,3,512]{2,1,0:T(4,128)(2,1)S(1)}, u32[]{:S(2)}, u32[]{:S(2)}) collective-permute-start(bf16[38,3,512]{2,1,0:T(4,128)(2,1)S(1)} %get-tuple-element.505), channel_id=1, source_target_pairs={{0,1},{1,2},{2,3},{3,4},{4,5},{5,6},{6,7},{7,8},{8,9},{9,10},{10,1... | collective-permute-start | bytes 350216 | tf_op jit(solution)/shard_map/ppermute | solution.py:23
  24.2 7.1 %collective-permute-start.3 = (bf16[38,3,512]{2,1,0:T(4,128)(2,1)S(1)}, bf16[38,3,512]{2,1,0:T(4,128)(2,1)S(1)}, u32[]{:S(2)}, u32[]{:S(2)}) collective-permute-start(bf16[38,3,512]{2,1,0:T(4,128)(2,1)S(1)} %get-tuple-element.506), channel_id=1, source_target_pairs={{1,0},{2,1},{3,2},{4,3},{5,4},{6,5},{7,6},{8,7},{9,8},{10,9},{11,1... | collective-permute-start | bytes 350216 | tf_op jit(solution)/shard_map/ppermute | solution.py:26
  32.6 5.7 %copy-start.11 = (bf16[2,128,4,64]{1,3,2,0:T(8,128)(2,1)}, bf16[2,128,4,64]{1,3,2,0:T(8,128)(2,1)S(1)}, u32[]{:S(2)}) copy-start(bf16[2,128,4,64]{1,3,2,0:T(8,128)(2,1)S(1)} %get-tuple-element.714) | copy-start | bytes 393220 | tf_op jit(solution)/shard_map/while
  32.6 6.1 %copy-start.3 = (bf16[2,128,4,64]{1,3,2,0:T(8,128)(2,1)}, bf16[2,128,4,64]{1,3,2,0:T(8,128)(2,1)S(1)}, u32[]{:S(2)}) copy-start(bf16[2,128,4,64]{1,3,2,0:T(8,128)(2,1)S(1)} %get-tuple-element.710) | copy-start | bytes 393220 | tf_op jit(solution)/shard_map/while
  40.2 1.6 copy-start.12
  44.5 1.0 copy-start.22
  44.5 1.9 copy-start.4
  44.5 1.8 copy-start.13
  45.7 0.7 copy-start.23
  46.4 5.7 %copy-start.11 = (bf16[2,128,4,64]{1,3,2,0:T(8,128)(2,1)}, bf16[2,128,4,64]{1,3,2,0:T(8,128)(2,1)S(1)}, u32[]{:S(2)}) copy-start(bf16[2,128,4,64]{1,3,2,0:T(8,128)(2,1)S(1)} %get-tuple-element.714) | copy-start | bytes 393220 | tf_op jit(solution)/shard_map/while
  46.4 6.1 %copy-start.3 = (bf16[2,128,4,64]{1,3,2,0:T(8,128)(2,1)}, bf16[2,128,4,64]{1,3,2,0:T(8,128)(2,1)S(1)}, u32[]{:S(2)}) copy-start(bf16[2,128,4,64]{1,3,2,0:T(8,128)(2,1)S(1)} %get-tuple-element.710) | copy-start | bytes 393220 | tf_op jit(solution)/shard_map/while
  53.9 1.6 copy-start.12
  58.2 1.0 copy-start.22
  58.3 1.9 copy-start.4
  58.3 1.8 copy-start.13
  59.4 0.7 copy-start.23
  60.1 7.2 %copy-start.24 = (f32[2,128,4,64]{1,3,2,0:T(8,128)S(1)}, f32[2,128,4,64]{1,3,2,0:T(8,128)}, u32[]{:S(2)}) copy-start(f32[2,128,4,64]{1,3,2,0:T(8,128)} %get-tuple-element.355) | copy-start | bytes 786436
  60.8 28.8 %collective-permute-start.4 = (bf16[3,14,512]{2,1,0:T(8,128)(2,1)S(1)}, bf16[3,14,512]{2,1,0:T(8,128)(2,1)}, u32[]{:S(2)}, u32[]{:S(2)}) collective-permute-start(bf16[3,14,512]{2,1,0:T(8,128)(2,1)S(1)} %get-tuple-element.499), channel_id=1, source_target_pairs={{0,32},{32,64},{64,96},{1,33},{33,65},{65,97},{2,34},{34,66},{66,9... | collective-permute-start | bytes 129032 | tf_op jit(solution)/shard_map/ppermute | solution.py:23
  65.1 24.5 %collective-permute-start.5 = (bf16[3,14,512]{2,1,0:T(8,128)(2,1)}, bf16[3,14,512]{2,1,0:T(8,128)(2,1)}, u32[]{:S(2)}, u32[]{:S(2)}) collective-permute-start(bf16[3,14,512]{2,1,0:T(8,128)(2,1)} %get-tuple-element.500), channel_id=1, source_target_pairs={{32,0},{64,32},{96,64},{33,1},{65,33},{97,65},{34,2},{66,34},{98,6... | collective-permute-start | bytes 129032 | tf_op jit(solution)/shard_map/ppermute | solution.py:26
  68.8 19.4 %copy-start.6 = (f32[32,8,1,4,64]{4,1,0,3,2:T(8,128)S(1)}, f32[32,8,1,4,64]{4,1,0,3,2:T(8,128)}, u32[]{:S(2)}) copy-start(f32[32,8,1,4,64]{4,1,0,3,2:T(8,128)} %copy-done.5) | copy-start | bytes 786436
  75.6 0.9 copy-start.19
  76.5 0.7 copy-start.20
  83.9 0.9 copy-start.19
  84.9 0.7 copy-start.20
  91.5 7.5 %collective-permute-start.6 = (bf16[32,3,512]{2,1,0:T(4,128)(2,1)S(1)}, bf16[32,3,512]{2,1,0:T(4,128)(2,1)S(1)}, u32[]{:S(2)}, u32[]{:S(2)}) collective-permute-start(bf16[32,3,512]{2,1,0:T(4,128)(2,1)S(1)} %get-tuple-element.503), channel_id=1, source_target_pairs={{0,1},{1,2},{2,3},{3,4},{4,5},{5,6},{6,7},{7,8},{8,9},{9,10},{10,1... | collective-permute-start | bytes 294920 | tf_op jit(solution)/shard_map/ppermute | solution.py:23
  96.0 7.8 %collective-permute-start.7 = (bf16[32,3,512]{2,1,0:T(4,128)(2,1)S(1)}, bf16[32,3,512]{2,1,0:T(4,128)(2,1)S(1)}, u32[]{:S(2)}, u32[]{:S(2)}) collective-permute-start(bf16[32,3,512]{2,1,0:T(4,128)(2,1)S(1)} %get-tuple-element.504), channel_id=1, source_target_pairs={{1,0},{2,1},{3,2},{4,3},{5,4},{6,5},{7,6},{8,7},{9,8},{10,9},{11,1... | collective-permute-start | bytes 294920 | tf_op jit(solution)/shard_map/ppermute | solution.py:26
  106.6 2.0 %copy-start.2 = (f32[32,8,3,4,64]{4,1,3,2,0:T(8,128)S(1)}, f32[32,8,3,4,64]{4,1,3,2,0:T(8,128)}, u32[]{:S(2)}) copy-start(f32[32,8,3,4,64]{4,1,3,2,0:T(8,128)} %copy-done.1) | copy-start | bytes 2359300
  107.9 2.3 %copy-start.7 = (f32[2,128,4,64]{3,1,0,2:T(8,128)S(1)}, f32[2,128,4,64]{3,1,0,2:T(8,128)}, u32[]{:S(2)}) copy-start(f32[2,128,4,64]{3,1,0,2:T(8,128)} %copy.157) | copy-start | bytes 786436
  107.9 2.3 %copy-start.25 = (f32[32,8,4]{1,2,0:T(4,128)S(1)}, f32[32,8,4]{1,2,0:T(4,128)}, u32[]{:S(2)}) copy-start(f32[32,8,4]{1,2,0:T(4,128)} %copy.158) | copy-start | bytes 12292
  108.6 1.6 copy-start.10
  112.4 1.0 copy-start.9
  112.4 1.1 copy-start.14
  112.4 1.1 copy-start.27
  112.9 1.0 copy-start.18
  113.4 0.7 copy-start.28
  113.4 0.8 copy-start.29
  113.4 0.9 copy-start.17
  138.1 25.7 %copy-start.21 = (bf16[2,128,256]{2,1,0:T(8,128)(2,1)S(1)}, bf16[2,128,256]{2,1,0:T(8,128)(2,1)}, u32[]{:S(2)}) copy-start(bf16[2,128,256]{2,1,0:T(8,128)(2,1)} %get-tuple-element.354) | copy-start | bytes 393220
  158.2 6.4 %copy-start.16 = (bf16[1,32,8,256]{3,2,1,0:T(8,128)(2,1)S(1)}, bf16[1,32,8,256]{3,2,1,0:T(8,128)(2,1)}, u32[]{:S(2)}) copy-start(bf16[1,32,8,256]{3,2,1,0:T(8,128)(2,1)} %param.20) | copy-start | bytes 393220
  159.1 24.6 %all-to-all-start.2 = ((bf16[32,8,1152]{2,1,0:T(8,128)(2,1)}), bf16[32,8,1152]{2,1,0:T(8,128)(2,1)S(1)}, u32[]{:S(2)}, u32[]{:S(2)}) async-start(bf16[32,8,1152]{2,1,0:T(8,128)(2,1)} %broadcast_in_dim.145), calls=%async_computation.2 | async-start | bytes 1179648 | tf_op jit(solution)/shard_map/all_to_all | solution.py:218

commit v2 on v0

v2 whole, which is shorter than its diff:
```python
import functools
import math

import jax
import jax.numpy as jnp
from jax import lax
from jax.experimental import pallas as pl
from jax.experimental.pallas import tpu as pltpu
from jax.sharding import PartitionSpec as P

HEAD_DIM = 64
CF = 256
RADIUS = 3
REACH = 2 * RADIUS
SPAN = 2
WINDOW = SPAN + REACH

score_scale = 6.0
epsilon = 1e-06


def fourier(step_value):
    half_count = CF // 2
    ladder = jnp.arange(half_count, dtype=jnp.float32)
    frequency = jnp.exp(ladder * (-math.log(1000.0) / half_count))
    phase_angle = step_value.astype(jnp.float32) * frequency
    return jnp.concatenate([jnp.cos(phase_angle), jnp.sin(phase_angle)])


def exchange(to_next, to_previous, axis):
    count = lax.axis_size(axis)
    forward = [(i, i + 1) for i in range(count - 1)]
    backward = [(target, source) for source, target in forward]
    return lax.ppermute(to_next, axis, forward), lax.ppermute(to_previous, axis, backward)


def nn(left, right):
    return lax.dot_general(left, right, (((1,), (0,)), ((), ())), preferred_element_type=jnp.float32)


def nt(left, right):
    return lax.dot_general(left, right, (((1,), (1,)), ((), ())), preferred_element_type=jnp.float32)


def tn(left, right):
    return lax.dot_general(left, right, (((0,), (0,)), ((), ())), preferred_element_type=jnp.float32)


def block_kernel(
    sizes,
    place_ref,
    tok_ref,
    cot_ref,
    low_ref,
    high_ref,
    adaptive_ref,
    qkv_ref,
    out_ref,
    result_ref,
    grad_tokens_ref,
    whole_ref,
    query_ref,
    key_ref,
    value_ref,
    grad_ref,
    mask_ref,
    attended_ref,
    grad_query_ref,
    grad_key_ref,
    grad_value_ref,
):
    height, total_rows, total_cols = sizes
    cols, rows, width = tok_ref.shape
    heads = width // HEAD_DIM
    around = cols + 2 * REACH
    query_cols = cols + REACH
    lanes = heads * SPAN * rows
    row_first = place_ref[0]
    col_first = place_ref[1]
    image = place_ref[2]
    step_value = place_ref[3]
    adaptive = adaptive_ref[...]
    factor = score_scale / HEAD_DIM

    own_head = lax.broadcasted_iota(jnp.int32, (width, width), 0) // HEAD_DIM
    other_head = lax.broadcasted_iota(jnp.int32, (width, width), 1) // HEAD_DIM
    average = jnp.where(own_head == other_head, 1.0 / HEAD_DIM, 0.0).astype(jnp.bfloat16)

    def head_mean(values):
        coarse = values.astype(jnp.bfloat16)
        fine = (values - coarse.astype(jnp.float32)).astype(jnp.bfloat16)
        return nn(coarse, average) + nn(fine, average)

    def normalized(pixels):
        inverse = lax.rsqrt(jnp.mean(pixels * pixels, axis=-1, keepdims=True) + epsilon)
        return inverse, (pixels * inverse * adaptive).astype(jnp.bfloat16)

    def put(first, count, project):
        query_raw = project[:, :width]
        key_raw = project[:, width : 2 * width]
        query_inv = lax.rsqrt(head_mean(query_raw * query_raw) + epsilon)
        key_inv = lax.rsqrt(head_mean(key_raw * key_raw) + epsilon)
        here = pl.ds(first, count)
        query_ref[here] = (query_raw * query_inv * factor).astype(jnp.bfloat16).reshape(count, rows, width)
        key_ref[here] = (key_raw * key_inv).astype(jnp.bfloat16).reshape(count, rows, width)
        value_ref[here] = project[:, 2 * width :].astype(jnp.bfloat16).reshape(count, rows, width)
        return query_raw, query_inv, key_raw, key_inv

    for ref, first in ((low_ref, 0), (high_ref, REACH + cols)):
        pixels = ref[:REACH].astype(jnp.float32).reshape(REACH * rows, width)
        put(first, REACH, nn(normalized(pixels)[1], qkv_ref[...]))
    pixels = tok_ref[...].astype(jnp.float32).reshape(cols * rows, width)
    inverse, normed = normalized(pixels)
    query_raw, query_inv, key_raw, key_inv = put(REACH, cols, nn(normed, qkv_ref[...]))

    cot_own = cot_ref[...].reshape(cols * rows, width)
    grad_ref[pl.ds(RADIUS, cols)] = nt(cot_own, out_ref[...]).astype(jnp.bfloat16).reshape(cols, rows, width)
    for ref, first in ((low_ref, 0), (high_ref, RADIUS + cols)):
        side = ref[REACH:].reshape(RADIUS * rows, width)
        grad_ref[pl.ds(first, RADIUS)] = nt(side, out_ref[...]).astype(jnp.bfloat16).reshape(RADIUS, rows, width)

    shape = (WINDOW, rows, lanes)
    key_row = lax.broadcasted_iota(jnp.int32, shape, 1)
    key_col = lax.broadcasted_iota(jnp.int32, shape, 0)
    lane = lax.broadcasted_iota(jnp.int32, (1, 1, lanes), 2) % (SPAN * rows)
    query_col = lane // rows
    query_row = lane % rows
    row_gap = key_row - query_row
    col_gap = key_col - query_col
    image_row = row_first + key_row - REACH
    allowed = (row_gap >= -RADIUS) & (row_gap <= RADIUS) & (col_gap >= 0) & (col_gap <= REACH)
    allowed = allowed & (image_row >= 0) & (image_row < total_rows)
    mask_ref[...] = jnp.where(allowed, 1.0, 0.0)

    grad_key_ref[...] = jnp.zeros_like(grad_key_ref)
    grad_value_ref[...] = jnp.zeros_like(grad_value_ref)
    lane_head = lax.broadcasted_iota(jnp.int32, (1, width), 1) // HEAD_DIM
    picks = [jnp.where(lane_head == head, 1.0, 0.0) for head in range(heads)]
    narrow = [pick.astype(jnp.bfloat16) for pick in picks]
    column = lax.broadcasted_iota(jnp.int32, (WINDOW, 1, 1), 0)

    def spread(values):
        return jnp.concatenate([values * pick for pick in narrow], axis=0)

    def gathered(values):
        total = values[: SPAN * rows] * picks[0]
        for head in range(1, heads):
            total = total + values[head * SPAN * rows : (head + 1) * SPAN * rows] * picks[head]
        return total

    def step(index, carry):
        start = SPAN * index
        near = pl.ds(start, WINDOW)
        keys = key_ref[near].reshape(WINDOW * rows, width)
        values = value_ref[near].reshape(WINDOW * rows, width)
        queries = spread(query_ref[pl.ds(start + RADIUS, SPAN)].reshape(SPAN * rows, width))
        grads = spread(grad_ref[pl.ds(start, SPAN)].reshape(SPAN * rows, width))
        image_col = col_first + start + column - REACH
        inside = jnp.where((image_col >= 0) & (image_col < total_cols), 1.0, 0.0)
        mask = (mask_ref[...] * inside).reshape(WINDOW * rows, lanes)
        exponent = jnp.exp(nt(keys, queries) - score_scale) * mask
        denominator = jnp.maximum(jnp.sum(exponent, axis=0, keepdims=True), 1e-30)
        weights = (exponent * (1.0 / denominator)).astype(jnp.bfloat16)
        wide = weights.astype(jnp.float32)
        slope = nt(values, grads)
        middle = jnp.sum(wide * slope, axis=0, keepdims=True)
        grad_score = (wide * (slope - middle)).astype(jnp.bfloat16)
        attended = gathered(tn(weights, values)).astype(jnp.bfloat16)
        attended_ref[pl.ds(start, SPAN)] = attended.reshape(SPAN, rows, width)
        grad_query_ref[pl.ds(start, SPAN)] = gathered(tn(grad_score, keys)).reshape(SPAN, rows, width)
        grad_key_ref[near] += nn(grad_score, queries).reshape(WINDOW, rows, width)
        grad_value_ref[near] += nn(weights, grads).reshape(WINDOW, rows, width)
        return carry

    lax.fori_loop(0, query_cols // SPAN, step, 0)

    row = lax.broadcasted_iota(jnp.int32, (cols, rows, 1), 1)
    own = jnp.where((row >= REACH) & (row < REACH + height), 1.0, 0.0).reshape(cols * rows, 1)
    attended = attended_ref[pl.ds(RADIUS, cols)].reshape(cols * rows, width)
    result = pixels + nn(attended, out_ref[...])
    result_ref[...] = result.astype(jnp.bfloat16).reshape(cols, rows, width)
    cotan = cot_own.astype(jnp.float32)
    grad_output = tn(attended, (cotan * own).astype(jnp.bfloat16))

    def back(raw, inv, grad, scale):
        return scale * inv * (grad - raw * inv * inv * head_mean(grad * raw))

    grad_query = grad_query_ref[pl.ds(RADIUS, cols)].reshape(cols * rows, width)
    grad_key = grad_key_ref[pl.ds(REACH, cols)].reshape(cols * rows, width)
    grad_value = grad_value_ref[pl.ds(REACH, cols)].reshape(cols * rows, width)
    grad_project = jnp.concatenate(
        [
            (back(query_raw, query_inv, grad_query, factor) * own).astype(jnp.bfloat16),
            (back(key_raw, key_inv, grad_key, 1.0) * own).astype(jnp.bfloat16),
            (grad_value * own).astype(jnp.bfloat16),
        ],
        axis=1,
    )
    grad_qkv = tn(normed, grad_project)
    grad_normed = nt(grad_project, qkv_ref[...])
    scaled = grad_normed * adaptive
    inner = jnp.mean(scaled * pixels, axis=-1, keepdims=True)
    grad_pixels = inverse * (scaled - pixels * (inverse * inverse * inner))
    grad_tokens_ref[...] = (cotan + grad_pixels).astype(jnp.bfloat16).reshape(cols, rows, width)
    grad_adaptive = jnp.sum(grad_normed * (pixels * inverse), axis=0, keepdims=True)

    whole_ref[:, : 3 * width] = grad_qkv.astype(jnp.bfloat16)
    whole_ref[:, 3 * width : 4 * width] = grad_output.astype(jnp.bfloat16)
    extra = whole_ref.shape[1] - 4 * width
    line = lax.broadcasted_iota(jnp.int32, (2 * SLOT, extra), 0)
    lane = lax.broadcasted_iota(jnp.int32, (2 * SLOT, extra), 1)
    pieces = width // extra
    side = jnp.zeros((2 * SLOT, extra), jnp.float32)
    for piece in range(pieces):
        part = grad_adaptive[:, piece * extra : (piece + 1) * extra]
        side = jnp.where(line == pieces * image + piece, part, side)
    high = (step_value // 32).astype(jnp.float32)
    low = (step_value % 32).astype(jnp.float32)
    side = jnp.where((line == SLOT) & (lane == 2 * image), high, side)
    side = jnp.where((line == SLOT) & (lane == 2 * image + 1), low, side)
    whole_ref[:, 4 * width :] = jnp.zeros((width, extra), jnp.bfloat16)
    whole_ref[: 2 * SLOT, 4 * width :] = side.astype(jnp.bfloat16)


SLOT = 8
EXTRA = 128


def block_call(sizes, place, tok, cot, low, high, adaptive, qkv_weight, output_weight):
    cols, rows, width = tok.shape
    around = cols + 2 * REACH
    query_cols = cols + REACH
    lanes = width // HEAD_DIM * SPAN * rows
    vmem = pl.BlockSpec(memory_space=pltpu.VMEM)
    return pl.pallas_call(
        functools.partial(block_kernel, sizes),
        out_shape=(
            jax.ShapeDtypeStruct((cols, rows, width), jnp.bfloat16),
            jax.ShapeDtypeStruct((cols, rows, width), jnp.bfloat16),
            jax.ShapeDtypeStruct((width, 4 * width + EXTRA), jnp.bfloat16),
        ),
        in_specs=[pl.BlockSpec(memory_space=pltpu.SMEM)] + [vmem] * 7,
        out_specs=(vmem,) * 3,
        scratch_shapes=[
            pltpu.VMEM((around, rows, width), jnp.bfloat16),
            pltpu.VMEM((around, rows, width), jnp.bfloat16),
            pltpu.VMEM((around, rows, width), jnp.bfloat16),
            pltpu.VMEM((query_cols, rows, width), jnp.bfloat16),
            pltpu.VMEM((WINDOW, rows, lanes), jnp.float32),
            pltpu.VMEM((query_cols, rows, width), jnp.bfloat16),
            pltpu.VMEM((query_cols, rows, width), jnp.float32),
            pltpu.VMEM((around, rows, width), jnp.float32),
            pltpu.VMEM((around, rows, width), jnp.float32),
        ],
        compiler_params=pltpu.CompilerParams(vmem_limit_bytes=48 * 2**20),
        cost_estimate=pl.CostEstimate(flops=8_000_000_000, bytes_accessed=4_000_000, transcendentals=1_000_000),
        name="block",
    )(place, tok, cot, low, high, adaptive, qkv_weight, output_weight)


def on_device(tokens, timesteps, cotangent, qkv_weight, output_weight, time_weight):
    height, cols, width = tokens.shape[1:]
    row_first = lax.axis_index("row") * height
    col_first = lax.axis_index("col") * cols
    total_rows = height * lax.axis_size("row")
    total_cols = cols * lax.axis_size("col")
    tok = tokens[0].transpose(1, 0, 2)
    cot = cotangent[0].transpose(1, 0, 2)
    both = jnp.concatenate([tok, cot], axis=0)
    above, below = exchange(both[:, height - REACH :], both[:, :REACH], "row")
    spare = -(height + 2 * REACH) % 16
    blank = jnp.zeros((2 * cols, spare, width), jnp.bfloat16)
    both = jnp.concatenate([above, both, below, blank], axis=1)
    tok, cot = both[:cols], both[cols:]
    to_next = jnp.concatenate([tok[cols - REACH :], cot[cols - RADIUS :]], axis=0)
    to_previous = jnp.concatenate([tok[:REACH], cot[:RADIUS]], axis=0)
    left, right = exchange(to_next, to_previous, "col")
    features = fourier(timesteps[0])
    adaptive = 1.0 + jnp.dot(
        features[None], time_weight.astype(jnp.float32), precision=lax.Precision.HIGHEST
    )
    place = jnp.stack([row_first, col_first, lax.axis_index("dp"), timesteps[0]]).astype(jnp.int32)
    result, grad_tokens, whole = block_call(
        (height, total_rows, total_cols), place, tok, cot, left, right, adaptive, qkv_weight, output_weight
    )
    result = result[:, REACH : REACH + height].transpose(1, 0, 2)
    grad_tokens = grad_tokens[:, REACH : REACH + height].transpose(1, 0, 2)
    total_qkv, total_output, total_time = summed(whole, width)
    return (result[None], grad_tokens[None], total_qkv, total_output, total_time)


def swap(pieces, axes):
    return lax.all_to_all(pieces, axes, 0, 0, tiled=True)


def summed(whole, width):
    rows, across = whole.shape
    images = lax.axis_size("dp")
    parts = lax.axis_size("col")
    others = lax.axis_size("dp") * lax.axis_size("row")
    pieces = whole.reshape(parts, rows // parts, across)
    piece = jnp.sum(swap(pieces, "col").astype(jnp.float32), axis=0).astype(jnp.bfloat16)
    copies = lax.optimization_barrier(jnp.broadcast_to(piece[None], (others,) + piece.shape))
    piece = jnp.sum(swap(copies, ("dp", "row")).astype(jnp.float32), axis=0).astype(jnp.bfloat16)
    copies = lax.optimization_barrier(jnp.broadcast_to(piece[None], (parts,) + piece.shape))
    whole = swap(copies, "col").astype(jnp.float32).reshape(rows, across)
    adaptives = whole[:SLOT, 4 * width :].reshape(images, width)
    steps = whole[SLOT, 4 * width : 4 * width + 2 * images].reshape(images, 2)
    steps = steps / (parts * lax.axis_size("row"))
    features = jax.vmap(fourier)(steps[:, 0] * 32.0 + steps[:, 1])
    total_time = jnp.sum(features[:, :, None] * adaptives[:, None, :], axis=0)
    return whole[:, : 3 * width], whole[:, 3 * width : 4 * width], total_time


def solution(mesh):
    in_specs = (P("dp", "row", "col", None), P("dp"), P("dp", "row", "col", None), P(), P(), P())
    out_specs = (P("dp", "row", "col", None), P("dp", "row", "col", None), P(), P(), P())
    return jax.shard_map(
        on_device, mesh=mesh, in_specs=in_specs, out_specs=out_specs, check_vma=False
    )
```

time: 414 us -> 109 us (0.26)
  the two profiles are of different devices: /device:TPU:1 before, /device:TPU:72 now
where the time goes in v2:
time: 109 us; the launch traced here: 108 us
  blocking collectives  46.6 us (43%)
  waiting for transfers between devices  22.5 us (21%)
  starting transfers between devices  19.8 us (18%)
  Pallas kernels  10.4 us (10%)
  local copies, waits for them, and re-layouts  5.38 us (5%)
  other arithmetic  1.98 us (2%)
  between operations  1.48 us (1%)
    all_to_all x2, blocking collectives, swap(): return lax.all_to_all(pieces, axes, 0, 0, tiled=True)  46.6 us
    all_to_all x1, waiting for transfers between devices, swap(): return lax.all_to_all(pieces, axes, 0, 0, tiled=True)  18.3 us
    pallas_call x1, Pallas kernels, block_call(): pl.pallas_call(functools.partial(block_kernel, sizes), out_shape=(jax.Sha...  10.4 us
    ppermute x2, starting transfers between devices, exchange(): lax.ppermute(to_next, axis, forward)  7.9 us
    ppermute x2, starting transfers between devices, exchange(): lax.ppermute(to_previous, axis, backward)  7.07 us
    all_to_all x1, starting transfers between devices, swap(): return lax.all_to_all(pieces, axes, 0, 0, tiled=True)  4.81 us
    ppermute x2, waiting for transfers between devices, exchange(): lax.ppermute(to_next, axis, forward)  2.69 us
  transfers between devices with their start and end apart: 5, of which 4 were waited for; matrix products, arithmetic and copies ran while one was open for 2% of the time, Pallas kernels for 0%

profile of v2, /device:TPU:72, one launch (start us, length us, event | category | flops | bytes accessed | tf_op | source)
XLA Modules:
  0.0 108.3 jit_solution(1949690145980783010)
XLA Ops:
  0.6 0.0 copy-start
  0.6 1.1 copy_bitcast_fusion
  1.7 1.9 %collective-permute-start.1 = (bf16[16,6,256]{2,1,0:T(8,128)(2,1)S(1)}, bf16[16,6,256]{2,1,0:T(8,128)(2,1)S(1)}, u32[]{:S(2)}, u32[]{:S(2)}) collective-permute-start(bf16[16,6,256]{2,1,0:T(8,128)(2,1)S(1)} %get-tuple-element.33), channel_id=1, source_target_pairs={{32,0},{64,32},{96,64},{33,1},{65,33},{97,65},{34,2},{66,34},{98,6... | collective-permute-start | bytes 147464 | tf_op jit(solution)/shard_map/ppermute | solution.py:34
  3.7 4.3 %collective-permute-start = (bf16[16,6,256]{2,1,0:T(8,128)(2,1)S(1)}, bf16[16,6,256]{2,1,0:T(8,128)(2,1)S(1)}, u32[]{:S(2)}, u32[]{:S(2)}) collective-permute-start(bf16[16,6,256]{2,1,0:T(8,128)(2,1)S(1)} %get-tuple-element.32), channel_id=1, source_target_pairs={{0,32},{32,64},{64,96},{1,33},{33,65},{65,97},{2,34},{34,66},{66,9... | collective-permute-start | bytes 147464 | tf_op jit(solution)/shard_map/ppermute | solution.py:34
  8.7 0.0 copy-done
  8.7 0.1 fusion.4
  8.8 0.1 pad_add_fusion.place_ref
  9.0 0.1 pad.12.clone
  9.0 0.0 collective-permute-done.1
  9.0 0.8 collective-permute-done
  9.8 0.3 maximum_maximum_fusion
  10.1 0.0 copy-start.1
  10.1 0.0 copy-start.2
  10.2 3.6 %collective-permute-start.2 = (bf16[9,48,256]{2,1,0:T(8,128)(2,1)S(1)}, bf16[9,48,256]{2,1,0:T(8,128)(2,1)S(1)}, u32[]{:S(2)}, u32[]{:S(2)}) collective-permute-start(bf16[9,48,256]{2,1,0:T(8,128)(2,1)S(1)} %pad_maximum_fusion), channel_id=1, source_target_pairs={{0,1},{1,2},{2,3},{3,4},{4,5},{5,6},{6,7},{7,8},{8,9},{9,10},{10,1... | collective-permute-start | bytes 663560 | tf_op jit(solution)/shard_map/ppermute | solution.py:34
  13.9 5.2 %collective-permute-start.3 = (bf16[9,48,256]{2,1,0:T(8,128)(2,1)S(1)}, bf16[9,48,256]{2,1,0:T(8,128)(2,1)S(1)}, u32[]{:S(2)}, u32[]{:S(2)}) collective-permute-start(bf16[9,48,256]{2,1,0:T(8,128)(2,1)S(1)} %pad_maximum_fusion.1), channel_id=1, source_target_pairs={{1,0},{2,1},{3,2},{4,3},{5,4},{6,5},{7,6},{8,7},{9,8},{10,9},{11,1... | collective-permute-start | bytes 663560 | tf_op jit(solution)/shard_map/ppermute | solution.py:34
  19.1 1.9 %collective-permute-done.2.low_ref = bf16[9,48,256]{2,1,0:T(8,128)(2,1)S(1)} collective-permute-done((bf16[9,48,256]{2,1,0:T(8,128)(2,1)S(1)}, bf16[9,48,256]{2,1,0:T(8,128)(2,1)S(1)}, u32[]{:S(2)}, u32[]{:S(2)}) %collective-permute-start.2) | collective-permute-done | bytes 221216 | tf_op jit(solution)/shard_map/ppermute | solution.py:34
  20.9 1.5 %collective-permute-done.3.high_ref = bf16[9,48,256]{2,1,0:T(8,128)(2,1)S(1)} collective-permute-done((bf16[9,48,256]{2,1,0:T(8,128)(2,1)S(1)}, bf16[9,48,256]{2,1,0:T(8,128)(2,1)S(1)}, u32[]{:S(2)}, u32[]{:S(2)}) %collective-permute-start.3) | collective-permute-done | bytes 221216 | tf_op jit(solution)/shard_map/ppermute | solution.py:34
  22.4 0.0 copy-done.1
  22.5 0.0 copy-done.2
  22.5 10.4 %block.1 = (bf16[8,48,256]{2,1,0:T(8,128)(2,1)S(1)}, bf16[8,48,256]{2,1,0:T(8,128)(2,1)S(1)}, bf16[256,1152]{1,0:T(8,128)(2,1)S(1)}) custom-call(s32[4]{0:T(128)S(1)} %pad_add_fusion.place_ref, bf16[8,48,256]{2,1,0:T(8,128)(2,1)S(1)} %get-tuple-element.31.tok_ref, bf16[8,48,256]{2,1,0:T(8,128)(2,1)S(1)} %get-tuple-element.30.cot_ref, ...), custom_call_target="tpu_custom_call" | custom-call | flops 8000000000 | bytes 4000000 | tf_op jit(solution)/shard_map/block/pallas_call | solution.py:235
  32.9 26.5 %all_to_all.15 = bf16[32,8,1152]{2,1,0:T(8,128)(2,1)S(1)} all-to-all(bf16[32,8,1152]{2,1,0:T(8,128)(2,1)S(1)} %bitcast.29), channel_id=1, replica_groups=mesh['dp'=4,'row'=4,'col'=32] {'col'}, dimensions={0} | all-to-all | bytes 1179648 | tf_op jit(solution)/shard_map/all_to_all | solution.py:293
  59.4 0.1 reduce_sum.33
  59.5 20.0 %all_to_all.16 = bf16[16,8,1152]{2,1,0:T(8,128)(2,1)S(1)} all-to-all(bf16[16,8,1152]{2,1,0:T(8,128)(2,1)S(1)} %broadcast_in_dim.13), channel_id=1, replica_groups=mesh['dp'=4,'row'=4,'col'=32] {'dp','row'}, dimensions={0} | all-to-all | bytes 589824 | tf_op jit(solution)/shard_map/all_to_all | solution.py:293
  79.6 0.9 broadcast_in_dim.14
  80.5 4.8 %all-to-all-start.2 = ((bf16[32,8,1152]{2,1,0:T(8,128)(2,1)}), bf16[32,8,1152]{2,1,0:T(8,128)(2,1)S(1)}, u32[]{:S(2)}, u32[]{:S(2)}) async-start(bf16[32,8,1152]{2,1,0:T(8,128)(2,1)} %broadcast_in_dim.14), calls=%async_computation.2 | async-start | bytes 1179648 | tf_op jit(solution)/shard_map/all_to_all | solution.py:293
  85.4 0.7 copy.21
  86.2 0.7 copy.22
  86.9 18.3 %all-to-all-done.2 = bf16[32,8,1152]{2,1,0:T(8,128)(2,1)S(1)} async-done(((bf16[32,8,1152]{2,1,0:T(8,128)(2,1)}), bf16[32,8,1152]{2,1,0:T(8,128)(2,1)S(1)}, u32[]{:S(2)}, u32[]{:S(2)}) %all-to-all-start.2) | async-done | bytes 589856 | tf_op jit(solution)/shard_map/all_to_all | solution.py:293
  105.2 0.1 bitcast_convert_fusion
  105.3 0.9 slice.74
  106.2 0.7 slice.75
  107.0 0.1 div.6
  107.1 0.2 add_reduce_fusion
  107.2 0.1 multiply_cosine_fusion
  107.4 0.9 multiply_reduce_fusion
  (19 shorter events, 0.4 us)
Async XLA Ops:
  0.6 8.0 %copy-start = (bf16[256,256]{1,0:T(8,128)(2,1)S(1)}, bf16[256,256]{1,0:T(8,128)(2,1)}, u32[]{:S(2)}) copy-start(bf16[256,256]{1,0:T(8,128)(2,1)} %param.11) | copy-start | bytes 393220
  1.7 7.3 %collective-permute-start.1 = (bf16[16,6,256]{2,1,0:T(8,128)(2,1)S(1)}, bf16[16,6,256]{2,1,0:T(8,128)(2,1)S(1)}, u32[]{:S(2)}, u32[]{:S(2)}) collective-permute-start(bf16[16,6,256]{2,1,0:T(8,128)(2,1)S(1)} %get-tuple-element.33), channel_id=1, source_target_pairs={{32,0},{64,32},{96,64},{33,1},{65,33},{97,65},{34,2},{66,34},{98,6... | collective-permute-start | bytes 147464 | tf_op jit(solution)/shard_map/ppermute | solution.py:34
  3.7 6.2 %collective-permute-start = (bf16[16,6,256]{2,1,0:T(8,128)(2,1)S(1)}, bf16[16,6,256]{2,1,0:T(8,128)(2,1)S(1)}, u32[]{:S(2)}, u32[]{:S(2)}) collective-permute-start(bf16[16,6,256]{2,1,0:T(8,128)(2,1)S(1)} %get-tuple-element.32), channel_id=1, source_target_pairs={{0,32},{32,64},{64,96},{1,33},{33,65},{65,97},{2,34},{34,66},{66,9... | collective-permute-start | bytes 147464 | tf_op jit(solution)/shard_map/ppermute | solution.py:34
  10.1 12.3 %copy-start.1 = (bf16[256,768]{1,0:T(8,128)(2,1)S(1)}, bf16[256,768]{1,0:T(8,128)(2,1)}, u32[]{:S(2)}) copy-start(bf16[256,768]{1,0:T(8,128)(2,1)} %qkv_ref.1) | copy-start | bytes 1179652
  10.1 12.3 %copy-start.2 = (bf16[256,256]{1,0:T(8,128)(2,1)S(1)}, bf16[256,256]{1,0:T(8,128)(2,1)}, u32[]{:S(2)}) copy-start(bf16[256,256]{1,0:T(8,128)(2,1)} %out_ref.1) | copy-start | bytes 393220
  10.2 10.7 %collective-permute-start.2 = (bf16[9,48,256]{2,1,0:T(8,128)(2,1)S(1)}, bf16[9,48,256]{2,1,0:T(8,128)(2,1)S(1)}, u32[]{:S(2)}, u32[]{:S(2)}) collective-permute-start(bf16[9,48,256]{2,1,0:T(8,128)(2,1)S(1)} %pad_maximum_fusion), channel_id=1, source_target_pairs={{0,1},{1,2},{2,3},{3,4},{4,5},{5,6},{6,7},{7,8},{8,9},{9,10},{10,1... | collective-permute-start | bytes 663560 | tf_op jit(solution)/shard_map/ppermute | solution.py:34
  13.9 8.6 %collective-permute-start.3 = (bf16[9,48,256]{2,1,0:T(8,128)(2,1)S(1)}, bf16[9,48,256]{2,1,0:T(8,128)(2,1)S(1)}, u32[]{:S(2)}, u32[]{:S(2)}) collective-permute-start(bf16[9,48,256]{2,1,0:T(8,128)(2,1)S(1)} %pad_maximum_fusion.1), channel_id=1, source_target_pairs={{1,0},{2,1},{3,2},{4,3},{5,4},{6,5},{7,6},{8,7},{9,8},{10,9},{11,1... | collective-permute-start | bytes 663560 | tf_op jit(solution)/shard_map/ppermute | solution.py:34
  80.5 24.7 %all-to-all-start.2 = ((bf16[32,8,1152]{2,1,0:T(8,128)(2,1)}), bf16[32,8,1152]{2,1,0:T(8,128)(2,1)S(1)}, u32[]{:S(2)}, u32[]{:S(2)}) async-start(bf16[32,8,1152]{2,1,0:T(8,128)(2,1)} %broadcast_in_dim.14), calls=%async_computation.2 | async-start | bytes 1179648 | tf_op jit(solution)/shard_map/all_to_all | solution.py:293

commit v3 on v2

v3 whole, which is shorter than its diff:
```python
import functools
import math

import jax
import jax.numpy as jnp
from jax import lax
from jax.experimental import pallas as pl
from jax.experimental.pallas import tpu as pltpu
from jax.sharding import PartitionSpec as P

HEAD_DIM = 64
CF = 256
RADIUS = 3
REACH = 2 * RADIUS
SPAN = 2
WINDOW = SPAN + REACH

score_scale = 6.0
epsilon = 1e-06


def fourier(step_value):
    half_count = CF // 2
    ladder = jnp.arange(half_count, dtype=jnp.float32)
    frequency = jnp.exp(ladder * (-math.log(1000.0) / half_count))
    phase_angle = step_value.astype(jnp.float32) * frequency
    return jnp.concatenate([jnp.cos(phase_angle), jnp.sin(phase_angle)])


def exchange(to_next, to_previous, axis):
    count = lax.axis_size(axis)
    forward = [(i, i + 1) for i in range(count - 1)]
    backward = [(target, source) for source, target in forward]
    return lax.ppermute(to_next, axis, forward), lax.ppermute(to_previous, axis, backward)


def nn(left, right):
    return lax.dot_general(left, right, (((1,), (0,)), ((), ())), preferred_element_type=jnp.float32)


def nt(left, right):
    return lax.dot_general(left, right, (((1,), (1,)), ((), ())), preferred_element_type=jnp.float32)


def tn(left, right):
    return lax.dot_general(left, right, (((0,), (0,)), ((), ())), preferred_element_type=jnp.float32)


def average_matrix(width):
    own_head = lax.broadcasted_iota(jnp.int32, (width, width), 0) // HEAD_DIM
    other_head = lax.broadcasted_iota(jnp.int32, (width, width), 1) // HEAD_DIM
    return jnp.where(own_head == other_head, 1.0 / HEAD_DIM, 0.0).astype(jnp.bfloat16)


def head_mean(values, average):
    coarse = values.astype(jnp.bfloat16)
    fine = (values - coarse.astype(jnp.float32)).astype(jnp.bfloat16)
    return nn(coarse, average) + nn(fine, average)


def normalized(pixels, adaptive):
    inverse = lax.rsqrt(jnp.mean(pixels * pixels, axis=-1, keepdims=True) + epsilon)
    return inverse, (pixels * inverse * adaptive).astype(jnp.bfloat16)


def project_to(pixels, adaptive, qkv_ref, average, query_ref, key_ref, value_ref, here):
    width = pixels.shape[-1]
    shape = (-1,) + query_ref.shape[1:]
    inverse, normed = normalized(pixels, adaptive)
    project = nn(normed, qkv_ref[...])
    query_raw = project[:, :width]
    key_raw = project[:, width : 2 * width]
    query_inv = lax.rsqrt(head_mean(query_raw * query_raw, average) + epsilon)
    key_inv = lax.rsqrt(head_mean(key_raw * key_raw, average) + epsilon)
    factor = score_scale / HEAD_DIM
    query_ref[here] = (query_raw * query_inv * factor).astype(jnp.bfloat16).reshape(shape)
    key_ref[here] = (key_raw * key_inv).astype(jnp.bfloat16).reshape(shape)
    value_ref[here] = project[:, 2 * width :].astype(jnp.bfloat16).reshape(shape)
    return inverse, normed, query_raw, query_inv, key_raw, key_inv


def own_kernel(
    total_rows,
    place_ref,
    tok_ref,
    cot_ref,
    adaptive_ref,
    qkv_ref,
    out_ref,
    query_ref,
    key_ref,
    value_ref,
    grad_ref,
    mask_ref,
    query_raw_ref,
    query_inv_ref,
    key_raw_ref,
    key_inv_ref,
):
    cols, rows, width = tok_ref.shape
    lanes = mask_ref.shape[2]
    row_first = place_ref[0]
    pixels = tok_ref[...].astype(jnp.float32).reshape(cols * rows, width)
    _, _, query_raw, query_inv, key_raw, key_inv = project_to(
        pixels, adaptive_ref[...], qkv_ref, average_matrix(width), query_ref, key_ref, value_ref, pl.ds(0, cols)
    )
    query_raw_ref[...] = query_raw
    query_inv_ref[...] = query_inv
    key_raw_ref[...] = key_raw
    key_inv_ref[...] = key_inv
    cot_own = cot_ref[...].reshape(cols * rows, width)
    grad_ref[...] = nt(cot_own, out_ref[...]).astype(jnp.bfloat16).reshape(cols, rows, width)

    shape = (WINDOW, rows, lanes)
    key_row = lax.broadcasted_iota(jnp.int32, shape, 1)
    key_col = lax.broadcasted_iota(jnp.int32, shape, 0)
    lane = lax.broadcasted_iota(jnp.int32, (1, 1, lanes), 2) % (SPAN * rows)
    query_col = lane // rows
    query_row = lane % rows
    row_gap = key_row - query_row
    col_gap = key_col - query_col
    image_row = row_first + key_row - REACH
    allowed = (row_gap >= -RADIUS) & (row_gap <= RADIUS) & (col_gap >= 0) & (col_gap <= REACH)
    allowed = allowed & (image_row >= 0) & (image_row < total_rows)
    mask_ref[...] = jnp.where(allowed, 1.0, 0.0)


def block_kernel(
    sizes,
    place_ref,
    tok_ref,
    cot_ref,
    low_ref,
    high_ref,
    adaptive_ref,
    qkv_ref,
    out_ref,
    own_query_ref,
    own_key_ref,
    own_value_ref,
    own_grad_ref,
    mask_ref,
    query_raw_ref,
    query_inv_ref,
    key_raw_ref,
    key_inv_ref,
    result_ref,
    grad_tokens_ref,
    mine_ref,
    other_ref,
    query_ref,
    key_ref,
    value_ref,
    grad_ref,
    attended_ref,
    grad_query_ref,
    grad_key_ref,
    grad_value_ref,
    whole_ref,
):
    height, total_cols = sizes
    cols, rows, width = tok_ref.shape
    heads = width // HEAD_DIM
    query_cols = cols + REACH
    lanes = heads * SPAN * rows
    col_first = place_ref[1]
    image = place_ref[2]
    core = place_ref[3]
    step_value = place_ref[4]
    adaptive = adaptive_ref[...]
    factor = score_scale / HEAD_DIM
    average = average_matrix(width)

    for ref, first in ((low_ref, 0), (high_ref, REACH + cols)):
        pixels = ref[:REACH].astype(jnp.float32).reshape(REACH * rows, width)
        project_to(pixels, adaptive, qkv_ref, average, query_ref, key_ref, value_ref, pl.ds(first, REACH))
    query_ref[pl.ds(REACH, cols)] = own_query_ref[...]
    key_ref[pl.ds(REACH, cols)] = own_key_ref[...]
    value_ref[pl.ds(REACH, cols)] = own_value_ref[...]
    grad_ref[pl.ds(RADIUS, cols)] = own_grad_ref[...]
    for ref, first in ((low_ref, 0), (high_ref, RADIUS + cols)):
        side = ref[REACH:].reshape(RADIUS * rows, width)
        grad_ref[pl.ds(first, RADIUS)] = nt(side, out_ref[...]).astype(jnp.bfloat16).reshape(RADIUS, rows, width)

    grad_key_ref[...] = jnp.zeros_like(grad_key_ref)
    grad_value_ref[...] = jnp.zeros_like(grad_value_ref)
    lane_head = lax.broadcasted_iota(jnp.int32, (1, width), 1) // HEAD_DIM
    picks = [jnp.where(lane_head == head, 1.0, 0.0) for head in range(heads)]
    narrow = [pick.astype(jnp.bfloat16) for pick in picks]
    column = lax.broadcasted_iota(jnp.int32, (WINDOW, 1, 1), 0)

    def spread(values):
        return jnp.concatenate([values * pick for pick in narrow], axis=0)

    def gathered(values):
        total = values[: SPAN * rows] * picks[0]
        for head in range(1, heads):
            total = total + values[head * SPAN * rows : (head + 1) * SPAN * rows] * picks[head]
        return total

    def step(index, carry):
        start = SPAN * index
        near = pl.ds(start, WINDOW)
        keys = key_ref[near].reshape(WINDOW * rows, width)
        values = value_ref[near].reshape(WINDOW * rows, width)
        queries = spread(query_ref[pl.ds(start + RADIUS, SPAN)].reshape(SPAN * rows, width))
        grads = spread(grad_ref[pl.ds(start, SPAN)].reshape(SPAN * rows, width))
        image_col = col_first + start + column - REACH
        inside = jnp.where((image_col >= 0) & (image_col < total_cols), 1.0, 0.0)
        mask = (mask_ref[...] * inside).reshape(WINDOW * rows, lanes)
        exponent = jnp.exp(nt(keys, queries) - score_scale) * mask
        denominator = jnp.maximum(jnp.sum(exponent, axis=0, keepdims=True), 1e-30)
        weights = (exponent * (1.0 / denominator)).astype(jnp.bfloat16)
        wide = weights.astype(jnp.float32)
        slope = nt(values, grads)
        middle = jnp.sum(wide * slope, axis=0, keepdims=True)
        grad_score = (wide * (slope - middle)).astype(jnp.bfloat16)
        attended = gathered(tn(weights, values)).astype(jnp.bfloat16)
        attended_ref[pl.ds(start, SPAN)] = attended.reshape(SPAN, rows, width)
        grad_query_ref[pl.ds(start, SPAN)] = gathered(tn(grad_score, keys)).reshape(SPAN, rows, width)
        grad_key_ref[near] += nn(grad_score, queries).reshape(WINDOW, rows, width)
        grad_value_ref[near] += nn(weights, grads).reshape(WINDOW, rows, width)
        return carry

    lax.fori_loop(0, query_cols // SPAN, step, 0)

    pixels = tok_ref[...].astype(jnp.float32).reshape(cols * rows, width)
    inverse, normed = normalized(pixels, adaptive)
    cot_own = cot_ref[...].reshape(cols * rows, width)
    row = lax.broadcasted_iota(jnp.int32, (cols, rows, 1), 1)
    own = jnp.where((row >= REACH) & (row < REACH + height), 1.0, 0.0).reshape(cols * rows, 1)
    attended = attended_ref[pl.ds(RADIUS, cols)].reshape(cols * rows, width)
    result = pixels + nn(attended, out_ref[...])
    result_ref[...] = result.astype(jnp.bfloat16).reshape(cols, rows, width)
    cotan = cot_own.astype(jnp.float32)
    whole_ref[:, 3 * width :] = tn(attended, (cotan * own).astype(jnp.bfloat16))

    def back(raw, inv, grad, scale):
        return scale * inv * (grad - raw * inv * inv * head_mean(grad * raw, average))

    grad_query = grad_query_ref[pl.ds(RADIUS, cols)].reshape(cols * rows, width)
    grad_key = grad_key_ref[pl.ds(REACH, cols)].reshape(cols * rows, width)
    grad_value = grad_value_ref[pl.ds(REACH, cols)].reshape(cols * rows, width)
    grad_project = jnp.concatenate(
        [
            (back(query_raw_ref[...], query_inv_ref[...], grad_query, factor) * own).astype(jnp.bfloat16),
            (back(key_raw_ref[...], key_inv_ref[...], grad_key, 1.0) * own).astype(jnp.bfloat16),
            (grad_value * own).astype(jnp.bfloat16),
        ],
        axis=1,
    )
    whole_ref[:, : 3 * width] = tn(normed, grad_project)
    grad_normed = nt(grad_project, qkv_ref[...])
    scaled = grad_normed * adaptive
    inner = jnp.mean(scaled * pixels, axis=-1, keepdims=True)
    grad_pixels = inverse * (scaled - pixels * (inverse * inverse * inner))
    grad_tokens_ref[...] = (cotan + grad_pixels).astype(jnp.bfloat16).reshape(cols, rows, width)
    grad_adaptive = jnp.sum(grad_normed * (pixels * inverse), axis=0, keepdims=True)

    half = width // CORES
    across = 4 * width // LANES
    blocks = mine_ref.shape[0]
    line = lax.broadcasted_iota(jnp.int32, (SLOT, LANES), 0)
    lane = lax.broadcasted_iota(jnp.int32, (SLOT, LANES), 1)
    high = (step_value // 32).astype(jnp.float32)
    low = (step_value % 32).astype(jnp.float32)
    for ref, which in ((mine_ref, core), (other_ref, 1 - core)):
        part = whole_ref[pl.ds(pl.multiple_of(which * half, half), half), :].astype(jnp.bfloat16)
        for block in range(blocks):
            top = block // across * LINES
            first = block % across * LANES
            ref[block, :LINES] = part[top : top + LINES, first : first + LANES]
            if block < width // LANES:
                side = jnp.where(line == image, grad_adaptive[:, block * LANES : (block + 1) * LANES], 0.0)
                if block == 0:
                    there = line == SLOT // 2 + image
                    side = jnp.where(there & (lane == 0), high, side)
                    side = jnp.where(there & (lane == 1), low, side)
                ref[block, LINES:] = side.astype(jnp.bfloat16)
            else:
                ref[block, LINES:] = jnp.zeros((SLOT, LANES), jnp.bfloat16)


def finish_kernel(senders, place_ref, mine_ref, other_ref, qkv_ref, output_ref, time_ref):
    width = output_ref.shape[0]
    images = senders[0]
    half = width // CORES
    across = 4 * width // LANES
    core = place_ref[3]
    for ref, which in ((mine_ref, core), (other_ref, 1 - core)):
        for block in range(mine_ref.shape[0]):
            top = pl.multiple_of(which * half, half) + block // across * LINES
            first = block % across * LANES
            values = ref[block, :LINES].astype(jnp.float32)
            if first < 3 * width:
                qkv_ref[pl.ds(top, LINES), first : first + LANES] = values
            else:
                output_ref[pl.ds(top, LINES), first - 3 * width : first - 3 * width + LANES] = values
    sides = [mine_ref[block, LINES:].astype(jnp.float32) for block in range(width // LANES)]
    adaptives = jnp.concatenate(sides, axis=1)
    adaptives = jnp.where(lax.broadcasted_iota(jnp.int32, adaptives.shape, 0) < images, adaptives, 0.0)
    ladder = lax.broadcasted_iota(jnp.int32, (1, CF // 2), 1).astype(jnp.float32)
    frequency = jnp.exp(ladder * (-math.log(1000.0) / (CF // 2)))
    steps = (sides[0][:, 0:1] * 32.0 + sides[0][:, 1:2]) / senders[1]
    steps = jnp.concatenate([steps[SLOT // 2 :], steps[: SLOT // 2] * 0.0], axis=0)
    angle = steps * frequency
    features = jnp.concatenate([jnp.cos(angle), jnp.sin(angle)], axis=1)
    time_ref[...] = lax.dot_general(
        features,
        adaptives,
        (((0,), (0,)), ((), ())),
        precision=lax.Precision.HIGHEST,
        preferred_element_type=jnp.float32,
    )


CORES = 2
SLOT = 8
LINES = 32
LANES = 128


def on_device(tokens, timesteps, cotangent, qkv_weight, output_weight, time_weight):
    height, cols, width = tokens.shape[1:]
    row_first = lax.axis_index("row") * height
    col_first = lax.axis_index("col") * cols
    total_rows = height * lax.axis_size("row")
    total_cols = cols * lax.axis_size("col")
    tok = tokens[0].transpose(1, 0, 2)
    cot = cotangent[0].transpose(1, 0, 2)
    both = jnp.concatenate([tok, cot], axis=0)
    above, below = exchange(both[:, height - REACH :], both[:, :REACH], "row")
    rows = -(-(height + 2 * REACH) // 16) * 16
    blank = jnp.zeros((2 * cols, rows - height - 2 * REACH, width), jnp.bfloat16)
    both = jnp.concatenate([above, both, below, blank], axis=1)
    tok, cot = both[:cols], both[cols:]
    to_next = jnp.concatenate([tok[cols - REACH :], cot[cols - RADIUS :]], axis=0)
    to_previous = jnp.concatenate([tok[:REACH], cot[:RADIUS]], axis=0)
    left, right = exchange(to_next, to_previous, "col")
    features = fourier(timesteps[0])
    adaptive = 1.0 + jnp.dot(
        features[None], time_weight.astype(jnp.float32), precision=lax.Precision.HIGHEST
    )
    image = lax.axis_index(("zone", "core"))
    place = [row_first, col_first, image, lax.axis_index("core"), timesteps[0]]
    place = jnp.stack(place).astype(jnp.int32)

    around = cols + 2 * REACH
    query_cols = cols + REACH
    lanes = width // HEAD_DIM * SPAN * rows
    smem = pl.BlockSpec(memory_space=pltpu.SMEM)
    vmem = pl.BlockSpec(memory_space=pltpu.VMEM)
    limits = pltpu.CompilerParams(vmem_limit_bytes=40 * 2**20)
    block = jax.ShapeDtypeStruct((cols, rows, width), jnp.bfloat16)
    flat = jax.ShapeDtypeStruct((cols * rows, width), jnp.float32)
    prepared = pl.pallas_call(
        functools.partial(own_kernel, total_rows),
        out_shape=(block,) * 4 + (jax.ShapeDtypeStruct((WINDOW, rows, lanes), jnp.float32),) + (flat,) * 4,
        in_specs=[smem] + [vmem] * 5,
        out_specs=(vmem,) * 9,
        compiler_params=limits,
        cost_estimate=pl.CostEstimate(flops=1_000_000_000, bytes_accessed=4_000_000, transcendentals=200_000),
        name="own",
    )(place, tok, cot, adaptive, qkv_weight, output_weight)
    pieces = width // CORES // LINES * (4 * width // LANES)
    chunks = jax.ShapeDtypeStruct((pieces, LINES + SLOT, LANES), jnp.bfloat16)
    wide = pltpu.VMEM((around, rows, width), jnp.bfloat16)
    result, grad_tokens, mine, other = pl.pallas_call(
        functools.partial(block_kernel, (height, total_cols)),
        out_shape=(block, block, chunks, chunks),
        in_specs=[smem] + [vmem] * 16,
        out_specs=(vmem,) * 4,
        scratch_shapes=[
            wide,
            wide,
            wide,
            pltpu.VMEM((query_cols, rows, width), jnp.bfloat16),
            pltpu.VMEM((query_cols, rows, width), jnp.bfloat16),
            pltpu.VMEM((query_cols, rows, width), jnp.float32),
            pltpu.VMEM((around, rows, width), jnp.float32),
            pltpu.VMEM((around, rows, width), jnp.float32),
            pltpu.VMEM((width, 4 * width), jnp.float32),
        ],
        compiler_params=limits,
        cost_estimate=pl.CostEstimate(flops=8_000_000_000, bytes_accessed=4_000_000, transcendentals=1_000_000),
        name="block",
    )(place, tok, cot, left, right, adaptive, qkv_weight, output_weight, *prepared)
    result = result[:, REACH : REACH + height].transpose(1, 0, 2)
    grad_tokens = grad_tokens[:, REACH : REACH + height].transpose(1, 0, 2)

    mine, other = summed(mine, other)
    total_qkv, total_output, total_time = pl.pallas_call(
        functools.partial(finish_kernel, (lax.axis_size("zone") * CORES, lax.axis_size("row") * lax.axis_size("col"))),
        out_shape=(
            jax.ShapeDtypeStruct((width, 3 * width), jnp.float32),
            jax.ShapeDtypeStruct((width, width), jnp.float32),
            jax.ShapeDtypeStruct((CF, width), jnp.float32),
        ),
        in_specs=[smem, vmem, vmem],
        out_specs=(vmem,) * 3,
        name="finish",
    )(place, mine, other)
    return (result[None], grad_tokens[None], total_qkv, total_output, total_time)


def swap(pieces, axes):
    return lax.all_to_all(pieces, axes, 0, 0, tiled=True)


def total(pieces):
    return jnp.sum(pieces.astype(jnp.float32), axis=0).astype(jnp.bfloat16)


def copied(piece, axes):
    count = lax.axis_size(axes)
    return lax.optimization_barrier(jnp.broadcast_to(piece[None], (count,) + piece.shape))


def summed(mine, other):
    partner = [(0, 1), (1, 0)]
    mine = total(jnp.stack([mine, lax.ppermute(other, "core", partner)]))
    piece = total(swap(mine, "col"))
    piece = total(swap(copied(piece, ("zone", "row")), ("zone", "row")))
    mine = swap(copied(piece, "col"), "col")
    return mine, lax.ppermute(mine, "core", partner)


def solution(mesh):
    shape = (mesh.shape["dp"] // CORES, CORES, mesh.shape["row"], mesh.shape["col"])
    mesh = jax.sharding.Mesh(mesh.devices.reshape(shape), ("zone", "core", "row", "col"))
    grid = P(("zone", "core"), "row", "col", None)
    in_specs = (grid, P(("zone", "core")), grid, P(), P(), P())
    out_specs = (grid, grid, P(), P(), P())
    return jax.shard_map(
        on_device, mesh=mesh, in_specs=in_specs, out_specs=out_specs, check_vma=False
    )
```

time: 109 us -> 105 us (0.963)
  the two profiles are of different devices: /device:TPU:72 before, /device:TPU:1 now
where the time goes in v3:
time: 105 us; the launch traced here: 104 us
  blocking collectives  53.4 us (51%)
  starting transfers between devices  22.2 us (21%)
  Pallas kernels  14.2 us (14%)
  waiting for transfers between devices  8.49 us (8%)
  local copies, waits for them, and re-layouts  3.64 us (3%)
  between operations  1.54 us (1%)
    all_to_all x3, blocking collectives, swap(): return lax.all_to_all(pieces, axes, 0, 0, tiled=True)  53.4 us
    pallas_call x1, Pallas kernels, on_device(): pl.pallas_call(functools.partial(block_kernel, (height, total_cols)), out...  10.2 us
    ppermute x2, starting transfers between devices, exchange(): lax.ppermute(to_next, axis, forward)  8.03 us
    ppermute x2, waiting for transfers between devices, exchange(): lax.ppermute(to_previous, axis, backward)  7.25 us
    ppermute x1, starting transfers between devices, summed(): return (mine, lax.ppermute(mine, 'core', partner))  6.32 us
    ppermute x1, starting transfers between devices, summed(): mine = total(jnp.stack([mine, lax.ppermute(other, 'core', partner)]))  5.16 us
    pallas_call x1, Pallas kernels, on_device(): pl.pallas_call(functools.partial(finish_kernel, (lax.axis_size('zone') *...  2.72 us
    ppermute x2, starting transfers between devices, exchange(): lax.ppermute(to_previous, axis, backward)  2.72 us
  transfers between devices with their start and end apart: 6, of which 3 were waited for; matrix products, arithmetic and copies ran while one was open for 2% of the time, Pallas kernels for 1%

profile of v3, /device:TPU:1, one launch (start us, length us, event | category | flops | bytes accessed | tf_op | source)
XLA Modules:
  0.0 104.3 jit_solution(15186150109651125225)
XLA Ops:
  0.6 0.0 copy-start
  0.6 1.1 %copy_bitcast_fusion = (bf16[8,32,256]{2,1,0:T(8,128)(2,1)S(1)}, bf16[8,32,256]{2,1,0:T(8,128)(2,1)S(1)}) fusion(bf16[1,32,8,256]{3,2,1,0:T(8,128)(2,1)} %param.8, bf16[1,32,8,256]{3,2,1,0:T(8,128)(2,1)} %param.6), kind=kLoop, calls=%fused_computation.3 | loop fusion | bytes 524288 | tf_op jit(solution)/shard_map/transpose | solution.py:330
  1.7 4.8 %collective-permute-start = (bf16[16,6,256]{2,1,0:T(8,128)(2,1)S(1)}, bf16[16,6,256]{2,1,0:T(8,128)(2,1)S(1)}, u32[]{:S(2)}, u32[]{:S(2)}) collective-permute-start(bf16[16,6,256]{2,1,0:T(8,128)(2,1)S(1)} %get-tuple-element.53), channel_id=1, source_target_pairs={{0,32},{32,64},{64,96},{1,33},{33,65},{65,97},{2,34},{34,66},{66,9... | collective-permute-start | bytes 147464 | tf_op jit(solution)/shard_map/ppermute | solution.py:34
  6.6 1.3 %collective-permute-start.1 = (bf16[16,6,256]{2,1,0:T(8,128)(2,1)S(1)}, bf16[16,6,256]{2,1,0:T(8,128)(2,1)S(1)}, u32[]{:S(2)}, u32[]{:S(2)}) collective-permute-start(bf16[16,6,256]{2,1,0:T(8,128)(2,1)S(1)} %get-tuple-element.54), channel_id=1, source_target_pairs={{32,0},{64,32},{96,64},{33,1},{65,33},{97,65},{34,2},{66,34},{98,6... | collective-permute-start | bytes 147464 | tf_op jit(solution)/shard_map/ppermute | solution.py:34
  8.6 0.0 copy-done
  8.6 0.1 fusion.5
  8.8 0.1 pad.10.clone
  8.9 0.1 stack.22.place_ref
  8.9 0.0 copy-start.1
  8.9 0.0 collective-permute-done
  8.9 3.3 %collective-permute-done.1 = bf16[16,6,256]{2,1,0:T(8,128)(2,1)S(1)} collective-permute-done((bf16[16,6,256]{2,1,0:T(8,128)(2,1)S(1)}, bf16[16,6,256]{2,1,0:T(8,128)(2,1)S(1)}, u32[]{:S(2)}, u32[]{:S(2)}) %collective-permute-start.1) | collective-permute-done | bytes 49184 | tf_op jit(solution)/shard_map/ppermute | solution.py:34
  12.2 0.3 maximum_maximum_fusion
  12.6 3.2 %collective-permute-start.2 = (bf16[9,48,256]{2,1,0:T(8,128)(2,1)S(1)}, bf16[9,48,256]{2,1,0:T(8,128)(2,1)S(1)}, u32[]{:S(2)}, u32[]{:S(2)}) collective-permute-start(bf16[9,48,256]{2,1,0:T(8,128)(2,1)S(1)} %pad_maximum_fusion), channel_id=1, source_target_pairs={{0,1},{1,2},{2,3},{3,4},{4,5},{5,6},{6,7},{7,8},{8,9},{9,10},{10,1... | collective-permute-start | bytes 663560 | tf_op jit(solution)/shard_map/ppermute | solution.py:34
  15.8 0.0 copy-start.2
  15.8 0.0 copy-start.3
  15.8 1.4 %collective-permute-start.3 = (bf16[9,48,256]{2,1,0:T(8,128)(2,1)S(1)}, bf16[9,48,256]{2,1,0:T(8,128)(2,1)S(1)}, u32[]{:S(2)}, u32[]{:S(2)}) collective-permute-start(bf16[9,48,256]{2,1,0:T(8,128)(2,1)S(1)} %pad_maximum_fusion.1), channel_id=1, source_target_pairs={{1,0},{2,1},{3,2},{4,3},{5,4},{6,5},{7,6},{8,7},{9,8},{10,9},{11,1... | collective-permute-start | bytes 663560 | tf_op jit(solution)/shard_map/ppermute | solution.py:34
  17.3 0.0 copy-done.2
  17.3 0.0 copy-done.3
  17.3 1.3 %own.1 = (bf16[8,48,256]{2,1,0:T(8,128)(2,1)S(1)}, bf16[8,48,256]{2,1,0:T(8,128)(2,1)S(1)}, bf16[8,48,256]{2,1,0:T(8,128)(2,1)S(1)}, bf16[8,48,256]{2,1,0:T(8,12...) custom-call(s32[5]{0:T(128)S(1)} %stack.22.place_ref, ...), custom_call_target="tpu_custom_call" | custom-call | flops 1000000000 | bytes 4000000 | tf_op jit(solution)/shard_map/own/pallas_call | solution.py:356
  18.7 0.0 collective-permute-done.2.low_ref
  18.7 4.0 %collective-permute-done.3.high_ref = bf16[9,48,256]{2,1,0:T(8,128)(2,1)S(1)} collective-permute-done((bf16[9,48,256]{2,1,0:T(8,128)(2,1)S(1)}, bf16[9,48,256]{2,1,0:T(8,128)(2,1)S(1)}, u32[]{:S(2)}, u32[]{:S(2)}) %collective-permute-start.3) | collective-permute-done | bytes 221216 | tf_op jit(solution)/shard_map/ppermute | solution.py:34
  22.6 0.0 copy-done.1
  22.6 10.2 %block.1 = (bf16[8,48,256]{2,1,0:T(8,128)(2,1)S(1)}, bf16[8,48,256]{2,1,0:T(8,128)(2,1)S(1)}, bf16[32,40,128]{2,1,0:T(8,128)(2,1)S(1)}, bf16[32,40,128]{2,1,0:T(8,128)(2,1)S(1)}) custom-call(s32[5]{0:T(128)S(1)} %stack.22.place_ref, bf16[8,48,256]{2,1,0:T(8,128)(2,1)S(1)} %get-tuple-element.52.tok_ref, bf16[8,48,256]{2,1,0:T(8,128)(2,1)S(1)} %get-tuple-element.51.cot_ref, ...), custom_call_target="tpu_custom_call" | custom-call | flops 8000000000 | bytes 4000000 | tf_op jit(solution)/shard_map/block/pallas_call | solution.py:368
  32.8 5.2 %collective-permute-start.4 = (bf16[32,40,128]{2,1,0:T(8,128)(2,1)S(1)}, bf16[32,40,128]{2,1,0:T(8,128)(2,1)S(1)}, u32[]{:S(2)}, u32[]{:S(2)}) collective-permute-start(bf16[32,40,128]{2,1,0:T(8,128)(2,1)S(1)} %get-tuple-element.33), channel_id=1, source_target_pairs={{0,128},{128,0},{1,129},{129,1},{2,130},{130,2},{3,131},{131,3},{4... | collective-permute-start | bytes 983048 | tf_op jit(solution)/shard_map/ppermute | solution.py:421
  38.0 1.2 %collective-permute-done.4 = bf16[32,40,128]{2,1,0:T(8,128)(2,1)S(1)} collective-permute-done((bf16[32,40,128]{2,1,0:T(8,128)(2,1)S(1)}, bf16[32,40,128]{2,1,0:T(8,128)(2,1)S(1)}, u32[]{:S(2)}, u32[]{:S(2)}) %collective-permute-start.4) | collective-permute-done | bytes 327712 | tf_op jit(solution)/shard_map/ppermute | solution.py:421
  39.2 0.1 reduce_sum.34
  39.3 20.1 %all_to_all.15 = bf16[32,40,128]{2,1,0:T(8,128)(2,1)S(1)} all-to-all(bf16[32,40,128]{2,1,0:T(8,128)(2,1)S(1)} %reduce_sum.34), channel_id=1, replica_groups=mesh['zone'=2,'core'=2,'row'=4,'col'=32] {'col'}, dimensions={0} | all-to-all | bytes 655360 | tf_op jit(solution)/shard_map/all_to_all | solution.py:407
  59.5 0.1 reduce_sum.35
  59.6 16.0 %all_to_all.16 = bf16[8,40,128]{2,1,0:T(8,128)(2,1)S(1)} all-to-all(bf16[8,40,128]{2,1,0:T(8,128)(2,1)S(1)} %broadcast_in_dim.25), channel_id=1, replica_groups=mesh['zone'=2,'core'=2,'row'=4,'col'=32] {'zone','row'}, dimensions={0} | all-to-all | bytes 163840 | tf_op jit(solution)/shard_map/all_to_all | solution.py:407
  75.6 17.3 %all_to_all.17.mine_ref = bf16[32,40,128]{2,1,0:T(8,128)(2,1)S(1)} all-to-all(bf16[32,40,128]{2,1,0:T(8,128)(2,1)S(1)} %broadcast_in_dim.26), channel_id=1, replica_groups=mesh['zone'=2,'core'=2,'row'=4,'col'=32] {'col'}, dimensions={0} | all-to-all | bytes 655360 | tf_op jit(solution)/shard_map/all_to_all | solution.py:407
  92.9 0.0 copy-start.4
  92.9 6.3 %collective-permute-start.5 = (bf16[32,40,128]{2,1,0:T(8,128)(2,1)S(1)}, bf16[32,40,128]{2,1,0:T(8,128)(2,1)S(1)}, u32[]{:S(2)}, u32[]{:S(2)}) collective-permute-start(bf16[32,40,128]{2,1,0:T(8,128)(2,1)S(1)} %all_to_all.17.mine_ref), channel_id=1, source_target_pairs={{0,128},{128,0},{1,129},{129,1},{2,130},{130,2},{3,131},{131,3},{4... | collective-permute-start | bytes 983048 | tf_op jit(solution)/shard_map/ppermute | solution.py:425
  99.3 0.7 copy.17
  100.1 0.0 copy-done.4
  100.1 0.7 copy.18
  100.8 0.0 collective-permute-done.5.other_ref
  100.8 0.0 copy-start.5
  100.8 0.7 copy-done.5
  101.6 2.7 %finish.1 = (f32[256,768]{1,0:T(8,128)}, f32[256,256]{1,0:T(8,128)}, f32[256,256]{1,0:T(8,128)}) custom-call(s32[5]{0:T(128)} %copy-done.1, bf16[32,40,128]{2,1,0:T(8,128)(2,1)} %copy-done.4, bf16[32,40,128]{2,1,0:T(8,128)(2,1)} %copy-done.5), custom_call_target="tpu_custom_call" | custom-call | tf_op jit(solution)/shard_map/finish/pallas_call | solution.py:392
  (15 shorter events, 0.4 us)
Async XLA Ops:
  0.6 7.9 %copy-start = (bf16[256,256]{1,0:T(8,128)(2,1)S(1)}, bf16[256,256]{1,0:T(8,128)(2,1)}, u32[]{:S(2)}) copy-start(bf16[256,256]{1,0:T(8,128)(2,1)} %param.11) | copy-start | bytes 393220
  1.7 7.2 %collective-permute-start = (bf16[16,6,256]{2,1,0:T(8,128)(2,1)S(1)}, bf16[16,6,256]{2,1,0:T(8,128)(2,1)S(1)}, u32[]{:S(2)}, u32[]{:S(2)}) collective-permute-start(bf16[16,6,256]{2,1,0:T(8,128)(2,1)S(1)} %get-tuple-element.53), channel_id=1, source_target_pairs={{0,32},{32,64},{64,96},{1,33},{33,65},{65,97},{2,34},{34,66},{66,9... | collective-permute-start | bytes 147464 | tf_op jit(solution)/shard_map/ppermute | solution.py:34
  6.6 5.6 %collective-permute-start.1 = (bf16[16,6,256]{2,1,0:T(8,128)(2,1)S(1)}, bf16[16,6,256]{2,1,0:T(8,128)(2,1)S(1)}, u32[]{:S(2)}, u32[]{:S(2)}) collective-permute-start(bf16[16,6,256]{2,1,0:T(8,128)(2,1)S(1)} %get-tuple-element.54), channel_id=1, source_target_pairs={{32,0},{64,32},{96,64},{33,1},{65,33},{97,65},{34,2},{66,34},{98,6... | collective-permute-start | bytes 147464 | tf_op jit(solution)/shard_map/ppermute | solution.py:34
  8.9 13.7 %copy-start.1 = (s32[5]{0:T(128)}, s32[5]{0:T(128)S(1)}, u32[]{:S(2)}) copy-start(s32[5]{0:T(128)S(1)} %stack.22.place_ref) | copy-start | bytes 64
  12.6 6.1 %collective-permute-start.2 = (bf16[9,48,256]{2,1,0:T(8,128)(2,1)S(1)}, bf16[9,48,256]{2,1,0:T(8,128)(2,1)S(1)}, u32[]{:S(2)}, u32[]{:S(2)}) collective-permute-start(bf16[9,48,256]{2,1,0:T(8,128)(2,1)S(1)} %pad_maximum_fusion), channel_id=1, source_target_pairs={{0,1},{1,2},{2,3},{3,4},{4,5},{5,6},{6,7},{7,8},{8,9},{9,10},{10,1... | collective-permute-start | bytes 663560 | tf_op jit(solution)/shard_map/ppermute | solution.py:34
  15.8 1.5 %copy-start.2 = (bf16[256,768]{1,0:T(8,128)(2,1)S(1)}, bf16[256,768]{1,0:T(8,128)(2,1)}, u32[]{:S(2)}) copy-start(bf16[256,768]{1,0:T(8,128)(2,1)} %qkv_ref.3) | copy-start | bytes 1179652
  15.8 1.5 %copy-start.3 = (bf16[256,256]{1,0:T(8,128)(2,1)S(1)}, bf16[256,256]{1,0:T(8,128)(2,1)}, u32[]{:S(2)}) copy-start(bf16[256,256]{1,0:T(8,128)(2,1)} %out_ref.3) | copy-start | bytes 393220
  15.8 6.8 %collective-permute-start.3 = (bf16[9,48,256]{2,1,0:T(8,128)(2,1)S(1)}, bf16[9,48,256]{2,1,0:T(8,128)(2,1)S(1)}, u32[]{:S(2)}, u32[]{:S(2)}) collective-permute-start(bf16[9,48,256]{2,1,0:T(8,128)(2,1)S(1)} %pad_maximum_fusion.1), channel_id=1, source_target_pairs={{1,0},{2,1},{3,2},{4,3},{5,4},{6,5},{7,6},{8,7},{9,8},{10,9},{11,1... | collective-permute-start | bytes 663560 | tf_op jit(solution)/shard_map/ppermute | solution.py:34
  32.8 6.4 %collective-permute-start.4 = (bf16[32,40,128]{2,1,0:T(8,128)(2,1)S(1)}, bf16[32,40,128]{2,1,0:T(8,128)(2,1)S(1)}, u32[]{:S(2)}, u32[]{:S(2)}) collective-permute-start(bf16[32,40,128]{2,1,0:T(8,128)(2,1)S(1)} %get-tuple-element.33), channel_id=1, source_target_pairs={{0,128},{128,0},{1,129},{129,1},{2,130},{130,2},{3,131},{131,3},{4... | collective-permute-start | bytes 983048 | tf_op jit(solution)/shard_map/ppermute | solution.py:421
  92.9 7.2 %copy-start.4 = (bf16[32,40,128]{2,1,0:T(8,128)(2,1)}, bf16[32,40,128]{2,1,0:T(8,128)(2,1)S(1)}, u32[]{:S(2)}) copy-start(bf16[32,40,128]{2,1,0:T(8,128)(2,1)S(1)} %all_to_all.17.mine_ref) | copy-start | bytes 983044
  92.9 7.9 %collective-permute-start.5 = (bf16[32,40,128]{2,1,0:T(8,128)(2,1)S(1)}, bf16[32,40,128]{2,1,0:T(8,128)(2,1)S(1)}, u32[]{:S(2)}, u32[]{:S(2)}) collective-permute-start(bf16[32,40,128]{2,1,0:T(8,128)(2,1)S(1)} %all_to_all.17.mine_ref), channel_id=1, source_target_pairs={{0,128},{128,0},{1,129},{129,1},{2,130},{130,2},{3,131},{131,3},{4... | collective-permute-start | bytes 983048 | tf_op jit(solution)/shard_map/ppermute | solution.py:425
  100.8 0.7 copy-start.5

commit v4 on v3

--- a/solution.py
+++ b/solution.py
@@ -12,6 +12,7 @@
 CF = 256
 RADIUS = 3
 REACH = 2 * RADIUS
+EDGE = 8
 SPAN = 2
 WINDOW = SPAN + REACH
 
@@ -27,11 +28,16 @@
     return jnp.concatenate([jnp.cos(phase_angle), jnp.sin(phase_angle)])
 
 
-def exchange(to_next, to_previous, axis):
-    count = lax.axis_size(axis)
-    forward = [(i, i + 1) for i in range(count - 1)]
-    backward = [(target, source) for source, target in forward]
-    return lax.ppermute(to_next, axis, forward), lax.ppermute(to_previous, axis, backward)
+def shifted(block, row_step, col_step):
+    down = lax.axis_size("row")
+    across = lax.axis_size("col")
+    pairs = [
+        (row * across + col, (row + row_step) * across + col + col_step)
+        for row in range(down)
+        for col in range(across)
+        if 0 <= row + row_step < down and 0 <= col + col_step < across
+    ]
+    return lax.ppermute(block, ("row", "col"), pairs)
 
 
 def nn(left, right):
@@ -63,20 +69,16 @@
     return inverse, (pixels * inverse * adaptive).astype(jnp.bfloat16)
 
 
-def project_to(pixels, adaptive, qkv_ref, average, query_ref, key_ref, value_ref, here):
+def projected(pixels, adaptive, qkv_ref, average):
     width = pixels.shape[-1]
-    shape = (-1,) + query_ref.shape[1:]
     inverse, normed = normalized(pixels, adaptive)
     project = nn(normed, qkv_ref[...])
     query_raw = project[:, :width]
     key_raw = project[:, width : 2 * width]
     query_inv = lax.rsqrt(head_mean(query_raw * query_raw, average) + epsilon)
     key_inv = lax.rsqrt(head_mean(key_raw * key_raw, average) + epsilon)
-    factor = score_scale / HEAD_DIM
-    query_ref[here] = (query_raw * query_inv * factor).astype(jnp.bfloat16).reshape(shape)
-    key_ref[here] = (key_raw * key_inv).astype(jnp.bfloat16).reshape(shape)
-    value_ref[here] = project[:, 2 * width :].astype(jnp.bfloat16).reshape(shape)
-    return inverse, normed, query_raw, query_inv, key_raw, key_inv
+    query = query_raw * query_inv * (score_scale / HEAD_DIM)
+    return inverse, normed, query, key_raw * key_inv, project[:, 2 * width :], (query_raw, query_inv, key_raw, key_inv)
 
 
 def own_kernel(
@@ -97,41 +99,49 @@
     key_raw_ref,
     key_inv_ref,
 ):
-    cols, rows, width = tok_ref.shape
-    lanes = mask_ref.shape[2]
+    cols, height, width = tok_ref.shape
+    _, rows, lanes = mask_ref.shape
     row_first = place_ref[0]
-    pixels = tok_ref[...].astype(jnp.float32).reshape(cols * rows, width)
-    _, _, query_raw, query_inv, key_raw, key_inv = project_to(
-        pixels, adaptive_ref[...], qkv_ref, average_matrix(width), query_ref, key_ref, value_ref, pl.ds(0, cols)
-    )
-    query_raw_ref[...] = query_raw
-    query_inv_ref[...] = query_inv
-    key_raw_ref[...] = key_raw
-    key_inv_ref[...] = key_inv
-    cot_own = cot_ref[...].reshape(cols * rows, width)
-    grad_ref[...] = nt(cot_own, out_ref[...]).astype(jnp.bfloat16).reshape(cols, rows, width)
-
-    shape = (WINDOW, rows, lanes)
-    key_row = lax.broadcasted_iota(jnp.int32, shape, 1)
-    key_col = lax.broadcasted_iota(jnp.int32, shape, 0)
+    pixels = tok_ref[...].astype(jnp.float32).reshape(cols * height, width)
+    _, _, query, key, value, raw = projected(pixels, adaptive_ref[...], qkv_ref, average_matrix(width))
+    query_ref[...] = query.astype(jnp.bfloat16).reshape(cols, height, width)
+    key_ref[...] = key.astype(jnp.bfloat16).reshape(cols, height, width)
+    value_ref[...] = value.astype(jnp.bfloat16).reshape(cols, height, width)
+    for ref, values in zip((query_raw_ref, query_inv_ref, key_raw_ref, key_inv_ref), raw):
+        ref[...] = values
+    cot_own = cot_ref[...].reshape(cols * height, width)
+    grad_ref[...] = nt(cot_own, out_ref[...]).astype(jnp.bfloat16).reshape(cols, height, width)
+
+    def row_at(position):
+        halo = jnp.where(position < height + EDGE, position - height - EDGE, position - EDGE)
+        return jnp.where(position < height, position, halo)
+
+    key_row = row_at(lax.broadcasted_iota(jnp.int32, (1, rows, 1), 1))
+    key_col = lax.broadcasted_iota(jnp.int32, (WINDOW, 1, 1), 0)
     lane = lax.broadcasted_iota(jnp.int32, (1, 1, lanes), 2) % (SPAN * rows)
+    query_row = row_at(lane % rows)
     query_col = lane // rows
-    query_row = lane % rows
     row_gap = key_row - query_row
     col_gap = key_col - query_col
-    image_row = row_first + key_row - REACH
-    allowed = (row_gap >= -RADIUS) & (row_gap <= RADIUS) & (col_gap >= 0) & (col_gap <= REACH)
-    allowed = allowed & (image_row >= 0) & (image_row < total_rows)
-    mask_ref[...] = jnp.where(allowed, 1.0, 0.0)
+    image_row = jnp.broadcast_to(row_first + key_row, row_gap.shape)
+    near_row = (row_gap >= -RADIUS) & (row_gap <= RADIUS) & (image_row >= 0) & (image_row < total_rows)
+    near_col = (col_gap >= 0) & (col_gap <= REACH)
+    mask_ref[...] = jnp.where(near_row, 1.0, 0.0) * jnp.where(near_col, 1.0, 0.0)
 
 
 def block_kernel(
-    sizes,
+    total_cols,
     place_ref,
     tok_ref,
     cot_ref,
-    low_ref,
-    high_ref,
+    above_ref,
+    below_ref,
+    left_ref,
+    left_above_ref,
+    left_below_ref,
+    right_ref,
+    right_above_ref,
+    right_below_ref,
     adaptive_ref,
     qkv_ref,
     out_ref,
@@ -158,11 +168,10 @@
     grad_value_ref,
     whole_ref,
 ):
-    height, total_cols = sizes
-    cols, rows, width = tok_ref.shape
+    cols, height, width = tok_ref.shape
+    rows = mask_ref.shape[1]
     heads = width // HEAD_DIM
     query_cols = cols + REACH
-    lanes = heads * SPAN * rows
     col_first = place_ref[1]
     image = place_ref[2]
     core = place_ref[3]
@@ -171,23 +180,53 @@
     factor = score_scale / HEAD_DIM
     average = average_matrix(width)
 
-    for ref, first in ((low_ref, 0), (high_ref, REACH + cols)):
-        pixels = ref[:REACH].astype(jnp.float32).reshape(REACH * rows, width)
-        project_to(pixels, adaptive, qkv_ref, average, query_ref, key_ref, value_ref, pl.ds(first, REACH))
-    query_ref[pl.ds(REACH, cols)] = own_query_ref[...]
-    key_ref[pl.ds(REACH, cols)] = own_key_ref[...]
-    value_ref[pl.ds(REACH, cols)] = own_value_ref[...]
-    grad_ref[pl.ds(RADIUS, cols)] = own_grad_ref[...]
-    for ref, first in ((low_ref, 0), (high_ref, RADIUS + cols)):
-        side = ref[REACH:].reshape(RADIUS * rows, width)
-        grad_ref[pl.ds(first, RADIUS)] = nt(side, out_ref[...]).astype(jnp.bfloat16).reshape(RADIUS, rows, width)
+    last = REACH + cols
+    pieces = (
+        (left_ref, REACH, 0, 0),
+        (right_ref, REACH, last, 0),
+        (above_ref, cols, REACH, height),
+        (below_ref, cols, REACH, height + EDGE),
+        (left_above_ref, REACH, 0, height),
+        (left_below_ref, REACH, 0, height + EDGE),
+        (right_above_ref, REACH, last, height),
+        (right_below_ref, REACH, last, height + EDGE),
+    )
+
+    def place_rows(values, targets):
+        first = 0
+        for ref, count, tall, col, row in targets:
+            part = values[first : first + count * tall].reshape(count, tall, width)
+            ref[pl.ds(col, count), pl.ds(row, tall)] = part.astype(jnp.bfloat16)
+            first += count * tall
+
+    for group in (pieces[:2], pieces[2:]):
+        pixels = jnp.concatenate(
+            [ref[:count].astype(jnp.float32).reshape(count * ref.shape[1], width) for ref, count, _, _ in group], axis=0
+        )
+        _, _, query, key, value, _ = projected(pixels, adaptive, qkv_ref, average)
+        for values, target in ((query, query_ref), (key, key_ref), (value, value_ref)):
+            place_rows(values, [(target, count, ref.shape[1], col, row) for ref, count, col, row in group])
+    sides = []
+    targets = []
+    for ref, count, col, row in pieces:
+        tall = ref.shape[1]
+        sides.append(ref[count:].astype(jnp.float32).reshape(-1, width))
+        targets.append((grad_ref, ref.shape[0] - count, tall, 0 if col == 0 else col - RADIUS, row))
+    side = jnp.concatenate(sides, axis=0).astype(jnp.bfloat16)
+    place_rows(nt(side, out_ref[...]), targets)
+    for target, source, col in (
+        (query_ref, own_query_ref, REACH),
+        (key_ref, own_key_ref, REACH),
+        (value_ref, own_value_ref, REACH),
+        (grad_ref, own_grad_ref, RADIUS),
+    ):
+        target[pl.ds(col, cols), pl.ds(0, height)] = source[...]
 
     grad_key_ref[...] = jnp.zeros_like(grad_key_ref)
     grad_value_ref[...] = jnp.zeros_like(grad_value_ref)
     lane_head = lax.broadcasted_iota(jnp.int32, (1, width), 1) // HEAD_DIM
     picks = [jnp.where(lane_head == head, 1.0, 0.0) for head in range(heads)]
     narrow = [pick.astype(jnp.bfloat16) for pick in picks]
-    column = lax.broadcasted_iota(jnp.int32, (WINDOW, 1, 1), 0)
 
     def spread(values):
         return jnp.concatenate([values * pick for pick in narrow], axis=0)
@@ -196,56 +235,64 @@
         total = values[: SPAN * rows] * picks[0]
         for head in range(1, heads):
             total = total + values[head * SPAN * rows : (head + 1) * SPAN * rows] * picks[head]
-        return total
-
-    def step(index, carry):
-        start = SPAN * index
+        return total.reshape(SPAN, rows, width)[:, :height]
+
+    for start in range(0, query_cols, SPAN):
         near = pl.ds(start, WINDOW)
         keys = key_ref[near].reshape(WINDOW * rows, width)
         values = value_ref[near].reshape(WINDOW * rows, width)
         queries = spread(query_ref[pl.ds(start + RADIUS, SPAN)].reshape(SPAN * rows, width))
         grads = spread(grad_ref[pl.ds(start, SPAN)].reshape(SPAN * rows, width))
-        image_col = col_first + start + column - REACH
-        inside = jnp.where((image_col >= 0) & (image_col < total_cols), 1.0, 0.0)
-        mask = (mask_ref[...] * inside).reshape(WINDOW * rows, lanes)
-        exponent = jnp.exp(nt(keys, queries) - score_scale) * mask
+        masks = []
+        for column in range(WINDOW):
+            mask = mask_ref[column]
+            if start + column < REACH or start + column >= last:
+                image_col = col_first + (start + column - REACH)
+                mask = mask * jnp.where((image_col >= 0) & (image_col < total_cols), 1.0, 0.0)
+            masks.append(mask)
+        exponent = jnp.exp(nt(keys, queries) - score_scale) * jnp.concatenate(masks, axis=0)
         denominator = jnp.maximum(jnp.sum(exponent, axis=0, keepdims=True), 1e-30)
         weights = (exponent * (1.0 / denominator)).astype(jnp.bfloat16)
         wide = weights.astype(jnp.float32)
         slope = nt(values, grads)
         middle = jnp.sum(wide * slope, axis=0, keepdims=True)
         grad_score = (wide * (slope - middle)).astype(jnp.bfloat16)
-        attended = gathered(tn(weights, values)).astype(jnp.bfloat16)
-        attended_ref[pl.ds(start, SPAN)] = attended.reshape(SPAN, rows, width)
-        grad_query_ref[pl.ds(start, SPAN)] = gathered(tn(grad_score, keys)).reshape(SPAN, rows, width)
-        grad_key_ref[near] += nn(grad_score, queries).reshape(WINDOW, rows, width)
-        grad_value_ref[near] += nn(weights, grads).reshape(WINDOW, rows, width)
-        return carry
-
-    lax.fori_loop(0, query_cols // SPAN, step, 0)
-
-    pixels = tok_ref[...].astype(jnp.float32).reshape(cols * rows, width)
+        low = max(start + RADIUS, REACH)
+        high = min(start + RADIUS + SPAN, last)
+        if low < high:
+            skip = slice(low - start - RADIUS, high - start - RADIUS)
+            there = pl.ds(low - REACH, high - low)
+            attended_ref[there] = gathered(tn(weights, values))[skip].astype(jnp.bfloat16)
+            grad_query_ref[there] = gathered(tn(grad_score, keys))[skip]
+        low = max(start, REACH)
+        high = min(start + WINDOW, last)
+        there = pl.ds(low - REACH, high - low)
+        shape = (WINDOW, rows, heads * SPAN * rows)
+        kept = (high - low, height, width)
+        kept_score = grad_score.reshape(shape)[low - start : high - start, :height].reshape(-1, shape[2])
+        kept_weights = weights.reshape(shape)[low - start : high - start, :height].reshape(-1, shape[2])
+        grad_key_ref[there] += nn(kept_score, queries).reshape(kept)
+        grad_value_ref[there] += nn(kept_weights, grads).reshape(kept)
+
+    tokens = cols * height
+    pixels = tok_ref[...].astype(jnp.float32).reshape(tokens, width)
     inverse, normed = normalized(pixels, adaptive)
-    cot_own = cot_ref[...].reshape(cols * rows, width)
-    row = lax.broadcasted_iota(jnp.int32, (cols, rows, 1), 1)
-    own = jnp.where((row >= REACH) & (row < REACH + height), 1.0, 0.0).reshape(cols * rows, 1)
-    attended = attended_ref[pl.ds(RADIUS, cols)].reshape(cols * rows, width)
+    cot_own = cot_ref[...].reshape(tokens, width)
+    attended = attended_ref[...].reshape(tokens, width)
     result = pixels + nn(attended, out_ref[...])
-    result_ref[...] = result.astype(jnp.bfloat16).reshape(cols, rows, width)
-    cotan = cot_own.astype(jnp.float32)
-    whole_ref[:, 3 * width :] = tn(attended, (cotan * own).astype(jnp.bfloat16))
+    result_ref[...] = result.astype(jnp.bfloat16).reshape(cols, height, width)
+    whole_ref[:, 3 * width :] = tn(attended, cot_own)
 
     def back(raw, inv, grad, scale):
         return scale * inv * (grad - raw * inv * inv * head_mean(grad * raw, average))
 
-    grad_query = grad_query_ref[pl.ds(RADIUS, cols)].reshape(cols * rows, width)
-    grad_key = grad_key_ref[pl.ds(REACH, cols)].reshape(cols * rows, width)
-    grad_value = grad_value_ref[pl.ds(REACH, cols)].reshape(cols * rows, width)
+    grad_query = grad_query_ref[...].reshape(tokens, width)
+    grad_key = grad_key_ref[...].reshape(tokens, width)
     grad_project = jnp.concatenate(
         [
-            (back(query_raw_ref[...], query_inv_ref[...], grad_query, factor) * own).astype(jnp.bfloat16),
-            (back(key_raw_ref[...], key_inv_ref[...], grad_key, 1.0) * own).astype(jnp.bfloat16),
-            (grad_value * own).astype(jnp.bfloat16),
+            back(query_raw_ref[...], query_inv_ref[...], grad_query, factor).astype(jnp.bfloat16),
+            back(key_raw_ref[...], key_inv_ref[...], grad_key, 1.0).astype(jnp.bfloat16),
+            grad_value_ref[...].reshape(tokens, width).astype(jnp.bfloat16),
         ],
         axis=1,
     )
@@ -254,19 +301,19 @@
     scaled = grad_normed * adaptive
     inner = jnp.mean(scaled * pixels, axis=-1, keepdims=True)
     grad_pixels = inverse * (scaled - pixels * (inverse * inverse * inner))
-    grad_tokens_ref[...] = (cotan + grad_pixels).astype(jnp.bfloat16).reshape(cols, rows, width)
+    grad_tokens = cot_own.astype(jnp.float32) + grad_pixels
+    grad_tokens_ref[...] = grad_tokens.astype(jnp.bfloat16).reshape(cols, height, width)
     grad_adaptive = jnp.sum(grad_normed * (pixels * inverse), axis=0, keepdims=True)
 
     half = width // CORES
     across = 4 * width // LANES
-    blocks = mine_ref.shape[0]
     line = lax.broadcasted_iota(jnp.int32, (SLOT, LANES), 0)
     lane = lax.broadcasted_iota(jnp.int32, (SLOT, LANES), 1)
     high = (step_value // 32).astype(jnp.float32)
     low = (step_value % 32).astype(jnp.float32)
     for ref, which in ((mine_ref, core), (other_ref, 1 - core)):
         part = whole_ref[pl.ds(pl.multiple_of(which * half, half), half), :].astype(jnp.bfloat16)
-        for block in range(blocks):
+        for block in range(ref.shape[0]):
             top = block // across * LINES
             first = block % across * LANES
             ref[block, :LINES] = part[top : top + LINES, first : first + LANES]
@@ -328,15 +375,19 @@
     total_cols = cols * lax.axis_size("col")
     tok = tokens[0].transpose(1, 0, 2)
     cot = cotangent[0].transpose(1, 0, 2)
+    rows = height + 2 * EDGE
+    to_right = jnp.concatenate([tok[cols - REACH :], cot[cols - RADIUS :]], axis=0)
+    to_left = jnp.concatenate([tok[:REACH], cot[:RADIUS]], axis=0)
     both = jnp.concatenate([tok, cot], axis=0)
-    above, below = exchange(both[:, height - REACH :], both[:, :REACH], "row")
-    rows = -(-(height + 2 * REACH) // 16) * 16
-    blank = jnp.zeros((2 * cols, rows - height - 2 * REACH, width), jnp.bfloat16)
-    both = jnp.concatenate([above, both, below, blank], axis=1)
-    tok, cot = both[:cols], both[cols:]
-    to_next = jnp.concatenate([tok[cols - REACH :], cot[cols - RADIUS :]], axis=0)
-    to_previous = jnp.concatenate([tok[:REACH], cot[:RADIUS]], axis=0)
-    left, right = exchange(to_next, to_previous, "col")
+    left = shifted(to_right, 0, 1)
+    right = shifted(to_left, 0, -1)
+    above = shifted(both[:, height - EDGE :], 1, 0)
+    below = shifted(both[:, :EDGE], -1, 0)
+    left_above = shifted(to_right[:, height - EDGE :], 1, 1)
+    left_below = shifted(to_right[:, :EDGE], -1, 1)
+    right_above = shifted(to_left[:, height - EDGE :], 1, -1)
+    right_below = shifted(to_left[:, :EDGE], -1, -1)
+    halos = (above, below, left, left_above, left_below, right, right_above, right_below)
     features = fourier(timesteps[0])
     adaptive = 1.0 + jnp.dot(
         features[None], time_weight.astype(jnp.float32), precision=lax.Precision.HIGHEST
@@ -351,8 +402,8 @@
     smem = pl.BlockSpec(memory_space=pltpu.SMEM)
     vmem = pl.BlockSpec(memory_space=pltpu.VMEM)
     limits = pltpu.CompilerParams(vmem_limit_bytes=40 * 2**20)
-    block = jax.ShapeDtypeStruct((cols, rows, width), jnp.bfloat16)
-    flat = jax.ShapeDtypeStruct((cols * rows, width), jnp.float32)
+    block = jax.ShapeDtypeStruct((cols, height, width), jnp.bfloat16)
+    flat = jax.ShapeDtypeStruct((cols * height, width), jnp.float32)
     prepared = pl.pallas_call(
         functools.partial(own_kernel, total_rows),
         out_shape=(block,) * 4 + (jax.ShapeDtypeStruct((WINDOW, rows, lanes), jnp.float32),) + (flat,) * 4,
@@ -366,27 +417,27 @@
     chunks = jax.ShapeDtypeStruct((pieces, LINES + SLOT, LANES), jnp.bfloat16)
     wide = pltpu.VMEM((around, rows, width), jnp.bfloat16)
     result, grad_tokens, mine, other = pl.pallas_call(
-        functools.partial(block_kernel, (height, total_cols)),
+        functools.partial(block_kernel, total_cols),
         out_shape=(block, block, chunks, chunks),
-        in_specs=[smem] + [vmem] * 16,
+        in_specs=[smem] + [vmem] * 22,
         out_specs=(vmem,) * 4,
         scratch_shapes=[
             wide,
             wide,
             wide,
             pltpu.VMEM((query_cols, rows, width), jnp.bfloat16),
-            pltpu.VMEM((query_cols, rows, width), jnp.bfloat16),
-            pltpu.VMEM((query_cols, rows, width), jnp.float32),
-            pltpu.VMEM((around, rows, width), jnp.float32),
-            pltpu.VMEM((around, rows, width), jnp.float32),
+            pltpu.VMEM((cols, height, width), jnp.bfloat16),
+            pltpu.VMEM((cols, height, width), jnp.float32),
+            pltpu.VMEM((cols, height, width), jnp.float32),
+            pltpu.VMEM((cols, height, width), jnp.float32),
             pltpu.VMEM((width, 4 * width), jnp.float32),
         ],
         compiler_params=limits,
         cost_estimate=pl.CostEstimate(flops=8_000_000_000, bytes_accessed=4_000_000, transcendentals=1_000_000),
         name="block",
-    )(place, tok, cot, left, right, adaptive, qkv_weight, output_weight, *prepared)
-    result = result[:, REACH : REACH + height].transpose(1, 0, 2)
-    grad_tokens = grad_tokens[:, REACH : REACH + height].transpose(1, 0, 2)
+    )(place, tok, cot, *halos, adaptive, qkv_weight, output_weight, *prepared)
+    result = result.transpose(1, 0, 2)
+    grad_tokens = grad_tokens.transpose(1, 0, 2)
 
     mine, other = summed(mine, other)
     total_qkv, total_output, total_time = pl.pallas_call(
@@ -398,6 +449,7 @@
         ),
         in_specs=[smem, vmem, vmem],
         out_specs=(vmem,) * 3,
+        compiler_params=pltpu.CompilerParams(vmem_limit_bytes=16 * 2**20),
         name="finish",
     )(place, mine, other)
     return (result[None], grad_tokens[None], total_qkv, total_output, total_time)

time: 105 us -> 110 us (1.048)
  starting transfers between devices: 22.2 us -> 40.7 us
  waiting for transfers between devices: 8.49 us -> 1.26 us
  Pallas kernels: 14.2 us -> 10.2 us
  blocking collectives: 53.4 us -> 52.3 us
    ppermute x4 -> x8, starting transfers between devices: 10.7 us -> 25.3 us  [shifted(): return lax.ppermute(block, ('row', 'col'), pairs)]
    ppermute x4 -> x8, waiting for transfers between devices: 7.25 us -> 0.02 us  [shifted(): return lax.ppermute(block, ('row', 'col'), pairs)]
    ppermute x1, starting transfers between devices: 5.16 us -> 9.16 us  [summed(): mine = total(jnp.stack([mine, lax.ppermute(other, 'core', partner)]))]
    pallas_call x1, Pallas kernels: 10.2 us -> 6.81 us  [on_device(): pl.pallas_call(functools.partial(block_kernel, total_cols), out_shape=(bl...]
    all_to_all x3, blocking collectives: 53.4 us -> 52.3 us  [swap(): return lax.all_to_all(pieces, axes, 0, 0, tiled=True)]
    unnamed x14 -> x8, local copies, waits for them, and re-layouts: 2.22 us -> 1.48 us
  transfers between devices with their start and end apart: 6 -> 10, of which waited for: 3 -> 1; matrix products, arithmetic and copies ran while one was open for 2% -> 2% of each run, Pallas kernels for 1% -> 1%
where the time goes in v4:
time: 110 us; the launch traced here: 109 us
  blocking collectives  52.3 us (48%)
  starting transfers between devices  40.7 us (37%)
  Pallas kernels  10.2 us (9%)
  local copies, waits for them, and re-layouts  2.7 us (2%)
  between operations  1.58 us (1%)
  waiting for transfers between devices  1.26 us (1%)
    all_to_all x3, blocking collectives, swap(): return lax.all_to_all(pieces, axes, 0, 0, tiled=True)  52.3 us
    ppermute x8, starting transfers between devices, shifted(): return lax.ppermute(block, ('row', 'col'), pairs)  25.3 us
    ppermute x1, starting transfers between devices, summed(): mine = total(jnp.stack([mine, lax.ppermute(other, 'core', partner)]))  9.16 us
    pallas_call x1, Pallas kernels, on_device(): pl.pallas_call(functools.partial(block_kernel, total_cols), out_shape=(bl...  6.81 us
    ppermute x1, starting transfers between devices, summed(): return (mine, lax.ppermute(mine, 'core', partner))  6.32 us
  transfers between devices with their start and end apart: 10, of which 1 were waited for; matrix products, arithmetic and copies ran while one was open for 2% of the time, Pallas kernels for 1%

profile of v4, /device:TPU:1, one launch (start us, length us, event | category | flops | bytes accessed | tf_op | source)
XLA Modules:
  0.0 109.3 jit_solution(10953045613961102411)
XLA Ops:
  0.6 0.0 copy-start
  0.6 1.1 copy_bitcast_fusion
  1.8 1.3 %collective-permute-start.7 = (bf16[9,8,256]{2,1,0:T(8,128)(2,1)S(1)}, bf16[9,8,256]{2,1,0:T(8,128)(2,1)S(1)}, u32[]{:S(2)}, u32[]{:S(2)}) collective-permute-start(bf16[9,8,256]{2,1,0:T(8,128)(2,1)S(1)} %get-tuple-element.49), channel_id=1, source_target_pairs={{33,0},{34,1},{35,2},{36,3},{37,4},{38,5},{39,6},{40,7},{41,8},{42... | collective-permute-start | bytes 110600 | tf_op jit(solution)/shard_map/ppermute | solution.py:40
  3.1 0.7 collective-permute-start.6
  3.8 0.7 collective-permute-start.4
  4.4 0.0 copy-start.1
  4.5 8.0 %collective-permute-start.2 = (bf16[9,32,256]{2,1,0:T(8,128)(2,1)S(1)}, bf16[9,32,256]{2,1,0:T(8,128)(2,1)S(1)}, u32[]{:S(2)}, u32[]{:S(2)}) collective-permute-start(bf16[9,32,256]{2,1,0:T(8,128)(2,1)S(1)} %pad_maximum_fusion), channel_id=1, source_target_pairs={{0,1},{1,2},{2,3},{3,4},{4,5},{5,6},{6,7},{7,8},{8,9},{9,10},{10,1... | collective-permute-start | bytes 442376 | tf_op jit(solution)/shard_map/ppermute | solution.py:40
  12.5 1.3 %collective-permute-start.5 = (bf16[9,32,256]{2,1,0:T(8,128)(2,1)S(1)}, bf16[9,32,256]{2,1,0:T(8,128)(2,1)S(1)}, u32[]{:S(2)}, u32[]{:S(2)}) collective-permute-start(bf16[9,32,256]{2,1,0:T(8,128)(2,1)S(1)} %pad_maximum_fusion.1), channel_id=1, source_target_pairs={{1,0},{2,1},{3,2},{4,3},{5,4},{6,5},{7,6},{8,7},{9,8},{10,9},{11,1... | collective-permute-start | bytes 442376 | tf_op jit(solution)/shard_map/ppermute | solution.py:40
  14.5 0.0 copy-done
  14.5 0.1 fusion.8
  14.7 0.0 copy-start.2
  14.7 0.1 stack.22.place_ref
  14.8 0.0 collective-permute-done.7.right_below_ref
  14.8 1.3 %collective-permute-start.1 = (bf16[16,8,256]{2,1,0:T(8,128)(2,1)S(1)}, bf16[16,8,256]{2,1,0:T(8,128)(2,1)S(1)}, u32[]{:S(2)}, u32[]{:S(2)}) collective-permute-start(bf16[16,8,256]{2,1,0:T(8,128)(2,1)S(1)} %get-tuple-element.47), channel_id=1, source_target_pairs={{32,0},{33,1},{34,2},{35,3},{36,4},{37,5},{38,6},{39,7},{40,8},{41... | collective-permute-start | bytes 196616 | tf_op jit(solution)/shard_map/ppermute | solution.py:40
  16.1 0.0 collective-permute-done.6.right_above_ref
  16.1 6.3 %collective-permute-start = (bf16[16,8,256]{2,1,0:T(8,128)(2,1)S(1)}, bf16[16,8,256]{2,1,0:T(8,128)(2,1)S(1)}, u32[]{:S(2)}, u32[]{:S(2)}) collective-permute-start(bf16[16,8,256]{2,1,0:T(8,128)(2,1)S(1)} %get-tuple-element.48), channel_id=1, source_target_pairs={{0,32},{1,33},{2,34},{3,35},{4,36},{5,37},{6,38},{7,39},{8,40},{9,... | collective-permute-start | bytes 196616 | tf_op jit(solution)/shard_map/ppermute | solution.py:40
  22.4 0.0 collective-permute-done.4.left_below_ref
  22.4 5.8 %collective-permute-start.3 = (bf16[9,8,256]{2,1,0:T(8,128)(2,1)S(1)}, bf16[9,8,256]{2,1,0:T(8,128)(2,1)S(1)}, u32[]{:S(2)}, u32[]{:S(2)}) collective-permute-start(bf16[9,8,256]{2,1,0:T(8,128)(2,1)S(1)} %get-tuple-element.52), channel_id=1, source_target_pairs={{0,33},{1,34},{2,35},{3,36},{4,37},{5,38},{6,39},{7,40},{8,41},{9,... | collective-permute-start | bytes 110600 | tf_op jit(solution)/shard_map/ppermute | solution.py:40
  28.2 0.0 copy-done.1
  28.2 0.0 copy-done.2
  28.2 1.2 %own.1 = (bf16[8,32,256]{2,1,0:T(8,128)(2,1)S(1)}, bf16[8,32,256]{2,1,0:T(8,128)(2,1)S(1)}, bf16[8,32,256]{2,1,0:T(8,128)(2,1)S(1)}, bf16[8,32,256]{2,1,0:T(8,12...) custom-call(s32[5]{0:T(128)S(1)} %stack.22.place_ref, ...), custom_call_target="tpu_custom_call" | custom-call | flops 1000000000 | bytes 4000000 | tf_op jit(solution)/shard_map/own/pallas_call | solution.py:407
  29.4 0.0 collective-permute-done.3.left_above_ref
  29.4 0.0 collective-permute-done.1.below_ref
  29.5 0.0 collective-permute-done.above_ref
  29.5 0.0 collective-permute-done.2.left_ref
  29.5 0.0 collective-permute-done.5.right_ref
  29.5 6.8 %block.1 = (bf16[8,32,256]{2,1,0:T(8,128)(2,1)S(1)}, bf16[8,32,256]{2,1,0:T(8,128)(2,1)S(1)}, bf16[32,40,128]{2,1,0:T(8,128)(2,1)S(1)}, bf16[32,40,128]{2,1,0:T(8,128)(2,1)S(1)}) custom-call(s32[5]{0:T(128)S(1)} %stack.22.place_ref, bf16[8,32,256]{2,1,0:T(8,128)(2,1)S(1)} %get-tuple-element.58.tok_ref, bf16[8,32,256]{2,1,0:T(8,128)(2,1)S(1)} %get-tuple-element.57.cot_ref, ...), custom_call_target="tpu_custom_call" | custom-call | flops 8000000000 | bytes 4000000 | tf_op jit(solution)/shard_map/block/pallas_call | solution.py:419
  36.3 9.2 %collective-permute-start.8 = (bf16[32,40,128]{2,1,0:T(8,128)(2,1)S(1)}, bf16[32,40,128]{2,1,0:T(8,128)(2,1)S(1)}, u32[]{:S(2)}, u32[]{:S(2)}) collective-permute-start(bf16[32,40,128]{2,1,0:T(8,128)(2,1)S(1)} %get-tuple-element.33), channel_id=1, source_target_pairs={{0,128},{128,0},{1,129},{129,1},{2,130},{130,2},{3,131},{131,3},{4... | collective-permute-start | bytes 983048 | tf_op jit(solution)/shard_map/ppermute | solution.py:473
  45.5 1.2 %collective-permute-done.8 = bf16[32,40,128]{2,1,0:T(8,128)(2,1)S(1)} collective-permute-done((bf16[32,40,128]{2,1,0:T(8,128)(2,1)S(1)}, bf16[32,40,128]{2,1,0:T(8,128)(2,1)S(1)}, u32[]{:S(2)}, u32[]{:S(2)}) %collective-permute-start.8) | collective-permute-done | bytes 327712 | tf_op jit(solution)/shard_map/ppermute | solution.py:473
  46.7 0.1 reduce_sum.34
  46.8 17.1 %all_to_all.15 = bf16[32,40,128]{2,1,0:T(8,128)(2,1)S(1)} all-to-all(bf16[32,40,128]{2,1,0:T(8,128)(2,1)S(1)} %reduce_sum.34), channel_id=1, replica_groups=mesh['zone'=2,'core'=2,'row'=4,'col'=32] {'col'}, dimensions={0} | all-to-all | bytes 655360 | tf_op jit(solution)/shard_map/all_to_all | solution.py:459
  63.9 0.1 reduce_sum.35
  64.0 17.9 %all_to_all.16 = bf16[8,40,128]{2,1,0:T(8,128)(2,1)S(1)} all-to-all(bf16[8,40,128]{2,1,0:T(8,128)(2,1)S(1)} %broadcast_in_dim.10), channel_id=1, replica_groups=mesh['zone'=2,'core'=2,'row'=4,'col'=32] {'zone','row'}, dimensions={0} | all-to-all | bytes 163840 | tf_op jit(solution)/shard_map/all_to_all | solution.py:459
  81.9 17.3 %all_to_all.17.mine_ref = bf16[32,40,128]{2,1,0:T(8,128)(2,1)S(1)} all-to-all(bf16[32,40,128]{2,1,0:T(8,128)(2,1)S(1)} %broadcast_in_dim.22), channel_id=1, replica_groups=mesh['zone'=2,'core'=2,'row'=4,'col'=32] {'col'}, dimensions={0} | all-to-all | bytes 655360 | tf_op jit(solution)/shard_map/all_to_all | solution.py:459
  99.3 6.3 %collective-permute-start.9 = (bf16[32,40,128]{2,1,0:T(8,128)(2,1)S(1)}, bf16[32,40,128]{2,1,0:T(8,128)(2,1)S(1)}, u32[]{:S(2)}, u32[]{:S(2)}) collective-permute-start(bf16[32,40,128]{2,1,0:T(8,128)(2,1)S(1)} %all_to_all.17.mine_ref), channel_id=1, source_target_pairs={{0,128},{128,0},{1,129},{129,1},{2,130},{130,2},{3,131},{131,3},{4... | collective-permute-start | bytes 983048 | tf_op jit(solution)/shard_map/ppermute | solution.py:477
  105.6 0.7 copy.17
  106.3 0.7 copy.18
  107.1 0.0 collective-permute-done.9.other_ref
  107.1 2.2 %finish.1 = (f32[256,768]{1,0:T(8,128)}, f32[256,256]{1,0:T(8,128)}, f32[256,256]{1,0:T(8,128)}) custom-call(s32[5]{0:T(128)S(1)} %stack.22.place_ref, bf16[32,40,128]{2,1,0:T(8,128)(2,1)S(1)} %all_to_all.17.mine_ref, bf16[32,40,128]{2,1,0:T(8,128)(2,1)S(1)} %collective-permute-done.9.other_ref), custom_call_target="tpu_custom_call" | custom-call | tf_op jit(solution)/shard_map/finish/pallas_call | solution.py:443
  (13 shorter events, 0.3 us)
Async XLA Ops:
  0.6 13.9 %copy-start = (bf16[256,256]{1,0:T(8,128)(2,1)S(1)}, bf16[256,256]{1,0:T(8,128)(2,1)}, u32[]{:S(2)}) copy-start(bf16[256,256]{1,0:T(8,128)(2,1)} %param.11) | copy-start | bytes 393220
  1.8 13.1 %collective-permute-start.7 = (bf16[9,8,256]{2,1,0:T(8,128)(2,1)S(1)}, bf16[9,8,256]{2,1,0:T(8,128)(2,1)S(1)}, u32[]{:S(2)}, u32[]{:S(2)}) collective-permute-start(bf16[9,8,256]{2,1,0:T(8,128)(2,1)S(1)} %get-tuple-element.49), channel_id=1, source_target_pairs={{33,0},{34,1},{35,2},{36,3},{37,4},{38,5},{39,6},{40,7},{41,8},{42... | collective-permute-start | bytes 110600 | tf_op jit(solution)/shard_map/ppermute | solution.py:40
  3.1 13.1 %collective-permute-start.6 = (bf16[9,8,256]{2,1,0:T(8,128)(2,1)S(1)}, bf16[9,8,256]{2,1,0:T(8,128)(2,1)S(1)}, u32[]{:S(2)}, u32[]{:S(2)}) collective-permute-start(bf16[9,8,256]{2,1,0:T(8,128)(2,1)S(1)} %get-tuple-element.50), channel_id=1, source_target_pairs={{1,32},{2,33},{3,34},{4,35},{5,36},{6,37},{7,38},{8,39},{9,40},{10... | collective-permute-start | bytes 110600 | tf_op jit(solution)/shard_map/ppermute | solution.py:40
  3.8 18.7 %collective-permute-start.4 = (bf16[9,8,256]{2,1,0:T(8,128)(2,1)S(1)}, bf16[9,8,256]{2,1,0:T(8,128)(2,1)S(1)}, u32[]{:S(2)}, u32[]{:S(2)}) collective-permute-start(bf16[9,8,256]{2,1,0:T(8,128)(2,1)S(1)} %get-tuple-element.51), channel_id=1, source_target_pairs={{32,1},{33,2},{34,3},{35,4},{36,5},{37,6},{38,7},{39,8},{40,9},{41... | collective-permute-start | bytes 110600 | tf_op jit(solution)/shard_map/ppermute | solution.py:40
  4.4 23.8 %copy-start.1 = (bf16[256,768]{1,0:T(8,128)(2,1)S(1)}, bf16[256,768]{1,0:T(8,128)(2,1)}, u32[]{:S(2)}) copy-start(bf16[256,768]{1,0:T(8,128)(2,1)} %qkv_ref.3) | copy-start | bytes 1179652
  4.5 25.0 %collective-permute-start.2 = (bf16[9,32,256]{2,1,0:T(8,128)(2,1)S(1)}, bf16[9,32,256]{2,1,0:T(8,128)(2,1)S(1)}, u32[]{:S(2)}, u32[]{:S(2)}) collective-permute-start(bf16[9,32,256]{2,1,0:T(8,128)(2,1)S(1)} %pad_maximum_fusion), channel_id=1, source_target_pairs={{0,1},{1,2},{2,3},{3,4},{4,5},{5,6},{6,7},{7,8},{8,9},{9,10},{10,1... | collective-permute-start | bytes 442376 | tf_op jit(solution)/shard_map/ppermute | solution.py:40
  12.5 17.0 %collective-permute-start.5 = (bf16[9,32,256]{2,1,0:T(8,128)(2,1)S(1)}, bf16[9,32,256]{2,1,0:T(8,128)(2,1)S(1)}, u32[]{:S(2)}, u32[]{:S(2)}) collective-permute-start(bf16[9,32,256]{2,1,0:T(8,128)(2,1)S(1)} %pad_maximum_fusion.1), channel_id=1, source_target_pairs={{1,0},{2,1},{3,2},{4,3},{5,4},{6,5},{7,6},{8,7},{9,8},{10,9},{11,1... | collective-permute-start | bytes 442376 | tf_op jit(solution)/shard_map/ppermute | solution.py:40
  14.7 13.6 %copy-start.2 = (bf16[256,256]{1,0:T(8,128)(2,1)S(1)}, bf16[256,256]{1,0:T(8,128)(2,1)}, u32[]{:S(2)}) copy-start(bf16[256,256]{1,0:T(8,128)(2,1)} %out_ref.3) | copy-start | bytes 393220
  14.8 14.6 %collective-permute-start.1 = (bf16[16,8,256]{2,1,0:T(8,128)(2,1)S(1)}, bf16[16,8,256]{2,1,0:T(8,128)(2,1)S(1)}, u32[]{:S(2)}, u32[]{:S(2)}) collective-permute-start(bf16[16,8,256]{2,1,0:T(8,128)(2,1)S(1)} %get-tuple-element.47), channel_id=1, source_target_pairs={{32,0},{33,1},{34,2},{35,3},{36,4},{37,5},{38,6},{39,7},{40,8},{41... | collective-permute-start | bytes 196616 | tf_op jit(solution)/shard_map/ppermute | solution.py:40
  16.1 13.3 %collective-permute-start = (bf16[16,8,256]{2,1,0:T(8,128)(2,1)S(1)}, bf16[16,8,256]{2,1,0:T(8,128)(2,1)S(1)}, u32[]{:S(2)}, u32[]{:S(2)}) collective-permute-start(bf16[16,8,256]{2,1,0:T(8,128)(2,1)S(1)} %get-tuple-element.48), channel_id=1, source_target_pairs={{0,32},{1,33},{2,34},{3,35},{4,36},{5,37},{6,38},{7,39},{8,40},{9,... | collective-permute-start | bytes 196616 | tf_op jit(solution)/shard_map/ppermute | solution.py:40
  22.4 7.0 %collective-permute-start.3 = (bf16[9,8,256]{2,1,0:T(8,128)(2,1)S(1)}, bf16[9,8,256]{2,1,0:T(8,128)(2,1)S(1)}, u32[]{:S(2)}, u32[]{:S(2)}) collective-permute-start(bf16[9,8,256]{2,1,0:T(8,128)(2,1)S(1)} %get-tuple-element.52), channel_id=1, source_target_pairs={{0,33},{1,34},{2,35},{3,36},{4,37},{5,38},{6,39},{7,40},{8,41},{9,... | collective-permute-start | bytes 110600 | tf_op jit(solution)/shard_map/ppermute | solution.py:40
  36.3 10.4 %collective-permute-start.8 = (bf16[32,40,128]{2,1,0:T(8,128)(2,1)S(1)}, bf16[32,40,128]{2,1,0:T(8,128)(2,1)S(1)}, u32[]{:S(2)}, u32[]{:S(2)}) collective-permute-start(bf16[32,40,128]{2,1,0:T(8,128)(2,1)S(1)} %get-tuple-element.33), channel_id=1, source_target_pairs={{0,128},{128,0},{1,129},{129,1},{2,130},{130,2},{3,131},{131,3},{4... | collective-permute-start | bytes 983048 | tf_op jit(solution)/shard_map/ppermute | solution.py:473
  99.3 7.8 %collective-permute-start.9 = (bf16[32,40,128]{2,1,0:T(8,128)(2,1)S(1)}, bf16[32,40,128]{2,1,0:T(8,128)(2,1)S(1)}, u32[]{:S(2)}, u32[]{:S(2)}) collective-permute-start(bf16[32,40,128]{2,1,0:T(8,128)(2,1)S(1)} %all_to_all.17.mine_ref), channel_id=1, source_target_pairs={{0,128},{128,0},{1,129},{129,1},{2,130},{130,2},{3,131},{131,3},{4... | collective-permute-start | bytes 983048 | tf_op jit(solution)/shard_map/ppermute | solution.py:477

commit v5 on v4

--- a/solution.py
+++ b/solution.py
@@ -28,16 +28,11 @@
     return jnp.concatenate([jnp.cos(phase_angle), jnp.sin(phase_angle)])
 
 
-def shifted(block, row_step, col_step):
-    down = lax.axis_size("row")
-    across = lax.axis_size("col")
-    pairs = [
-        (row * across + col, (row + row_step) * across + col + col_step)
-        for row in range(down)
-        for col in range(across)
-        if 0 <= row + row_step < down and 0 <= col + col_step < across
-    ]
-    return lax.ppermute(block, ("row", "col"), pairs)
+def exchange(to_next, to_previous, axis):
+    count = lax.axis_size(axis)
+    forward = [(i, i + 1) for i in range(count - 1)]
+    backward = [(target, source) for source, target in forward]
+    return lax.ppermute(to_next, axis, forward), lax.ppermute(to_previous, axis, backward)
 
 
 def nn(left, right):
@@ -79,6 +74,46 @@
     key_inv = lax.rsqrt(head_mean(key_raw * key_raw, average) + epsilon)
     query = query_raw * query_inv * (score_scale / HEAD_DIM)
     return inverse, normed, query, key_raw * key_inv, project[:, 2 * width :], (query_raw, query_inv, key_raw, key_inv)
+
+
+def head_picks(width):
+    lane_head = lax.broadcasted_iota(jnp.int32, (1, width), 1) // HEAD_DIM
+    return [jnp.where(lane_head == head, 1.0, 0.0) for head in range(width // HEAD_DIM)]
+
+
+def attend(keys, values, queries, grads, mask, rows, height, wanted, first, count):
+    width = keys.shape[-1]
+    picks = head_picks(width)
+    narrow = [pick.astype(jnp.bfloat16) for pick in picks]
+
+    def spread(part):
+        return jnp.concatenate([part * pick for pick in narrow], axis=0)
+
+    def gathered(part):
+        total = part[: SPAN * rows] * picks[0]
+        for head in range(1, len(picks)):
+            total = total + part[head * SPAN * rows : (head + 1) * SPAN * rows] * picks[head]
+        return total.reshape(SPAN, rows, width)[:, :height]
+
+    def kept(part):
+        shape = (WINDOW, rows, part.shape[1])
+        return part.reshape(shape)[first : first + count, :height].reshape(-1, part.shape[1])
+
+    queries = spread(queries)
+    grads = spread(grads)
+    exponent = jnp.exp(nt(keys, queries) - score_scale) * mask
+    denominator = jnp.maximum(jnp.sum(exponent, axis=0, keepdims=True), 1e-30)
+    weights = (exponent * (1.0 / denominator)).astype(jnp.bfloat16)
+    wide = weights.astype(jnp.float32)
+    slope = nt(values, grads)
+    middle = jnp.sum(wide * slope, axis=0, keepdims=True)
+    grad_score = (wide * (slope - middle)).astype(jnp.bfloat16)
+    attended = grad_query = None
+    if wanted:
+        attended = gathered(tn(weights, values)).astype(jnp.bfloat16)
+        grad_query = gathered(tn(grad_score, keys))
+    shape = (count, height, width)
+    return attended, grad_query, nn(kept(grad_score), queries).reshape(shape), nn(kept(weights), grads).reshape(shape)
 
 
 def own_kernel(
@@ -98,19 +133,25 @@
     query_inv_ref,
     key_raw_ref,
     key_inv_ref,
+    attended_ref,
+    grad_query_ref,
+    grad_key_ref,
+    grad_value_ref,
 ):
-    cols, height, width = tok_ref.shape
-    _, rows, lanes = mask_ref.shape
+    cols, rows, width = tok_ref.shape
+    lanes = mask_ref.shape[2]
+    height = rows - 2 * EDGE
     row_first = place_ref[0]
-    pixels = tok_ref[...].astype(jnp.float32).reshape(cols * height, width)
+    pixels = tok_ref[...].astype(jnp.float32).reshape(cols * rows, width)
     _, _, query, key, value, raw = projected(pixels, adaptive_ref[...], qkv_ref, average_matrix(width))
-    query_ref[...] = query.astype(jnp.bfloat16).reshape(cols, height, width)
-    key_ref[...] = key.astype(jnp.bfloat16).reshape(cols, height, width)
-    value_ref[...] = value.astype(jnp.bfloat16).reshape(cols, height, width)
+    query = query.astype(jnp.bfloat16)
+    key = key.astype(jnp.bfloat16)
+    value = value.astype(jnp.bfloat16)
+    grad = nt(cot_ref[...].reshape(cols * rows, width), out_ref[...]).astype(jnp.bfloat16)
+    for ref, values in ((query_ref, query), (key_ref, key), (value_ref, value), (grad_ref, grad)):
+        ref[...] = values.reshape(cols, rows, width)
     for ref, values in zip((query_raw_ref, query_inv_ref, key_raw_ref, key_inv_ref), raw):
-        ref[...] = values
-    cot_own = cot_ref[...].reshape(cols * height, width)
-    grad_ref[...] = nt(cot_own, out_ref[...]).astype(jnp.bfloat16).reshape(cols, height, width)
+        ref[...] = values.reshape(cols, rows, width)[:, :height]
 
     def row_at(position):
         halo = jnp.where(position < height + EDGE, position - height - EDGE, position - EDGE)
@@ -126,7 +167,13 @@
     image_row = jnp.broadcast_to(row_first + key_row, row_gap.shape)
     near_row = (row_gap >= -RADIUS) & (row_gap <= RADIUS) & (image_row >= 0) & (image_row < total_rows)
     near_col = (col_gap >= 0) & (col_gap <= REACH)
-    mask_ref[...] = jnp.where(near_row, 1.0, 0.0) * jnp.where(near_col, 1.0, 0.0)
+    mask = jnp.where(near_row, 1.0, 0.0) * jnp.where(near_col, 1.0, 0.0)
+    mask_ref[...] = mask
+
+    pair = slice(RADIUS * rows, (RADIUS + SPAN) * rows)
+    attended_ref[...], grad_query_ref[...], grad_key_ref[...], grad_value_ref[...] = attend(
+        key, value, query[pair], grad[pair], mask.reshape(cols * rows, lanes), rows, height, True, 0, cols
+    )
 
 
 def block_kernel(
@@ -134,14 +181,8 @@
     place_ref,
     tok_ref,
     cot_ref,
-    above_ref,
-    below_ref,
     left_ref,
-    left_above_ref,
-    left_below_ref,
     right_ref,
-    right_above_ref,
-    right_below_ref,
     adaptive_ref,
     qkv_ref,
     out_ref,
@@ -154,6 +195,10 @@
     query_inv_ref,
     key_raw_ref,
     key_inv_ref,
+    own_attended_ref,
+    own_grad_query_ref,
+    own_grad_key_ref,
+    own_grad_value_ref,
     result_ref,
     grad_tokens_ref,
     mine_ref,
@@ -168,10 +213,10 @@
     grad_value_ref,
     whole_ref,
 ):
-    cols, height, width = tok_ref.shape
-    rows = mask_ref.shape[1]
-    heads = width // HEAD_DIM
+    cols, rows, width = tok_ref.shape
+    height = rows - 2 * EDGE
     query_cols = cols + REACH
+    last = REACH + cols
     col_first = place_ref[1]
     image = place_ref[2]
     core = place_ref[3]
@@ -180,69 +225,29 @@
     factor = score_scale / HEAD_DIM
     average = average_matrix(width)
 
-    last = REACH + cols
-    pieces = (
-        (left_ref, REACH, 0, 0),
-        (right_ref, REACH, last, 0),
-        (above_ref, cols, REACH, height),
-        (below_ref, cols, REACH, height + EDGE),
-        (left_above_ref, REACH, 0, height),
-        (left_below_ref, REACH, 0, height + EDGE),
-        (right_above_ref, REACH, last, height),
-        (right_below_ref, REACH, last, height + EDGE),
-    )
-
-    def place_rows(values, targets):
-        first = 0
-        for ref, count, tall, col, row in targets:
-            part = values[first : first + count * tall].reshape(count, tall, width)
-            ref[pl.ds(col, count), pl.ds(row, tall)] = part.astype(jnp.bfloat16)
-            first += count * tall
-
-    for group in (pieces[:2], pieces[2:]):
-        pixels = jnp.concatenate(
-            [ref[:count].astype(jnp.float32).reshape(count * ref.shape[1], width) for ref, count, _, _ in group], axis=0
-        )
+    for ref, col in ((left_ref, 0), (right_ref, last)):
+        pixels = ref[:REACH].astype(jnp.float32).reshape(REACH * rows, width)
         _, _, query, key, value, _ = projected(pixels, adaptive, qkv_ref, average)
-        for values, target in ((query, query_ref), (key, key_ref), (value, value_ref)):
-            place_rows(values, [(target, count, ref.shape[1], col, row) for ref, count, col, row in group])
-    sides = []
-    targets = []
-    for ref, count, col, row in pieces:
-        tall = ref.shape[1]
-        sides.append(ref[count:].astype(jnp.float32).reshape(-1, width))
-        targets.append((grad_ref, ref.shape[0] - count, tall, 0 if col == 0 else col - RADIUS, row))
-    side = jnp.concatenate(sides, axis=0).astype(jnp.bfloat16)
-    place_rows(nt(side, out_ref[...]), targets)
-    for target, source, col in (
-        (query_ref, own_query_ref, REACH),
-        (key_ref, own_key_ref, REACH),
-        (value_ref, own_value_ref, REACH),
-        (grad_ref, own_grad_ref, RADIUS),
-    ):
-        target[pl.ds(col, cols), pl.ds(0, height)] = source[...]
-
-    grad_key_ref[...] = jnp.zeros_like(grad_key_ref)
-    grad_value_ref[...] = jnp.zeros_like(grad_value_ref)
-    lane_head = lax.broadcasted_iota(jnp.int32, (1, width), 1) // HEAD_DIM
-    picks = [jnp.where(lane_head == head, 1.0, 0.0) for head in range(heads)]
-    narrow = [pick.astype(jnp.bfloat16) for pick in picks]
-
-    def spread(values):
-        return jnp.concatenate([values * pick for pick in narrow], axis=0)
-
-    def gathered(values):
-        total = values[: SPAN * rows] * picks[0]
-        for head in range(1, heads):
-            total = total + values[head * SPAN * rows : (head + 1) * SPAN * rows] * picks[head]
-        return total.reshape(SPAN, rows, width)[:, :height]
+        here = pl.ds(col, REACH)
+        query_ref[here] = query.astype(jnp.bfloat16).reshape(REACH, rows, width)
+        key_ref[here] = key.astype(jnp.bfloat16).reshape(REACH, rows, width)
+        value_ref[here] = value.astype(jnp.bfloat16).reshape(REACH, rows, width)
+        side = ref[REACH:].reshape(RADIUS * rows, width)
+        grad = nt(side, out_ref[...]).astype(jnp.bfloat16).reshape(RADIUS, rows, width)
+        grad_ref[pl.ds(0 if col == 0 else col - RADIUS, RADIUS)] = grad
+    query_ref[pl.ds(REACH, cols)] = own_query_ref[...]
+    key_ref[pl.ds(REACH, cols)] = own_key_ref[...]
+    value_ref[pl.ds(REACH, cols)] = own_value_ref[...]
+    grad_ref[pl.ds(RADIUS, cols)] = own_grad_ref[...]
+    attended_ref[pl.ds(RADIUS, SPAN)] = own_attended_ref[...]
+    grad_query_ref[pl.ds(RADIUS, SPAN)] = own_grad_query_ref[...]
+    grad_key_ref[...] = own_grad_key_ref[...]
+    grad_value_ref[...] = own_grad_value_ref[...]
 
     for start in range(0, query_cols, SPAN):
+        if start == REACH:
+            continue
         near = pl.ds(start, WINDOW)
-        keys = key_ref[near].reshape(WINDOW * rows, width)
-        values = value_ref[near].reshape(WINDOW * rows, width)
-        queries = spread(query_ref[pl.ds(start + RADIUS, SPAN)].reshape(SPAN * rows, width))
-        grads = spread(grad_ref[pl.ds(start, SPAN)].reshape(SPAN * rows, width))
         masks = []
         for column in range(WINDOW):
             mask = mask_ref[column]
@@ -250,34 +255,35 @@
                 image_col = col_first + (start + column - REACH)
                 mask = mask * jnp.where((image_col >= 0) & (image_col < total_cols), 1.0, 0.0)
             masks.append(mask)
-        exponent = jnp.exp(nt(keys, queries) - score_scale) * jnp.concatenate(masks, axis=0)
-        denominator = jnp.maximum(jnp.sum(exponent, axis=0, keepdims=True), 1e-30)
-        weights = (exponent * (1.0 / denominator)).astype(jnp.bfloat16)
-        wide = weights.astype(jnp.float32)
-        slope = nt(values, grads)
-        middle = jnp.sum(wide * slope, axis=0, keepdims=True)
-        grad_score = (wide * (slope - middle)).astype(jnp.bfloat16)
-        low = max(start + RADIUS, REACH)
-        high = min(start + RADIUS + SPAN, last)
-        if low < high:
-            skip = slice(low - start - RADIUS, high - start - RADIUS)
-            there = pl.ds(low - REACH, high - low)
-            attended_ref[there] = gathered(tn(weights, values))[skip].astype(jnp.bfloat16)
-            grad_query_ref[there] = gathered(tn(grad_score, keys))[skip]
         low = max(start, REACH)
         high = min(start + WINDOW, last)
+        query_low = max(start + RADIUS, REACH)
+        query_high = min(start + RADIUS + SPAN, last)
+        attended, grad_query, grad_key, grad_value = attend(
+            key_ref[near].reshape(WINDOW * rows, width),
+            value_ref[near].reshape(WINDOW * rows, width),
+            query_ref[pl.ds(start + RADIUS, SPAN)].reshape(SPAN * rows, width),
+            grad_ref[pl.ds(start, SPAN)].reshape(SPAN * rows, width),
+            jnp.concatenate(masks, axis=0),
+            rows,
+            height,
+            query_low < query_high,
+            low - start,
+            high - low,
+        )
+        if query_low < query_high:
+            own = slice(query_low - start - RADIUS, query_high - start - RADIUS)
+            there = pl.ds(query_low - REACH, query_high - query_low)
+            attended_ref[there] = attended[own]
+            grad_query_ref[there] = grad_query[own]
         there = pl.ds(low - REACH, high - low)
-        shape = (WINDOW, rows, heads * SPAN * rows)
-        kept = (high - low, height, width)
-        kept_score = grad_score.reshape(shape)[low - start : high - start, :height].reshape(-1, shape[2])
-        kept_weights = weights.reshape(shape)[low - start : high - start, :height].reshape(-1, shape[2])
-        grad_key_ref[there] += nn(kept_score, queries).reshape(kept)
-        grad_value_ref[there] += nn(kept_weights, grads).reshape(kept)
+        grad_key_ref[there] += grad_key
+        grad_value_ref[there] += grad_value
 
     tokens = cols * height
-    pixels = tok_ref[...].astype(jnp.float32).reshape(tokens, width)
+    pixels = tok_ref[:, :height].astype(jnp.float32).reshape(tokens, width)
     inverse, normed = normalized(pixels, adaptive)
-    cot_own = cot_ref[...].reshape(tokens, width)
+    cot_own = cot_ref[:, :height].reshape(tokens, width)
     attended = attended_ref[...].reshape(tokens, width)
     result = pixels + nn(attended, out_ref[...])
     result_ref[...] = result.astype(jnp.bfloat16).reshape(cols, height, width)
@@ -290,8 +296,8 @@
     grad_key = grad_key_ref[...].reshape(tokens, width)
     grad_project = jnp.concatenate(
         [
-            back(query_raw_ref[...], query_inv_ref[...], grad_query, factor).astype(jnp.bfloat16),
-            back(key_raw_ref[...], key_inv_ref[...], grad_key, 1.0).astype(jnp.bfloat16),
+            back(query_raw_ref[...].reshape(tokens, width), query_inv_ref[...].reshape(tokens, width), grad_query, factor).astype(jnp.bfloat16),
+            back(key_raw_ref[...].reshape(tokens, width), key_inv_ref[...].reshape(tokens, width), grad_key, 1.0).astype(jnp.bfloat16),
             grad_value_ref[...].reshape(tokens, width).astype(jnp.bfloat16),
         ],
         axis=1,
@@ -373,21 +379,14 @@
     col_first = lax.axis_index("col") * cols
     total_rows = height * lax.axis_size("row")
     total_cols = cols * lax.axis_size("col")
-    tok = tokens[0].transpose(1, 0, 2)
-    cot = cotangent[0].transpose(1, 0, 2)
     rows = height + 2 * EDGE
-    to_right = jnp.concatenate([tok[cols - REACH :], cot[cols - RADIUS :]], axis=0)
-    to_left = jnp.concatenate([tok[:REACH], cot[:RADIUS]], axis=0)
-    both = jnp.concatenate([tok, cot], axis=0)
-    left = shifted(to_right, 0, 1)
-    right = shifted(to_left, 0, -1)
-    above = shifted(both[:, height - EDGE :], 1, 0)
-    below = shifted(both[:, :EDGE], -1, 0)
-    left_above = shifted(to_right[:, height - EDGE :], 1, 1)
-    left_below = shifted(to_right[:, :EDGE], -1, 1)
-    right_above = shifted(to_left[:, height - EDGE :], 1, -1)
-    right_below = shifted(to_left[:, :EDGE], -1, -1)
-    halos = (above, below, left, left_above, left_below, right, right_above, right_below)
+    both = jnp.concatenate([tokens[0].transpose(1, 0, 2), cotangent[0].transpose(1, 0, 2)], axis=0)
+    above, below = exchange(both[:, height - EDGE :], both[:, :EDGE], "row")
+    both = jnp.concatenate([both, above, below], axis=1)
+    tok, cot = both[:cols], both[cols:]
+    to_next = jnp.concatenate([tok[cols - REACH :], cot[cols - RADIUS :]], axis=0)
+    to_previous = jnp.concatenate([tok[:REACH], cot[:RADIUS]], axis=0)
+    left, right = exchange(to_next, to_previous, "col")
     features = fourier(timesteps[0])
     adaptive = 1.0 + jnp.dot(
         features[None], time_weight.astype(jnp.float32), precision=lax.Precision.HIGHEST
@@ -402,13 +401,19 @@
     smem = pl.BlockSpec(memory_space=pltpu.SMEM)
     vmem = pl.BlockSpec(memory_space=pltpu.VMEM)
     limits = pltpu.CompilerParams(vmem_limit_bytes=40 * 2**20)
+    tall = jax.ShapeDtypeStruct((cols, rows, width), jnp.bfloat16)
     block = jax.ShapeDtypeStruct((cols, height, width), jnp.bfloat16)
-    flat = jax.ShapeDtypeStruct((cols * height, width), jnp.float32)
+    exact = jax.ShapeDtypeStruct((cols, height, width), jnp.float32)
+    mask = jax.ShapeDtypeStruct((WINDOW, rows, lanes), jnp.float32)
+    pair = (
+        jax.ShapeDtypeStruct((SPAN, height, width), jnp.bfloat16),
+        jax.ShapeDtypeStruct((SPAN, height, width), jnp.float32),
+    )
     prepared = pl.pallas_call(
         functools.partial(own_kernel, total_rows),
-        out_shape=(block,) * 4 + (jax.ShapeDtypeStruct((WINDOW, rows, lanes), jnp.float32),) + (flat,) * 4,
+        out_shape=(tall,) * 4 + (mask,) + (exact,) * 4 + pair + (exact,) * 2,
         in_specs=[smem] + [vmem] * 5,
-        out_specs=(vmem,) * 9,
+        out_specs=(vmem,) * 13,
         compiler_params=limits,
         cost_estimate=pl.CostEstimate(flops=1_000_000_000, bytes_accessed=4_000_000, transcendentals=200_000),
         name="own",
@@ -419,7 +424,7 @@
     result, grad_tokens, mine, other = pl.pallas_call(
         functools.partial(block_kernel, total_cols),
         out_shape=(block, block, chunks, chunks),
-        in_specs=[smem] + [vmem] * 22,
+        in_specs=[smem] + [vmem] * 20,
         out_specs=(vmem,) * 4,
         scratch_shapes=[
             wide,
@@ -435,7 +440,7 @@
         compiler_params=limits,
         cost_estimate=pl.CostEstimate(flops=8_000_000_000, bytes_accessed=4_000_000, transcendentals=1_000_000),
         name="block",
-    )(place, tok, cot, *halos, adaptive, qkv_weight, output_weight, *prepared)
+    )(place, tok, cot, left, right, adaptive, qkv_weight, output_weight, *prepared)
     result = result.transpose(1, 0, 2)
     grad_tokens = grad_tokens.transpose(1, 0, 2)
 

time: 110 us -> 98.9 us (0.90)
  starting transfers between devices: 40.7 us -> 22.2 us
  waiting for transfers between devices: 1.26 us -> 7.82 us
  blocking collectives: 52.3 us -> 53.4 us
    ppermute x8 -> x4, starting transfers between devices: 25.3 us -> 10.7 us  [the longest x2 8.03 us: exchange(): lax.ppermute(to_next, axis, forward)]
    ppermute x8 -> x4, waiting for transfers between devices: 0.02 us -> 6.59 us  [the longest x2 6.58 us: exchange(): lax.ppermute(to_previous, axis, backward)]
    ppermute x1, starting transfers between devices: 9.16 us -> 5.16 us  [summed(): mine = total(jnp.stack([mine, lax.ppermute(other, 'core', partner)]))]
    all_to_all x3, blocking collectives: 52.3 us -> 53.4 us  [swap(): return lax.all_to_all(pieces, axes, 0, 0, tiled=True)]
  transfers between devices with their start and end apart: 10 -> 6, of which waited for: 1 -> 3; matrix products, arithmetic and copies ran while one was open for 2% -> 2% of each run, Pallas kernels for 1% -> 2%
where the time goes in v5:
time: 98.9 us; the launch traced here: 98.6 us
  blocking collectives  53.4 us (54%)
  starting transfers between devices  22.2 us (22%)
  Pallas kernels  10.3 us (10%)
  waiting for transfers between devices  7.82 us (8%)
  local copies, waits for them, and re-layouts  2.78 us (3%)
  between operations  1.49 us (2%)
    all_to_all x3, blocking collectives, swap(): return lax.all_to_all(pieces, axes, 0, 0, tiled=True)  53.4 us
    ppermute x2, starting transfers between devices, exchange(): lax.ppermute(to_next, axis, forward)  8.03 us
    ppermute x2, waiting for transfers between devices, exchange(): lax.ppermute(to_previous, axis, backward)  6.58 us
    ppermute x1, starting transfers between devices, summed(): return (mine, lax.ppermute(mine, 'core', partner))  6.32 us
    pallas_call x1, Pallas kernels, on_device(): pl.pallas_call(functools.partial(block_kernel, total_cols), out_shape=(bl...  6.08 us
    ppermute x1, starting transfers between devices, summed(): mine = total(jnp.stack([mine, lax.ppermute(other, 'core', partner)]))  5.16 us
    ppermute x2, starting transfers between devices, exchange(): lax.ppermute(to_previous, axis, backward)  2.72 us
    pallas_call x1, Pallas kernels, on_device(): pl.pallas_call(functools.partial(finish_kernel, (lax.axis_size('zone') *...  2.18 us
  transfers between devices with their start and end apart: 6, of which 3 were waited for; matrix products, arithmetic and copies ran while one was open for 2% of the time, Pallas kernels for 2%

profile of v5, /device:TPU:1, one launch (start us, length us, event | category | flops | bytes accessed | tf_op | source)
XLA Modules:
  0.0 98.6 jit_solution(14812728418896334802)
XLA Ops:
  0.6 0.0 copy-start
  0.6 1.1 %copy_bitcast_fusion = (bf16[8,32,256]{2,1,0:T(8,128)(2,1)S(1)}, bf16[8,32,256]{2,1,0:T(8,128)(2,1)S(1)}) fusion(bf16[1,32,8,256]{3,2,1,0:T(8,128)(2,1)} %param.8, bf16[1,32,8,256]{3,2,1,0:T(8,128)(2,1)} %param.6), kind=kLoop, calls=%fused_computation.3 | loop fusion | bytes 524288 | tf_op jit(solution)/shard_map/transpose | solution.py:383
  1.7 4.8 %collective-permute-start = (bf16[16,8,256]{2,1,0:T(8,128)(2,1)S(1)}, bf16[16,8,256]{2,1,0:T(8,128)(2,1)S(1)}, u32[]{:S(2)}, u32[]{:S(2)}) collective-permute-start(bf16[16,8,256]{2,1,0:T(8,128)(2,1)S(1)} %get-tuple-element.61), channel_id=1, source_target_pairs={{0,32},{32,64},{64,96},{1,33},{33,65},{65,97},{2,34},{34,66},{66,9... | collective-permute-start | bytes 196616 | tf_op jit(solution)/shard_map/ppermute | solution.py:35
  6.5 1.3 %collective-permute-start.1 = (bf16[16,8,256]{2,1,0:T(8,128)(2,1)S(1)}, bf16[16,8,256]{2,1,0:T(8,128)(2,1)S(1)}, u32[]{:S(2)}, u32[]{:S(2)}) collective-permute-start(bf16[16,8,256]{2,1,0:T(8,128)(2,1)S(1)} %get-tuple-element.62), channel_id=1, source_target_pairs={{32,0},{64,32},{96,64},{33,1},{65,33},{97,65},{34,2},{66,34},{98,6... | collective-permute-start | bytes 196616 | tf_op jit(solution)/shard_map/ppermute | solution.py:35
  8.6 0.0 copy-done
  8.6 0.1 fusion.5
  8.7 0.1 stack.22.place_ref
  8.8 0.0 collective-permute-done
  8.8 3.4 %collective-permute-done.1 = bf16[16,8,256]{2,1,0:T(8,128)(2,1)S(1)} collective-permute-done((bf16[16,8,256]{2,1,0:T(8,128)(2,1)S(1)}, bf16[16,8,256]{2,1,0:T(8,128)(2,1)S(1)}, u32[]{:S(2)}, u32[]{:S(2)}) %collective-permute-start.1) | collective-permute-done | bytes 65568 | tf_op jit(solution)/shard_map/ppermute | solution.py:35
  12.3 3.2 %collective-permute-start.2 = (bf16[9,48,256]{2,1,0:T(8,128)(2,1)S(1)}, bf16[9,48,256]{2,1,0:T(8,128)(2,1)S(1)}, u32[]{:S(2)}, u32[]{:S(2)}) collective-permute-start(bf16[9,48,256]{2,1,0:T(8,128)(2,1)S(1)} %pad_maximum_fusion.1), channel_id=1, source_target_pairs={{0,1},{1,2},{2,3},{3,4},{4,5},{5,6},{6,7},{7,8},{8,9},{9,10},{10,1... | collective-permute-start | bytes 663560 | tf_op jit(solution)/shard_map/ppermute | solution.py:35
  15.6 0.0 copy-start.1
  15.6 0.0 copy-start.2
  15.6 1.4 %collective-permute-start.3 = (bf16[9,48,256]{2,1,0:T(8,128)(2,1)S(1)}, bf16[9,48,256]{2,1,0:T(8,128)(2,1)S(1)}, u32[]{:S(2)}, u32[]{:S(2)}) collective-permute-start(bf16[9,48,256]{2,1,0:T(8,128)(2,1)S(1)} %pad_maximum_fusion.2), channel_id=1, source_target_pairs={{1,0},{2,1},{3,2},{4,3},{5,4},{6,5},{7,6},{8,7},{9,8},{10,9},{11,1... | collective-permute-start | bytes 663560 | tf_op jit(solution)/shard_map/ppermute | solution.py:35
  17.1 0.0 copy-done.1
  17.1 0.0 copy-done.2
  17.1 2.1 %own.1 = (bf16[8,48,256]{2,1,0:T(8,128)(2,1)S(1)}, bf16[8,48,256]{2,1,0:T(8,128)(2,1)S(1)}, bf16[8,48,256]{2,1,0:T(8,128)(2,1)S(1)}, bf16[8,48,256]{2,1,0:T(8,12...) custom-call(s32[5]{0:T(128)S(1)} %stack.22.place_ref, ...), custom_call_target="tpu_custom_call" | custom-call | flops 1000000000 | bytes 4000000 | tf_op jit(solution)/shard_map/own/pallas_call | solution.py:412
  19.2 0.0 collective-permute-done.2.left_ref
  19.2 3.2 %collective-permute-done.3.right_ref = bf16[9,48,256]{2,1,0:T(8,128)(2,1)S(1)} collective-permute-done((bf16[9,48,256]{2,1,0:T(8,128)(2,1)S(1)}, bf16[9,48,256]{2,1,0:T(8,128)(2,1)S(1)}, u32[]{:S(2)}, u32[]{:S(2)}) %collective-permute-start.3) | collective-permute-done | bytes 221216 | tf_op jit(solution)/shard_map/ppermute | solution.py:35
  22.4 6.1 %block.1 = (bf16[8,32,256]{2,1,0:T(8,128)(2,1)S(1)}, bf16[8,32,256]{2,1,0:T(8,128)(2,1)S(1)}, bf16[32,40,128]{2,1,0:T(8,128)(2,1)S(1)}, bf16[32,40,128]{2,1,0:T(8,128)(2,1)S(1)}) custom-call(s32[5]{0:T(128)S(1)} %stack.22.place_ref, bf16[8,48,256]{2,1,0:T(8,128)(2,1)S(1)} %get-tuple-element.60.tok_ref, bf16[8,48,256]{2,1,0:T(8,128)(2,1)S(1)} %get-tuple-element.59.cot_ref, ...), custom_call_target="tpu_custom_call" | custom-call | flops 8000000000 | bytes 4000000 | tf_op jit(solution)/shard_map/block/pallas_call | solution.py:424
  28.5 5.2 %collective-permute-start.4 = (bf16[32,40,128]{2,1,0:T(8,128)(2,1)S(1)}, bf16[32,40,128]{2,1,0:T(8,128)(2,1)S(1)}, u32[]{:S(2)}, u32[]{:S(2)}) collective-permute-start(bf16[32,40,128]{2,1,0:T(8,128)(2,1)S(1)} %get-tuple-element.41), channel_id=1, source_target_pairs={{0,128},{128,0},{1,129},{129,1},{2,130},{130,2},{3,131},{131,3},{4... | collective-permute-start | bytes 983048 | tf_op jit(solution)/shard_map/ppermute | solution.py:478
  33.6 1.2 %collective-permute-done.4 = bf16[32,40,128]{2,1,0:T(8,128)(2,1)S(1)} collective-permute-done((bf16[32,40,128]{2,1,0:T(8,128)(2,1)S(1)}, bf16[32,40,128]{2,1,0:T(8,128)(2,1)S(1)}, u32[]{:S(2)}, u32[]{:S(2)}) %collective-permute-start.4) | collective-permute-done | bytes 327712 | tf_op jit(solution)/shard_map/ppermute | solution.py:478
  34.9 0.1 reduce_sum.34
  35.0 20.1 %all_to_all.15 = bf16[32,40,128]{2,1,0:T(8,128)(2,1)S(1)} all-to-all(bf16[32,40,128]{2,1,0:T(8,128)(2,1)S(1)} %reduce_sum.34), channel_id=1, replica_groups=mesh['zone'=2,'core'=2,'row'=4,'col'=32] {'col'}, dimensions={0} | all-to-all | bytes 655360 | tf_op jit(solution)/shard_map/all_to_all | solution.py:464
  55.1 0.1 reduce_sum.35
  55.2 16.0 %all_to_all.16 = bf16[8,40,128]{2,1,0:T(8,128)(2,1)S(1)} all-to-all(bf16[8,40,128]{2,1,0:T(8,128)(2,1)S(1)} %broadcast_in_dim.10), channel_id=1, replica_groups=mesh['zone'=2,'core'=2,'row'=4,'col'=32] {'zone','row'}, dimensions={0} | all-to-all | bytes 163840 | tf_op jit(solution)/shard_map/all_to_all | solution.py:464
  71.2 17.3 %all_to_all.17.mine_ref = bf16[32,40,128]{2,1,0:T(8,128)(2,1)S(1)} all-to-all(bf16[32,40,128]{2,1,0:T(8,128)(2,1)S(1)} %broadcast_in_dim.22), channel_id=1, replica_groups=mesh['zone'=2,'core'=2,'row'=4,'col'=32] {'col'}, dimensions={0} | all-to-all | bytes 655360 | tf_op jit(solution)/shard_map/all_to_all | solution.py:464
  88.6 6.3 %collective-permute-start.5 = (bf16[32,40,128]{2,1,0:T(8,128)(2,1)S(1)}, bf16[32,40,128]{2,1,0:T(8,128)(2,1)S(1)}, u32[]{:S(2)}, u32[]{:S(2)}) collective-permute-start(bf16[32,40,128]{2,1,0:T(8,128)(2,1)S(1)} %all_to_all.17.mine_ref), channel_id=1, source_target_pairs={{0,128},{128,0},{1,129},{129,1},{2,130},{130,2},{3,131},{131,3},{4... | collective-permute-start | bytes 983048 | tf_op jit(solution)/shard_map/ppermute | solution.py:482
  94.9 0.7 copy.17
  95.6 0.7 copy.18
  96.4 0.0 collective-permute-done.5.other_ref
  96.4 2.2 %finish.1 = (f32[256,768]{1,0:T(8,128)}, f32[256,256]{1,0:T(8,128)}, f32[256,256]{1,0:T(8,128)}) custom-call(s32[5]{0:T(128)S(1)} %stack.22.place_ref, bf16[32,40,128]{2,1,0:T(8,128)(2,1)S(1)} %all_to_all.17.mine_ref, bf16[32,40,128]{2,1,0:T(8,128)(2,1)S(1)} %collective-permute-done.5.other_ref), custom_call_target="tpu_custom_call" | custom-call | tf_op jit(solution)/shard_map/finish/pallas_call | solution.py:448
  (13 shorter events, 0.3 us)
Async XLA Ops:
  0.6 7.9 %copy-start = (bf16[256,256]{1,0:T(8,128)(2,1)S(1)}, bf16[256,256]{1,0:T(8,128)(2,1)}, u32[]{:S(2)}) copy-start(bf16[256,256]{1,0:T(8,128)(2,1)} %param.11) | copy-start | bytes 393220
  1.7 7.1 %collective-permute-start = (bf16[16,8,256]{2,1,0:T(8,128)(2,1)S(1)}, bf16[16,8,256]{2,1,0:T(8,128)(2,1)S(1)}, u32[]{:S(2)}, u32[]{:S(2)}) collective-permute-start(bf16[16,8,256]{2,1,0:T(8,128)(2,1)S(1)} %get-tuple-element.61), channel_id=1, source_target_pairs={{0,32},{32,64},{64,96},{1,33},{33,65},{65,97},{2,34},{34,66},{66,9... | collective-permute-start | bytes 196616 | tf_op jit(solution)/shard_map/ppermute | solution.py:35
  6.5 5.6 %collective-permute-start.1 = (bf16[16,8,256]{2,1,0:T(8,128)(2,1)S(1)}, bf16[16,8,256]{2,1,0:T(8,128)(2,1)S(1)}, u32[]{:S(2)}, u32[]{:S(2)}) collective-permute-start(bf16[16,8,256]{2,1,0:T(8,128)(2,1)S(1)} %get-tuple-element.62), channel_id=1, source_target_pairs={{32,0},{64,32},{96,64},{33,1},{65,33},{97,65},{34,2},{66,34},{98,6... | collective-permute-start | bytes 196616 | tf_op jit(solution)/shard_map/ppermute | solution.py:35
  12.3 6.9 %collective-permute-start.2 = (bf16[9,48,256]{2,1,0:T(8,128)(2,1)S(1)}, bf16[9,48,256]{2,1,0:T(8,128)(2,1)S(1)}, u32[]{:S(2)}, u32[]{:S(2)}) collective-permute-start(bf16[9,48,256]{2,1,0:T(8,128)(2,1)S(1)} %pad_maximum_fusion.1), channel_id=1, source_target_pairs={{0,1},{1,2},{2,3},{3,4},{4,5},{5,6},{6,7},{7,8},{8,9},{9,10},{10,1... | collective-permute-start | bytes 663560 | tf_op jit(solution)/shard_map/ppermute | solution.py:35
  15.6 1.5 %copy-start.1 = (bf16[256,768]{1,0:T(8,128)(2,1)S(1)}, bf16[256,768]{1,0:T(8,128)(2,1)}, u32[]{:S(2)}) copy-start(bf16[256,768]{1,0:T(8,128)(2,1)} %qkv_ref.3) | copy-start | bytes 1179652
  15.6 1.5 %copy-start.2 = (bf16[256,256]{1,0:T(8,128)(2,1)S(1)}, bf16[256,256]{1,0:T(8,128)(2,1)}, u32[]{:S(2)}) copy-start(bf16[256,256]{1,0:T(8,128)(2,1)} %out_ref.3) | copy-start | bytes 393220
  15.6 6.8 %collective-permute-start.3 = (bf16[9,48,256]{2,1,0:T(8,128)(2,1)S(1)}, bf16[9,48,256]{2,1,0:T(8,128)(2,1)S(1)}, u32[]{:S(2)}, u32[]{:S(2)}) collective-permute-start(bf16[9,48,256]{2,1,0:T(8,128)(2,1)S(1)} %pad_maximum_fusion.2), channel_id=1, source_target_pairs={{1,0},{2,1},{3,2},{4,3},{5,4},{6,5},{7,6},{8,7},{9,8},{10,9},{11,1... | collective-permute-start | bytes 663560 | tf_op jit(solution)/shard_map/ppermute | solution.py:35
  28.5 6.4 %collective-permute-start.4 = (bf16[32,40,128]{2,1,0:T(8,128)(2,1)S(1)}, bf16[32,40,128]{2,1,0:T(8,128)(2,1)S(1)}, u32[]{:S(2)}, u32[]{:S(2)}) collective-permute-start(bf16[32,40,128]{2,1,0:T(8,128)(2,1)S(1)} %get-tuple-element.41), channel_id=1, source_target_pairs={{0,128},{128,0},{1,129},{129,1},{2,130},{130,2},{3,131},{131,3},{4... | collective-permute-start | bytes 983048 | tf_op jit(solution)/shard_map/ppermute | solution.py:478
  88.6 7.8 %collective-permute-start.5 = (bf16[32,40,128]{2,1,0:T(8,128)(2,1)S(1)}, bf16[32,40,128]{2,1,0:T(8,128)(2,1)S(1)}, u32[]{:S(2)}, u32[]{:S(2)}) collective-permute-start(bf16[32,40,128]{2,1,0:T(8,128)(2,1)S(1)} %all_to_all.17.mine_ref), channel_id=1, source_target_pairs={{0,128},{128,0},{1,129},{129,1},{2,130},{130,2},{3,131},{131,3},{4... | collective-permute-start | bytes 983048 | tf_op jit(solution)/shard_map/ppermute | solution.py:482

commit v6 on v5

--- a/solution.py
+++ b/solution.py
@@ -5,6 +5,7 @@
 import jax.numpy as jnp
 from jax import lax
 from jax.experimental import pallas as pl
+from jax.experimental.layout import Layout, with_layout_constraint
 from jax.experimental.pallas import tpu as pltpu
 from jax.sharding import PartitionSpec as P
 
@@ -32,7 +33,9 @@
     count = lax.axis_size(axis)
     forward = [(i, i + 1) for i in range(count - 1)]
     backward = [(target, source) for source, target in forward]
-    return lax.ppermute(to_next, axis, forward), lax.ppermute(to_previous, axis, backward)
+    from_previous = lax.ppermute(to_next, axis, forward)
+    from_next = lax.ppermute(to_previous, axis, backward)
+    return from_previous, from_next
 
 
 def nn(left, right):
@@ -176,94 +179,64 @@
     )
 
 
-def block_kernel(
+def side_pairs(
+    starts,
     total_cols,
     place_ref,
-    tok_ref,
-    cot_ref,
-    left_ref,
-    right_ref,
+    side_ref,
     adaptive_ref,
     qkv_ref,
     out_ref,
-    own_query_ref,
-    own_key_ref,
-    own_value_ref,
-    own_grad_ref,
+    own,
     mask_ref,
-    query_raw_ref,
-    query_inv_ref,
-    key_raw_ref,
-    key_inv_ref,
-    own_attended_ref,
-    own_grad_query_ref,
-    own_grad_key_ref,
-    own_grad_value_ref,
-    result_ref,
-    grad_tokens_ref,
-    mine_ref,
-    other_ref,
-    query_ref,
-    key_ref,
-    value_ref,
-    grad_ref,
+    side,
     attended_ref,
     grad_query_ref,
     grad_key_ref,
     grad_value_ref,
-    whole_ref,
 ):
-    cols, rows, width = tok_ref.shape
+    cols, rows, width = own[0].shape
     height = rows - 2 * EDGE
-    query_cols = cols + REACH
     last = REACH + cols
     col_first = place_ref[1]
-    image = place_ref[2]
-    core = place_ref[3]
-    step_value = place_ref[4]
-    adaptive = adaptive_ref[...]
-    factor = score_scale / HEAD_DIM
-    average = average_matrix(width)
-
-    for ref, col in ((left_ref, 0), (right_ref, last)):
-        pixels = ref[:REACH].astype(jnp.float32).reshape(REACH * rows, width)
-        _, _, query, key, value, _ = projected(pixels, adaptive, qkv_ref, average)
-        here = pl.ds(col, REACH)
-        query_ref[here] = query.astype(jnp.bfloat16).reshape(REACH, rows, width)
-        key_ref[here] = key.astype(jnp.bfloat16).reshape(REACH, rows, width)
-        value_ref[here] = value.astype(jnp.bfloat16).reshape(REACH, rows, width)
-        side = ref[REACH:].reshape(RADIUS * rows, width)
-        grad = nt(side, out_ref[...]).astype(jnp.bfloat16).reshape(RADIUS, rows, width)
-        grad_ref[pl.ds(0 if col == 0 else col - RADIUS, RADIUS)] = grad
-    query_ref[pl.ds(REACH, cols)] = own_query_ref[...]
-    key_ref[pl.ds(REACH, cols)] = own_key_ref[...]
-    value_ref[pl.ds(REACH, cols)] = own_value_ref[...]
-    grad_ref[pl.ds(RADIUS, cols)] = own_grad_ref[...]
-    attended_ref[pl.ds(RADIUS, SPAN)] = own_attended_ref[...]
-    grad_query_ref[pl.ds(RADIUS, SPAN)] = own_grad_query_ref[...]
-    grad_key_ref[...] = own_grad_key_ref[...]
-    grad_value_ref[...] = own_grad_value_ref[...]
-
-    for start in range(0, query_cols, SPAN):
-        if start == REACH:
-            continue
-        near = pl.ds(start, WINDOW)
+    left = starts[0] == 0
+    pixels = side_ref[:REACH].astype(jnp.float32).reshape(REACH * rows, width)
+    _, _, query, key, value, _ = projected(pixels, adaptive_ref[...], qkv_ref, average_matrix(width))
+    for ref, values in zip(side, (query, key, value)):
+        ref[...] = values.astype(jnp.bfloat16).reshape(REACH, rows, width)
+    grad = nt(side_ref[REACH:].reshape(RADIUS * rows, width), out_ref[...])
+    side[3][...] = grad.astype(jnp.bfloat16).reshape(RADIUS, rows, width)
+
+    def columns(which, low, high):
+        beside = side[which]
+        base = (REACH - beside.shape[0]) if left else last
+        parts = []
+        if left and low < REACH:
+            parts.append(beside[low - base : min(high, REACH) - base])
+        if max(low, REACH) < min(high, last):
+            parts.append(own[which][max(low, REACH) - REACH : min(high, last) - REACH])
+        if not left and high > last:
+            parts.append(beside[max(low, last) - base : high - base])
+        joined = parts[0] if len(parts) == 1 else jnp.concatenate(parts, axis=0)
+        return joined.reshape((high - low) * rows, width)
+
+    done = 0
+    for start in starts:
         masks = []
-        for column in range(WINDOW):
-            mask = mask_ref[column]
-            if start + column < REACH or start + column >= last:
-                image_col = col_first + (start + column - REACH)
+        for column in range(start, start + WINDOW):
+            mask = mask_ref[column - start]
+            if column < REACH or column >= last:
+                image_col = col_first + (column - REACH)
                 mask = mask * jnp.where((image_col >= 0) & (image_col < total_cols), 1.0, 0.0)
             masks.append(mask)
-        low = max(start, REACH)
-        high = min(start + WINDOW, last)
-        query_low = max(start + RADIUS, REACH)
-        query_high = min(start + RADIUS + SPAN, last)
+        low, high = max(start, REACH), min(start + WINDOW, last)
+        first = start + RADIUS
+        query_low, query_high = max(first, REACH), min(first + SPAN, last)
         attended, grad_query, grad_key, grad_value = attend(
-            key_ref[near].reshape(WINDOW * rows, width),
-            value_ref[near].reshape(WINDOW * rows, width),
-            query_ref[pl.ds(start + RADIUS, SPAN)].reshape(SPAN * rows, width),
-            grad_ref[pl.ds(start, SPAN)].reshape(SPAN * rows, width),
+            columns(1, start, start + WINDOW),
+            columns(2, start, start + WINDOW),
+            columns(0, first, first + SPAN),
+            columns(3, first, first + SPAN),
             jnp.concatenate(masks, axis=0),
             rows,
             height,
@@ -272,19 +245,99 @@
             high - low,
         )
         if query_low < query_high:
-            own = slice(query_low - start - RADIUS, query_high - start - RADIUS)
-            there = pl.ds(query_low - REACH, query_high - query_low)
-            attended_ref[there] = attended[own]
-            grad_query_ref[there] = grad_query[own]
+            there = pl.ds(done, query_high - query_low)
+            attended_ref[there] = attended[query_low - first : query_high - first]
+            grad_query_ref[there] = grad_query[query_low - first : query_high - first]
+            done += query_high - query_low
         there = pl.ds(low - REACH, high - low)
         grad_key_ref[there] += grad_key
         grad_value_ref[there] += grad_value
+
+
+def left_kernel(
+    starts,
+    total_cols,
+    place_ref,
+    side_ref,
+    adaptive_ref,
+    qkv_ref,
+    out_ref,
+    query_ref,
+    key_ref,
+    value_ref,
+    grad_ref,
+    mask_ref,
+    own_grad_key_ref,
+    own_grad_value_ref,
+    attended_ref,
+    grad_query_ref,
+    grad_key_ref,
+    grad_value_ref,
+    *side,
+):
+    grad_key_ref[...] = own_grad_key_ref[...]
+    grad_value_ref[...] = own_grad_value_ref[...]
+    own = (query_ref, key_ref, value_ref, grad_ref)
+    results = (attended_ref, grad_query_ref, grad_key_ref, grad_value_ref)
+    side_pairs(starts, total_cols, place_ref, side_ref, adaptive_ref, qkv_ref, out_ref, own, mask_ref, side, *results)
+
+
+def right_kernel(
+    starts,
+    total_cols,
+    place_ref,
+    tok_ref,
+    cot_ref,
+    side_ref,
+    adaptive_ref,
+    qkv_ref,
+    out_ref,
+    query_ref,
+    key_ref,
+    value_ref,
+    grad_ref,
+    mask_ref,
+    query_raw_ref,
+    query_inv_ref,
+    key_raw_ref,
+    key_inv_ref,
+    own_attended_ref,
+    own_grad_query_ref,
+    left_attended_ref,
+    left_grad_query_ref,
+    left_grad_key_ref,
+    left_grad_value_ref,
+    result_ref,
+    grad_tokens_ref,
+    mine_ref,
+    other_ref,
+    attended_ref,
+    grad_query_ref,
+    grad_key_ref,
+    grad_value_ref,
+    whole_ref,
+    *side,
+):
+    cols, rows, width = tok_ref.shape
+    height = rows - 2 * EDGE
+    image = place_ref[2]
+    core = place_ref[3]
+    step_value = place_ref[4]
+    adaptive = adaptive_ref[...]
+    factor = score_scale / HEAD_DIM
+    average = average_matrix(width)
+    grad_key_ref[...] = left_grad_key_ref[...]
+    grad_value_ref[...] = left_grad_value_ref[...]
+    own = (query_ref, key_ref, value_ref, grad_ref)
+    results = (attended_ref, grad_query_ref, grad_key_ref, grad_value_ref)
+    side_pairs(starts, total_cols, place_ref, side_ref, adaptive_ref, qkv_ref, out_ref, own, mask_ref, side, *results)
 
     tokens = cols * height
     pixels = tok_ref[:, :height].astype(jnp.float32).reshape(tokens, width)
     inverse, normed = normalized(pixels, adaptive)
     cot_own = cot_ref[:, :height].reshape(tokens, width)
-    attended = attended_ref[...].reshape(tokens, width)
+    parts = (left_attended_ref[...], own_attended_ref[...], attended_ref[...])
+    attended = jnp.concatenate(parts, axis=0).reshape(tokens, width)
     result = pixels + nn(attended, out_ref[...])
     result_ref[...] = result.astype(jnp.bfloat16).reshape(cols, height, width)
     whole_ref[:, 3 * width :] = tn(attended, cot_own)
@@ -292,7 +345,8 @@
     def back(raw, inv, grad, scale):
         return scale * inv * (grad - raw * inv * inv * head_mean(grad * raw, average))
 
-    grad_query = grad_query_ref[...].reshape(tokens, width)
+    parts = (left_grad_query_ref[...], own_grad_query_ref[...], grad_query_ref[...])
+    grad_query = jnp.concatenate(parts, axis=0).reshape(tokens, width)
     grad_key = grad_key_ref[...].reshape(tokens, width)
     grad_project = jnp.concatenate(
         [
@@ -380,8 +434,17 @@
     total_rows = height * lax.axis_size("row")
     total_cols = cols * lax.axis_size("col")
     rows = height + 2 * EDGE
+
+    def lying(values):
+        return with_layout_constraint(values, Layout(major_to_minor=(0, 1, 2)))
+
+    def edge_rows(low, high):
+        return lying(jnp.concatenate([tokens[0, low:high], cotangent[0, low:high]], axis=0))
+
     both = jnp.concatenate([tokens[0].transpose(1, 0, 2), cotangent[0].transpose(1, 0, 2)], axis=0)
-    above, below = exchange(both[:, height - EDGE :], both[:, :EDGE], "row")
+    above, below = exchange(edge_rows(height - EDGE, height), edge_rows(0, EDGE), "row")
+    above, below = (lying(rows_).transpose(1, 0, 2).reshape(cols, 2, EDGE, width) for rows_ in (above, below))
+    above, below = (rows_.transpose(1, 0, 2, 3).reshape(2 * cols, EDGE, width) for rows_ in (above, below))
     both = jnp.concatenate([both, above, below], axis=1)
     tok, cot = both[:cols], both[cols:]
     to_next = jnp.concatenate([tok[cols - REACH :], cot[cols - RADIUS :]], axis=0)
@@ -395,8 +458,6 @@
     place = [row_first, col_first, image, lax.axis_index("core"), timesteps[0]]
     place = jnp.stack(place).astype(jnp.int32)
 
-    around = cols + 2 * REACH
-    query_cols = cols + REACH
     lanes = width // HEAD_DIM * SPAN * rows
     smem = pl.BlockSpec(memory_space=pltpu.SMEM)
     vmem = pl.BlockSpec(memory_space=pltpu.VMEM)
@@ -404,43 +465,75 @@
     tall = jax.ShapeDtypeStruct((cols, rows, width), jnp.bfloat16)
     block = jax.ShapeDtypeStruct((cols, height, width), jnp.bfloat16)
     exact = jax.ShapeDtypeStruct((cols, height, width), jnp.float32)
-    mask = jax.ShapeDtypeStruct((WINDOW, rows, lanes), jnp.float32)
+    masked = jax.ShapeDtypeStruct((WINDOW, rows, lanes), jnp.float32)
     pair = (
         jax.ShapeDtypeStruct((SPAN, height, width), jnp.bfloat16),
         jax.ShapeDtypeStruct((SPAN, height, width), jnp.float32),
     )
     prepared = pl.pallas_call(
         functools.partial(own_kernel, total_rows),
-        out_shape=(tall,) * 4 + (mask,) + (exact,) * 4 + pair + (exact,) * 2,
+        out_shape=(tall,) * 4 + (masked,) + (exact,) * 4 + pair + (exact,) * 2,
         in_specs=[smem] + [vmem] * 5,
         out_specs=(vmem,) * 13,
         compiler_params=limits,
         cost_estimate=pl.CostEstimate(flops=1_000_000_000, bytes_accessed=4_000_000, transcendentals=200_000),
         name="own",
     )(place, tok, cot, adaptive, qkv_weight, output_weight)
+    *own, mask, query_raw, query_inv, key_raw, key_inv, attended, grad_query, grad_key, grad_value = prepared
+    starts = tuple(range(0, cols + REACH, SPAN))
+    middle = starts.index(REACH)
+    third = (cols - SPAN) // 2
+    part = (
+        jax.ShapeDtypeStruct((third, height, width), jnp.bfloat16),
+        jax.ShapeDtypeStruct((third, height, width), jnp.float32),
+    )
+    side = [pltpu.VMEM((REACH, rows, width), jnp.bfloat16)] * 3 + [pltpu.VMEM((RADIUS, rows, width), jnp.bfloat16)]
+    from_left = pl.pallas_call(
+        functools.partial(left_kernel, starts[:middle], total_cols),
+        out_shape=part + (exact,) * 2,
+        in_specs=[smem] + [vmem] * 11,
+        out_specs=(vmem,) * 4,
+        scratch_shapes=side,
+        compiler_params=limits,
+        cost_estimate=pl.CostEstimate(flops=2_000_000_000, bytes_accessed=2_000_000, transcendentals=400_000),
+        name="left",
+    )(place, left, adaptive, qkv_weight, output_weight, *own, mask, grad_key, grad_value)
     pieces = width // CORES // LINES * (4 * width // LANES)
     chunks = jax.ShapeDtypeStruct((pieces, LINES + SLOT, LANES), jnp.bfloat16)
-    wide = pltpu.VMEM((around, rows, width), jnp.bfloat16)
     result, grad_tokens, mine, other = pl.pallas_call(
-        functools.partial(block_kernel, total_cols),
+        functools.partial(right_kernel, starts[middle + 1 :], total_cols),
         out_shape=(block, block, chunks, chunks),
-        in_specs=[smem] + [vmem] * 20,
+        in_specs=[smem] + [vmem] * 21,
         out_specs=(vmem,) * 4,
         scratch_shapes=[
-            wide,
-            wide,
-            wide,
-            pltpu.VMEM((query_cols, rows, width), jnp.bfloat16),
-            pltpu.VMEM((cols, height, width), jnp.bfloat16),
-            pltpu.VMEM((cols, height, width), jnp.float32),
+            pltpu.VMEM((third, height, width), jnp.bfloat16),
+            pltpu.VMEM((third, height, width), jnp.float32),
             pltpu.VMEM((cols, height, width), jnp.float32),
             pltpu.VMEM((cols, height, width), jnp.float32),
             pltpu.VMEM((width, 4 * width), jnp.float32),
-        ],
+        ]
+        + side,
         compiler_params=limits,
-        cost_estimate=pl.CostEstimate(flops=8_000_000_000, bytes_accessed=4_000_000, transcendentals=1_000_000),
-        name="block",
-    )(place, tok, cot, left, right, adaptive, qkv_weight, output_weight, *prepared)
+        cost_estimate=pl.CostEstimate(flops=3_000_000_000, bytes_accessed=3_000_000, transcendentals=400_000),
+        name="right",
+    )(
+        place,
+        tok,
+        cot,
+        right,
+        adaptive,
+        qkv_weight,
+        output_weight,
+        *own,
+        mask,
+        query_raw,
+        query_inv,
+        key_raw,
+        key_inv,
+        attended,
+        grad_query,
+        *from_left,
+    )
     result = result.transpose(1, 0, 2)
     grad_tokens = grad_tokens.transpose(1, 0, 2)
 

time: 98.9 us -> 98.7 us (level)
  starting transfers between devices: 22.2 us -> 28.2 us
  waiting for transfers between devices: 7.82 us -> 2.15 us
  blocking collectives: 53.4 us -> 52.2 us
    ppermute x4, waiting for transfers between devices: 6.59 us -> 0.91 us  [the longest x2 0.91 us: exchange(): from_previous = lax.ppermute(to_next, axis, forward)]
    ppermute x1, starting transfers between devices: 5.16 us -> 9.56 us  [summed(): mine = total(jnp.stack([mine, lax.ppermute(other, 'core', partner)]))]
    ppermute x4, starting transfers between devices: 10.7 us -> 12.3 us  [the longest x2 9.58 us: exchange(): from_previous = lax.ppermute(to_next, axis, forward)]
    all_to_all x3, blocking collectives: 53.4 us -> 52.2 us  [swap(): return lax.all_to_all(pieces, axes, 0, 0, tiled=True)]
    transpose x1, local copies, waits for them, and re-layouts: 1.05 us -> 0.05 us  [on_device(): cotangent[0].transpose(1, 0, 2)]
    pallas_call x1 -> x2, Pallas kernels: 6.08 us -> 6.84 us  [the longest x1 3.74 us: on_device(): pl.pallas_call(functools.partial(right_kernel, starts[middle + 1:], total...]
  transfers between devices with their start and end apart: 6 -> 6, of which waited for: 3 -> 3; matrix products, arithmetic and copies ran while one was open for 2% -> 2% of each run, Pallas kernels for 2% -> 5%
where the time goes in v6:
time: 98.7 us; the launch traced here: 98.3 us
  blocking collectives  52.2 us (53%)
  starting transfers between devices  28.2 us (29%)
  Pallas kernels  11.1 us (11%)
  local copies, waits for them, and re-layouts  2.68 us (3%)
  waiting for transfers between devices  2.15 us (2%)
  between operations  1.56 us (2%)
    all_to_all x3, blocking collectives, swap(): return lax.all_to_all(pieces, axes, 0, 0, tiled=True)  52.2 us
    ppermute x2, starting transfers between devices, exchange(): from_previous = lax.ppermute(to_next, axis, forward)  9.58 us
    ppermute x1, starting transfers between devices, summed(): mine = total(jnp.stack([mine, lax.ppermute(other, 'core', partner)]))  9.56 us
    ppermute x1, starting transfers between devices, summed(): return (mine, lax.ppermute(mine, 'core', partner))  6.32 us
    pallas_call x1, Pallas kernels, on_device(): pl.pallas_call(functools.partial(right_kernel, starts[middle + 1:], total...  3.74 us
    pallas_call x1, Pallas kernels, on_device(): pl.pallas_call(functools.partial(left_kernel, starts[:middle], total_cols...  3.1 us
    ppermute x2, starting transfers between devices, exchange(): from_next = lax.ppermute(to_previous, axis, backward)  2.72 us
    pallas_call x1, Pallas kernels, on_device(): pl.pallas_call(functools.partial(finish_kernel, (lax.axis_size('zone') *...  2.18 us
  transfers between devices with their start and end apart: 6, of which 3 were waited for; matrix products, arithmetic and copies ran while one was open for 2% of the time, Pallas kernels for 5%

profile of v6, /device:TPU:1, one launch (start us, length us, event | category | flops | bytes accessed | tf_op | source)
XLA Modules:
  0.0 98.3 jit_solution(11591181496102981288)
XLA Ops:
  0.6 0.0 copy-start
  0.6 0.9 slice_bitcast_fusion.2
  1.5 0.0 copy-start.3
  1.5 0.0 copy-start.4
  1.5 1.4 %collective-permute-start.1 = (bf16[16,8,256]{2,1,0:T(8,128)(2,1)S(1)}, bf16[16,8,256]{2,1,0:T(8,128)(2,1)S(1)}, u32[]{:S(2)}, u32[]{:S(2)}) collective-permute-start(bf16[16,8,256]{2,1,0:T(8,128)(2,1)S(1)} %pad_maximum_fusion.4), channel_id=1, source_target_pairs={{32,0},{64,32},{96,64},{33,1},{65,33},{97,65},{34,2},{66,34},{98,6... | collective-permute-start | bytes 196616 | tf_op jit(solution)/shard_map/ppermute | solution.py:37
  3.0 5.4 %collective-permute-start = (bf16[16,8,256]{2,1,0:T(8,128)(2,1)S(1)}, bf16[16,8,256]{2,1,0:T(8,128)(2,1)S(1)}, u32[]{:S(2)}, u32[]{:S(2)}) collective-permute-start(bf16[16,8,256]{2,1,0:T(8,128)(2,1)S(1)} %pad_maximum_fusion.3), channel_id=1, source_target_pairs={{0,32},{32,64},{64,96},{1,33},{33,65},{65,97},{2,34},{34,66},{66,9... | collective-permute-start | bytes 196616 | tf_op jit(solution)/shard_map/ppermute | solution.py:36
  8.4 0.0 copy-done.3
  8.5 0.0 copy-done.4
  8.5 0.1 copy_bitcast_fusion
  9.2 0.0 copy-done
  9.3 0.1 fusion.5
  9.4 0.1 stack.22.place_ref
  9.5 0.0 collective-permute-done.1
  9.6 0.2 collective-permute-done
  9.9 1.3 %collective-permute-start.2 = (bf16[9,48,256]{2,1,0:T(8,128)(2,1)S(1)}, bf16[9,48,256]{2,1,0:T(8,128)(2,1)S(1)}, u32[]{:S(2)}, u32[]{:S(2)}) collective-permute-start(bf16[9,48,256]{2,1,0:T(8,128)(2,1)S(1)} %pad_maximum_fusion.1), channel_id=1, source_target_pairs={{1,0},{2,1},{3,2},{4,3},{5,4},{6,5},{7,6},{8,7},{9,8},{10,9},{11,1... | collective-permute-start | bytes 663560 | tf_op jit(solution)/shard_map/ppermute | solution.py:37
  11.2 0.0 copy-start.1
  11.2 0.0 copy-start.2
  11.2 4.1 %collective-permute-start.3 = (bf16[9,48,256]{2,1,0:T(8,128)(2,1)S(1)}, bf16[9,48,256]{2,1,0:T(8,128)(2,1)S(1)}, u32[]{:S(2)}, u32[]{:S(2)}) collective-permute-start(bf16[9,48,256]{2,1,0:T(8,128)(2,1)S(1)} %pad_maximum_fusion.2), channel_id=1, source_target_pairs={{0,1},{1,2},{2,3},{3,4},{4,5},{5,6},{6,7},{7,8},{8,9},{9,10},{10,1... | collective-permute-start | bytes 663560 | tf_op jit(solution)/shard_map/ppermute | solution.py:36
  15.4 0.0 copy-done.1
  15.4 0.0 copy-done.2
  15.4 2.1 %own.1 = (bf16[8,48,256]{2,1,0:T(8,128)(2,1)S(1)}, bf16[8,48,256]{2,1,0:T(8,128)(2,1)S(1)}, bf16[8,48,256]{2,1,0:T(8,128)(2,1)S(1)}, bf16[8,48,256]{2,1,0:T(8,12...) custom-call(s32[5]{0:T(128)S(1)} %stack.22.place_ref, ...), custom_call_target="tpu_custom_call" | custom-call | flops 1000000000 | bytes 4000000 | tf_op jit(solution)/shard_map/own/pallas_call | solution.py:473
  17.5 0.7 collective-permute-done.3.side_ref
  18.2 3.1 %left.1 = (bf16[3,32,256]{2,1,0:T(8,128)(2,1)S(1)}, f32[3,32,256]{2,1,0:T(8,128)S(1)}, f32[8,32,256]{2,1,0:T(8,128)S(1)}, f32[8,32,256]{2,1,0:T(8,128)S(1)}) custom-call(s32[5]{0:T(128)S(1)} %stack.22.place_ref, bf16[9,48,256]{2,1,0:T(8,128)(2,1)S(1)} %collective-permute-done.3.side_ref, f32[1,256]{1,0:T(1,128)S(1)} %bitcast.47, ...), custom_call_target="tpu_custom_call" | custom-call | flops 2000000000 | bytes 2000000 | tf_op jit(solution)/shard_map/left/pallas_call | solution.py:491
  21.3 0.0 collective-permute-done.2.side_ref
  21.4 3.7 %right.1 = (bf16[8,32,256]{2,1,0:T(8,128)(2,1)S(1)}, bf16[8,32,256]{2,1,0:T(8,128)(2,1)S(1)}, bf16[32,40,128]{2,1,0:T(8,128)(2,1)S(1)}, bf16[32,40,128]{2,1,0:T(8,128)(2,1)S(1)}) custom-call(s32[5]{0:T(128)S(1)} %stack.22.place_ref, bf16[8,48,256]{2,1,0:T(8,128)(2,1)S(1)} %get-tuple-element.68.tok_ref, bf16[8,48,256]{2,1,0:T(8,128)(2,1)S(1)} %get-tuple-element.67.cot_ref, ...), custom_call_target="tpu_custom_call" | custom-call | flops 3000000000 | bytes 3000000 | tf_op jit(solution)/shard_map/right/pallas_call | solution.py:503
  25.1 9.6 %collective-permute-start.4 = (bf16[32,40,128]{2,1,0:T(8,128)(2,1)S(1)}, bf16[32,40,128]{2,1,0:T(8,128)(2,1)S(1)}, u32[]{:S(2)}, u32[]{:S(2)}) collective-permute-start(bf16[32,40,128]{2,1,0:T(8,128)(2,1)S(1)} %get-tuple-element.49), channel_id=1, source_target_pairs={{0,128},{128,0},{1,129},{129,1},{2,130},{130,2},{3,131},{131,3},{4... | collective-permute-start | bytes 983048 | tf_op jit(solution)/shard_map/ppermute | solution.py:571
  34.7 1.2 %collective-permute-done.4 = bf16[32,40,128]{2,1,0:T(8,128)(2,1)S(1)} collective-permute-done((bf16[32,40,128]{2,1,0:T(8,128)(2,1)S(1)}, bf16[32,40,128]{2,1,0:T(8,128)(2,1)S(1)}, u32[]{:S(2)}, u32[]{:S(2)}) %collective-permute-start.4) | collective-permute-done | bytes 327712 | tf_op jit(solution)/shard_map/ppermute | solution.py:571
  35.9 0.1 reduce_sum.34
  36.0 17.2 %all_to_all.15 = bf16[32,40,128]{2,1,0:T(8,128)(2,1)S(1)} all-to-all(bf16[32,40,128]{2,1,0:T(8,128)(2,1)S(1)} %reduce_sum.34), channel_id=1, replica_groups=mesh['zone'=2,'core'=2,'row'=4,'col'=32] {'col'}, dimensions={0} | all-to-all | bytes 655360 | tf_op jit(solution)/shard_map/all_to_all | solution.py:557
  53.2 0.1 reduce_sum.35
  53.3 17.7 %all_to_all.16 = bf16[8,40,128]{2,1,0:T(8,128)(2,1)S(1)} all-to-all(bf16[8,40,128]{2,1,0:T(8,128)(2,1)S(1)} %broadcast_in_dim.10), channel_id=1, replica_groups=mesh['zone'=2,'core'=2,'row'=4,'col'=32] {'zone','row'}, dimensions={0} | all-to-all | bytes 163840 | tf_op jit(solution)/shard_map/all_to_all | solution.py:557
  71.0 17.3 %all_to_all.17.mine_ref = bf16[32,40,128]{2,1,0:T(8,128)(2,1)S(1)} all-to-all(bf16[32,40,128]{2,1,0:T(8,128)(2,1)S(1)} %broadcast_in_dim.22), channel_id=1, replica_groups=mesh['zone'=2,'core'=2,'row'=4,'col'=32] {'col'}, dimensions={0} | all-to-all | bytes 655360 | tf_op jit(solution)/shard_map/all_to_all | solution.py:557
  88.3 6.3 %collective-permute-start.5 = (bf16[32,40,128]{2,1,0:T(8,128)(2,1)S(1)}, bf16[32,40,128]{2,1,0:T(8,128)(2,1)S(1)}, u32[]{:S(2)}, u32[]{:S(2)}) collective-permute-start(bf16[32,40,128]{2,1,0:T(8,128)(2,1)S(1)} %all_to_all.17.mine_ref), channel_id=1, source_target_pairs={{0,128},{128,0},{1,129},{129,1},{2,130},{130,2},{3,131},{131,3},{4... | collective-permute-start | bytes 983048 | tf_op jit(solution)/shard_map/ppermute | solution.py:575
  94.7 0.7 copy.21
  95.4 0.7 copy.22
  96.1 0.0 collective-permute-done.5.other_ref
  96.1 2.2 %finish.1 = (f32[256,768]{1,0:T(8,128)}, f32[256,256]{1,0:T(8,128)}, f32[256,256]{1,0:T(8,128)}) custom-call(s32[5]{0:T(128)S(1)} %stack.22.place_ref, bf16[32,40,128]{2,1,0:T(8,128)(2,1)S(1)} %all_to_all.17.mine_ref, bf16[32,40,128]{2,1,0:T(8,128)(2,1)S(1)} %collective-permute-done.5.other_ref), custom_call_target="tpu_custom_call" | custom-call | tf_op jit(solution)/shard_map/finish/pallas_call | solution.py:541
  (16 shorter events, 0.3 us)
Async XLA Ops:
  0.6 8.6 %copy-start = (bf16[256,256]{1,0:T(8,128)(2,1)S(1)}, bf16[256,256]{1,0:T(8,128)(2,1)}, u32[]{:S(2)}) copy-start(bf16[256,256]{1,0:T(8,128)(2,1)} %param.11) | copy-start | bytes 393220
  1.5 6.9 %copy-start.3 = (bf16[1,32,8,256]{3,2,1,0:T(8,128)(2,1)S(1)}, bf16[1,32,8,256]{3,2,1,0:T(8,128)(2,1)}, u32[]{:S(2)}) copy-start(bf16[1,32,8,256]{3,2,1,0:T(8,128)(2,1)} %param.8) | copy-start | bytes 393220
  1.5 6.9 %copy-start.4 = (bf16[1,32,8,256]{3,2,1,0:T(8,128)(2,1)S(1)}, bf16[1,32,8,256]{3,2,1,0:T(8,128)(2,1)}, u32[]{:S(2)}) copy-start(bf16[1,32,8,256]{3,2,1,0:T(8,128)(2,1)} %param.6) | copy-start | bytes 393220
  1.5 8.0 %collective-permute-start.1 = (bf16[16,8,256]{2,1,0:T(8,128)(2,1)S(1)}, bf16[16,8,256]{2,1,0:T(8,128)(2,1)S(1)}, u32[]{:S(2)}, u32[]{:S(2)}) collective-permute-start(bf16[16,8,256]{2,1,0:T(8,128)(2,1)S(1)} %pad_maximum_fusion.4), channel_id=1, source_target_pairs={{32,0},{64,32},{96,64},{33,1},{65,33},{97,65},{34,2},{66,34},{98,6... | collective-permute-start | bytes 196616 | tf_op jit(solution)/shard_map/ppermute | solution.py:37
  3.0 6.8 %collective-permute-start = (bf16[16,8,256]{2,1,0:T(8,128)(2,1)S(1)}, bf16[16,8,256]{2,1,0:T(8,128)(2,1)S(1)}, u32[]{:S(2)}, u32[]{:S(2)}) collective-permute-start(bf16[16,8,256]{2,1,0:T(8,128)(2,1)S(1)} %pad_maximum_fusion.3), channel_id=1, source_target_pairs={{0,32},{32,64},{64,96},{1,33},{33,65},{65,97},{2,34},{34,66},{66,9... | collective-permute-start | bytes 196616 | tf_op jit(solution)/shard_map/ppermute | solution.py:36
  9.9 11.4 %collective-permute-start.2 = (bf16[9,48,256]{2,1,0:T(8,128)(2,1)S(1)}, bf16[9,48,256]{2,1,0:T(8,128)(2,1)S(1)}, u32[]{:S(2)}, u32[]{:S(2)}) collective-permute-start(bf16[9,48,256]{2,1,0:T(8,128)(2,1)S(1)} %pad_maximum_fusion.1), channel_id=1, source_target_pairs={{1,0},{2,1},{3,2},{4,3},{5,4},{6,5},{7,6},{8,7},{9,8},{10,9},{11,1... | collective-permute-start | bytes 663560 | tf_op jit(solution)/shard_map/ppermute | solution.py:37
  11.2 4.2 %copy-start.1 = (bf16[256,768]{1,0:T(8,128)(2,1)S(1)}, bf16[256,768]{1,0:T(8,128)(2,1)}, u32[]{:S(2)}) copy-start(bf16[256,768]{1,0:T(8,128)(2,1)} %qkv_ref.5) | copy-start | bytes 1179652
  11.2 4.2 %copy-start.2 = (bf16[256,256]{1,0:T(8,128)(2,1)S(1)}, bf16[256,256]{1,0:T(8,128)(2,1)}, u32[]{:S(2)}) copy-start(bf16[256,256]{1,0:T(8,128)(2,1)} %out_ref.5) | copy-start | bytes 393220
  11.2 7.0 %collective-permute-start.3 = (bf16[9,48,256]{2,1,0:T(8,128)(2,1)S(1)}, bf16[9,48,256]{2,1,0:T(8,128)(2,1)S(1)}, u32[]{:S(2)}, u32[]{:S(2)}) collective-permute-start(bf16[9,48,256]{2,1,0:T(8,128)(2,1)S(1)} %pad_maximum_fusion.2), channel_id=1, source_target_pairs={{0,1},{1,2},{2,3},{3,4},{4,5},{5,6},{6,7},{7,8},{8,9},{9,10},{10,1... | collective-permute-start | bytes 663560 | tf_op jit(solution)/shard_map/ppermute | solution.py:36
  25.1 10.8 %collective-permute-start.4 = (bf16[32,40,128]{2,1,0:T(8,128)(2,1)S(1)}, bf16[32,40,128]{2,1,0:T(8,128)(2,1)S(1)}, u32[]{:S(2)}, u32[]{:S(2)}) collective-permute-start(bf16[32,40,128]{2,1,0:T(8,128)(2,1)S(1)} %get-tuple-element.49), channel_id=1, source_target_pairs={{0,128},{128,0},{1,129},{129,1},{2,130},{130,2},{3,131},{131,3},{4... | collective-permute-start | bytes 983048 | tf_op jit(solution)/shard_map/ppermute | solution.py:571
  88.3 7.8 %collective-permute-start.5 = (bf16[32,40,128]{2,1,0:T(8,128)(2,1)S(1)}, bf16[32,40,128]{2,1,0:T(8,128)(2,1)S(1)}, u32[]{:S(2)}, u32[]{:S(2)}) collective-permute-start(bf16[32,40,128]{2,1,0:T(8,128)(2,1)S(1)} %all_to_all.17.mine_ref), channel_id=1, source_target_pairs={{0,128},{128,0},{1,129},{129,1},{2,130},{130,2},{3,131},{131,3},{4... | collective-permute-start | bytes 983048 | tf_op jit(solution)/shard_map/ppermute | solution.py:575

commit v7 on v6

--- a/solution.py
+++ b/solution.py
@@ -84,13 +84,22 @@
     return [jnp.where(lane_head == head, 1.0, 0.0) for head in range(width // HEAD_DIM)]
 
 
-def attend(keys, values, queries, grads, mask, rows, height, wanted, first, count):
+def spread(part):
+    return jnp.concatenate([part * pick.astype(jnp.bfloat16) for pick in head_picks(part.shape[-1])], axis=0)
+
+
+def soften(scores, slope, mask):
+    exponent = jnp.exp(scores - score_scale) * mask
+    denominator = jnp.maximum(jnp.sum(exponent, axis=0, keepdims=True), 1e-30)
+    weights = (exponent * (1.0 / denominator)).astype(jnp.bfloat16)
+    wide = weights.astype(jnp.float32)
+    middle = jnp.sum(wide * slope, axis=0, keepdims=True)
+    return weights, (wide * (slope - middle)).astype(jnp.bfloat16)
+
+
+def combined(weights, grad_score, keys, values, queries, grads, rows, height, wanted, first, count):
     width = keys.shape[-1]
     picks = head_picks(width)
-    narrow = [pick.astype(jnp.bfloat16) for pick in picks]
-
-    def spread(part):
-        return jnp.concatenate([part * pick for pick in narrow], axis=0)
 
     def gathered(part):
         total = part[: SPAN * rows] * picks[0]
@@ -102,15 +111,6 @@
         shape = (WINDOW, rows, part.shape[1])
         return part.reshape(shape)[first : first + count, :height].reshape(-1, part.shape[1])
 
-    queries = spread(queries)
-    grads = spread(grads)
-    exponent = jnp.exp(nt(keys, queries) - score_scale) * mask
-    denominator = jnp.maximum(jnp.sum(exponent, axis=0, keepdims=True), 1e-30)
-    weights = (exponent * (1.0 / denominator)).astype(jnp.bfloat16)
-    wide = weights.astype(jnp.float32)
-    slope = nt(values, grads)
-    middle = jnp.sum(wide * slope, axis=0, keepdims=True)
-    grad_score = (wide * (slope - middle)).astype(jnp.bfloat16)
     attended = grad_query = None
     if wanted:
         attended = gathered(tn(weights, values)).astype(jnp.bfloat16)
@@ -174,8 +174,10 @@
     mask_ref[...] = mask
 
     pair = slice(RADIUS * rows, (RADIUS + SPAN) * rows)
-    attended_ref[...], grad_query_ref[...], grad_key_ref[...], grad_value_ref[...] = attend(
-        key, value, query[pair], grad[pair], mask.reshape(cols * rows, lanes), rows, height, True, 0, cols
+    queries, grads = spread(query[pair]), spread(grad[pair])
+    weights, grad_score = soften(nt(key, queries), nt(value, grads), mask.reshape(cols * rows, lanes))
+    attended_ref[...], grad_query_ref[...], grad_key_ref[...], grad_value_ref[...] = combined(
+        weights, grad_score, key, value, queries, grads, rows, height, True, 0, cols
     )
 
 
@@ -220,8 +222,13 @@
         joined = parts[0] if len(parts) == 1 else jnp.concatenate(parts, axis=0)
         return joined.reshape((high - low) * rows, width)
 
-    done = 0
-    for start in starts:
+    def scored(start):
+        first = start + RADIUS
+        keys, values = columns(1, start, start + WINDOW), columns(2, start, start + WINDOW)
+        queries, grads = spread(columns(0, first, first + SPAN)), spread(columns(3, first, first + SPAN))
+        return nt(keys, queries), nt(values, grads), (keys, values, queries, grads)
+
+    def softened(start, scores, slope):
         masks = []
         for column in range(start, start + WINDOW):
             mask = mask_ref[column - start]
@@ -229,20 +236,20 @@
                 image_col = col_first + (column - REACH)
                 mask = mask * jnp.where((image_col >= 0) & (image_col < total_cols), 1.0, 0.0)
             masks.append(mask)
+        return soften(scores, slope, jnp.concatenate(masks, axis=0))
+
+    done = 0
+    following = scored(starts[0])
+    for start in starts:
+        scores, slope, blocks = following
+        if start != starts[-1]:
+            following = scored(start + SPAN)
+        weights, grad_score = softened(start, scores, slope)
         low, high = max(start, REACH), min(start + WINDOW, last)
         first = start + RADIUS
         query_low, query_high = max(first, REACH), min(first + SPAN, last)
-        attended, grad_query, grad_key, grad_value = attend(
-            columns(1, start, start + WINDOW),
-            columns(2, start, start + WINDOW),
-            columns(0, first, first + SPAN),
-            columns(3, first, first + SPAN),
-            jnp.concatenate(masks, axis=0),
-            rows,
-            height,
-            query_low < query_high,
-            low - start,
-            high - low,
+        attended, grad_query, grad_key, grad_value = combined(
+            weights, grad_score, *blocks, rows, height, query_low < query_high, low - start, high - low
         )
         if query_low < query_high:
             there = pl.ds(done, query_high - query_low)
@@ -388,27 +395,38 @@
                 ref[block, LINES:] = jnp.zeros((SLOT, LANES), jnp.bfloat16)
 
 
-def finish_kernel(senders, place_ref, mine_ref, other_ref, qkv_ref, output_ref, time_ref):
+def half_gradients(which, half_ref, qkv_ref, output_ref, qkv_half, output_half, sems):
     width = output_ref.shape[0]
-    images = senders[0]
     half = width // CORES
     across = 4 * width // LANES
-    core = place_ref[3]
-    for ref, which in ((mine_ref, core), (other_ref, 1 - core)):
-        for block in range(mine_ref.shape[0]):
-            top = pl.multiple_of(which * half, half) + block // across * LINES
-            first = block % across * LANES
-            values = ref[block, :LINES].astype(jnp.float32)
-            if first < 3 * width:
-                qkv_ref[pl.ds(top, LINES), first : first + LANES] = values
-            else:
-                output_ref[pl.ds(top, LINES), first - 3 * width : first - 3 * width + LANES] = values
+    for block in range(half_ref.shape[0]):
+        top = block // across * LINES
+        first = block % across * LANES
+        values = half_ref[block, :LINES].astype(jnp.float32)
+        if first < 3 * width:
+            qkv_half[top : top + LINES, first : first + LANES] = values
+        else:
+            output_half[top : top + LINES, first - 3 * width : first - 3 * width + LANES] = values
+    there = pl.ds(pl.multiple_of(which * half, half), half)
+    copies = (
+        pltpu.make_async_copy(qkv_half, qkv_ref.at[there], sems.at[0]),
+        pltpu.make_async_copy(output_half, output_ref.at[there], sems.at[1]),
+    )
+    for copy in copies:
+        copy.start()
+    return copies
+
+
+def mine_kernel(senders, place_ref, mine_ref, qkv_ref, output_ref, time_ref, qkv_half, output_half, sems):
+    images, share = senders
+    width = output_ref.shape[0]
+    copies = half_gradients(place_ref[3], mine_ref, qkv_ref, output_ref, qkv_half, output_half, sems)
     sides = [mine_ref[block, LINES:].astype(jnp.float32) for block in range(width // LANES)]
     adaptives = jnp.concatenate(sides, axis=1)
     adaptives = jnp.where(lax.broadcasted_iota(jnp.int32, adaptives.shape, 0) < images, adaptives, 0.0)
     ladder = lax.broadcasted_iota(jnp.int32, (1, CF // 2), 1).astype(jnp.float32)
     frequency = jnp.exp(ladder * (-math.log(1000.0) / (CF // 2)))
-    steps = (sides[0][:, 0:1] * 32.0 + sides[0][:, 1:2]) / senders[1]
+    steps = (sides[0][:, 0:1] * 32.0 + sides[0][:, 1:2]) / share
     steps = jnp.concatenate([steps[SLOT // 2 :], steps[: SLOT // 2] * 0.0], axis=0)
     angle = steps * frequency
     features = jnp.concatenate([jnp.cos(angle), jnp.sin(angle)], axis=1)
@@ -419,12 +437,24 @@
         precision=lax.Precision.HIGHEST,
         preferred_element_type=jnp.float32,
     )
+    for copy in copies:
+        copy.wait()
+
+
+def other_kernel(place_ref, other_ref, qkv_in, output_in, qkv_ref, output_ref, qkv_half, output_half, sems):
+    for copy in half_gradients(1 - place_ref[3], other_ref, qkv_ref, output_ref, qkv_half, output_half, sems):
+        copy.wait()
 
 
 CORES = 2
+PARTNER = ((0, 1), (1, 0))
 SLOT = 8
 LINES = 32
 LANES = 128
+
+
+def lying(values):
+    return with_layout_constraint(values, Layout(major_to_minor=(0, 1, 2)))
 
 
 def on_device(tokens, timesteps, cotangent, qkv_weight, output_weight, time_weight):
@@ -434,9 +464,6 @@
     total_rows = height * lax.axis_size("row")
     total_cols = cols * lax.axis_size("col")
     rows = height + 2 * EDGE
-
-    def lying(values):
-        return with_layout_constraint(values, Layout(major_to_minor=(0, 1, 2)))
 
     def edge_rows(low, high):
         return lying(jnp.concatenate([tokens[0, low:high], cotangent[0, low:high]], axis=0))
@@ -534,22 +561,45 @@
         grad_query,
         *from_left,
     )
-    result = result.transpose(1, 0, 2)
-    grad_tokens = grad_tokens.transpose(1, 0, 2)
-
-    mine, other = summed(mine, other)
+    result = lying(result.transpose(1, 0, 2))
+    grad_tokens = lying(grad_tokens.transpose(1, 0, 2))
+
+    mine = summed(mine, other)
+    mine, result, grad_tokens = lax.optimization_barrier((mine, result, grad_tokens))
+    other = lax.ppermute(mine, "core", PARTNER)
+    anywhere = pl.BlockSpec(memory_space=pl.ANY)
+    gradients = (
+        jax.ShapeDtypeStruct((width, 3 * width), jnp.float32),
+        jax.ShapeDtypeStruct((width, width), jnp.float32),
+    )
+    halves = [
+        pltpu.VMEM((width // CORES, 3 * width), jnp.float32),
+        pltpu.VMEM((width // CORES, width), jnp.float32),
+        pltpu.SemaphoreType.DMA((2,)),
+    ]
+    small = pltpu.CompilerParams(vmem_limit_bytes=8 * 2**20)
+    senders = (lax.axis_size("zone") * CORES, lax.axis_size("row") * lax.axis_size("col"))
     total_qkv, total_output, total_time = pl.pallas_call(
-        functools.partial(finish_kernel, (lax.axis_size("zone") * CORES, lax.axis_size("row") * lax.axis_size("col"))),
-        out_shape=(
-            jax.ShapeDtypeStruct((width, 3 * width), jnp.float32),
-            jax.ShapeDtypeStruct((width, width), jnp.float32),
-            jax.ShapeDtypeStruct((CF, width), jnp.float32),
-        ),
-        in_specs=[smem, vmem, vmem],
-        out_specs=(vmem,) * 3,
-        compiler_params=pltpu.CompilerParams(vmem_limit_bytes=16 * 2**20),
-        name="finish",
-    )(place, mine, other)
+        functools.partial(mine_kernel, senders),
+        out_shape=gradients + (jax.ShapeDtypeStruct((CF, width), jnp.float32),),
+        in_specs=[smem, vmem],
+        out_specs=(anywhere, anywhere, vmem),
+        scratch_shapes=halves,
+        compiler_params=small,
+        cost_estimate=pl.CostEstimate(flops=200_000_000, bytes_accessed=1_500_000, transcendentals=2_000),
+        name="mine",
+    )(place, mine)
+    total_qkv, total_output = pl.pallas_call(
+        other_kernel,
+        out_shape=gradients,
+        in_specs=[smem, vmem, anywhere, anywhere],
+        out_specs=(anywhere, anywhere),
+        scratch_shapes=halves,
+        input_output_aliases={2: 0, 3: 1},
+        compiler_params=small,
+        cost_estimate=pl.CostEstimate(flops=200_000_000, bytes_accessed=1_000_000, transcendentals=0),
+        name="other",
+    )(place, other, total_qkv, total_output)
     return (result[None], grad_tokens[None], total_qkv, total_output, total_time)
 
 
@@ -567,12 +617,10 @@
 
 
 def summed(mine, other):
-    partner = [(0, 1), (1, 0)]
-    mine = total(jnp.stack([mine, lax.ppermute(other, "core", partner)]))
+    mine = total(jnp.stack([mine, lax.ppermute(other, "core", PARTNER)]))
     piece = total(swap(mine, "col"))
     piece = total(swap(copied(piece, ("zone", "row")), ("zone", "row")))
-    mine = swap(copied(piece, "col"), "col")
-    return mine, lax.ppermute(mine, "core", partner)
+    return swap(copied(piece, "col"), "col")
 
 
 def solution(mesh):

time: 98.7 us -> 99.2 us (level)
  blocking collectives: 52.2 us -> 34.8 us
  waiting for transfers between devices: 2.15 us -> 10.6 us
  starting transfers between devices: 28.2 us -> 35.8 us
  Pallas kernels: 11.1 us -> 12.1 us
    all_to_all x3 -> x2, blocking collectives: 52.2 us -> 34.8 us  [swap(): return lax.all_to_all(pieces, axes, 0, 0, tiled=True)]
    all_to_all x0 -> x1, waiting for transfers between devices: none -> 8.46 us  [swap(): return lax.all_to_all(pieces, axes, 0, 0, tiled=True)]
    all_to_all x0 -> x1, starting transfers between devices: none -> 7.6 us  [swap(): return lax.all_to_all(pieces, axes, 0, 0, tiled=True)]
    pallas_call x1 -> x2, Pallas kernels: 2.18 us -> 3.96 us  [the longest x1 2.59 us: on_device(): pl.pallas_call(functools.partial(mine_kernel, senders), out_shape=gradien...]
    pallas_call x0 -> x2, local copies, waits for them, and re-layouts: none -> 1.46 us  [on_device(): pl.pallas_call(functools.partial(right_kernel, starts[middle + 1:], total...]
    unnamed x12 -> x10, local copies, waits for them, and re-layouts: 1.5 us -> 0.03 us
  transfers between devices with their start and end apart: 6 -> 7, of which waited for: 3 -> 4; matrix products, arithmetic and copies ran while one was open for 2% -> 2% of each run, Pallas kernels for 5% -> 7%
where the time goes in v7:
time: 99.2 us; the launch traced here: 98.8 us
  starting transfers between devices  35.8 us (36%)
  blocking collectives  34.8 us (35%)
  Pallas kernels  12.1 us (12%)
  waiting for transfers between devices  10.6 us (11%)
  local copies, waits for them, and re-layouts  3.41 us (3%)
  between operations  1.57 us (2%)
    all_to_all x2, blocking collectives, swap(): return lax.all_to_all(pieces, axes, 0, 0, tiled=True)  34.8 us
    ppermute x2, starting transfers between devices, exchange(): from_previous = lax.ppermute(to_next, axis, forward)  9.58 us
    ppermute x1, starting transfers between devices, summed(): mine = total(jnp.stack([mine, lax.ppermute(other, 'core', PARTNER)]))  9.56 us
    all_to_all x1, waiting for transfers between devices, swap(): return lax.all_to_all(pieces, axes, 0, 0, tiled=True)  8.46 us
    all_to_all x1, starting transfers between devices, swap(): return lax.all_to_all(pieces, axes, 0, 0, tiled=True)  7.6 us
    ppermute x1, starting transfers between devices, on_device(): other = lax.ppermute(mine, 'core', PARTNER)  6.32 us
    pallas_call x1, Pallas kernels, on_device(): pl.pallas_call(functools.partial(right_kernel, starts[middle + 1:], total...  3.45 us
    ppermute x2, starting transfers between devices, exchange(): from_next = lax.ppermute(to_previous, axis, backward)  2.72 us
  transfers between devices with their start and end apart: 7, of which 4 were waited for; matrix products, arithmetic and copies ran while one was open for 2% of the time, Pallas kernels for 7%

profile of v7, /device:TPU:1, one launch (start us, length us, event | category | flops | bytes accessed | tf_op | source)
XLA Modules:
  0.0 98.8 jit_solution(10024140374724921199)
XLA Ops:
  0.6 0.0 copy-start
  0.6 0.9 slice_bitcast_fusion.2
  1.5 0.0 copy-start.3
  1.5 0.0 copy-start.4
  1.5 1.4 %collective-permute-start.1 = (bf16[16,8,256]{2,1,0:T(8,128)(2,1)S(1)}, bf16[16,8,256]{2,1,0:T(8,128)(2,1)S(1)}, u32[]{:S(2)}, u32[]{:S(2)}) collective-permute-start(bf16[16,8,256]{2,1,0:T(8,128)(2,1)S(1)} %pad_maximum_fusion.4), channel_id=1, source_target_pairs={{32,0},{64,32},{96,64},{33,1},{65,33},{97,65},{34,2},{66,34},{98,6... | collective-permute-start | bytes 196616 | tf_op jit(solution)/shard_map/ppermute | solution.py:37
  3.0 5.4 %collective-permute-start = (bf16[16,8,256]{2,1,0:T(8,128)(2,1)S(1)}, bf16[16,8,256]{2,1,0:T(8,128)(2,1)S(1)}, u32[]{:S(2)}, u32[]{:S(2)}) collective-permute-start(bf16[16,8,256]{2,1,0:T(8,128)(2,1)S(1)} %pad_maximum_fusion.3), channel_id=1, source_target_pairs={{0,32},{32,64},{64,96},{1,33},{33,65},{65,97},{2,34},{34,66},{66,9... | collective-permute-start | bytes 196616 | tf_op jit(solution)/shard_map/ppermute | solution.py:36
  8.4 0.0 copy-done.3
  8.5 0.0 copy-done.4
  8.5 0.1 copy_bitcast_fusion.2
  9.2 0.0 copy-done
  9.3 0.1 fusion.5
  9.4 0.1 stack.22.place_ref
  9.5 0.0 collective-permute-done.1
  9.6 0.2 collective-permute-done
  9.9 1.3 %collective-permute-start.2 = (bf16[9,48,256]{2,1,0:T(8,128)(2,1)S(1)}, bf16[9,48,256]{2,1,0:T(8,128)(2,1)S(1)}, u32[]{:S(2)}, u32[]{:S(2)}) collective-permute-start(bf16[9,48,256]{2,1,0:T(8,128)(2,1)S(1)} %pad_maximum_fusion.1), channel_id=1, source_target_pairs={{1,0},{2,1},{3,2},{4,3},{5,4},{6,5},{7,6},{8,7},{9,8},{10,9},{11,1... | collective-permute-start | bytes 663560 | tf_op jit(solution)/shard_map/ppermute | solution.py:37
  11.2 0.0 copy-start.1
  11.2 0.0 copy-start.2
  11.2 4.1 %collective-permute-start.3 = (bf16[9,48,256]{2,1,0:T(8,128)(2,1)S(1)}, bf16[9,48,256]{2,1,0:T(8,128)(2,1)S(1)}, u32[]{:S(2)}, u32[]{:S(2)}) collective-permute-start(bf16[9,48,256]{2,1,0:T(8,128)(2,1)S(1)} %pad_maximum_fusion.2), channel_id=1, source_target_pairs={{0,1},{1,2},{2,3},{3,4},{4,5},{5,6},{6,7},{7,8},{8,9},{9,10},{10,1... | collective-permute-start | bytes 663560 | tf_op jit(solution)/shard_map/ppermute | solution.py:36
  15.4 0.0 copy-done.1
  15.4 0.0 copy-done.2
  15.4 2.1 %own.1 = (bf16[8,48,256]{2,1,0:T(8,128)(2,1)S(1)}, bf16[8,48,256]{2,1,0:T(8,128)(2,1)S(1)}, bf16[8,48,256]{2,1,0:T(8,128)(2,1)S(1)}, bf16[8,48,256]{2,1,0:T(8,12...) custom-call(s32[5]{0:T(128)S(1)} %stack.22.place_ref, ...), custom_call_target="tpu_custom_call" | custom-call | flops 1000000000 | bytes 4000000 | tf_op jit(solution)/shard_map/own/pallas_call | solution.py:500
  17.5 0.7 collective-permute-done.3.side_ref
  18.2 2.6 %left.1 = (bf16[3,32,256]{2,1,0:T(8,128)(2,1)S(1)}, f32[3,32,256]{2,1,0:T(8,128)S(1)}, f32[8,32,256]{2,1,0:T(8,128)S(1)}, f32[8,32,256]{2,1,0:T(8,128)S(1)}) custom-call(s32[5]{0:T(128)S(1)} %stack.22.place_ref, bf16[9,48,256]{2,1,0:T(8,128)(2,1)S(1)} %collective-permute-done.3.side_ref, f32[1,256]{1,0:T(1,128)S(1)} %bitcast.47, ...), custom_call_target="tpu_custom_call" | custom-call | flops 2000000000 | bytes 2000000 | tf_op jit(solution)/shard_map/left/pallas_call | solution.py:518
  20.9 0.0 collective-permute-done.2.side_ref
  20.9 3.4 %right.1 = (bf16[8,32,256]{2,1,0:T(8,128)(2,1)S(1)}, bf16[8,32,256]{2,1,0:T(8,128)(2,1)S(1)}, bf16[32,40,128]{2,1,0:T(8,128)(2,1)S(1)}, bf16[32,40,128]{2,1,0:T(8,128)(2,1)S(1)}) custom-call(s32[5]{0:T(128)S(1)} %stack.22.place_ref, bf16[8,48,256]{2,1,0:T(8,128)(2,1)S(1)} %get-tuple-element.68.tok_ref, bf16[8,48,256]{2,1,0:T(8,128)(2,1)S(1)} %get-tuple-element.67.cot_ref, ...), custom_call_target="tpu_custom_call" | custom-call | flops 3000000000 | bytes 3000000 | tf_op jit(solution)/shard_map/right/pallas_call | solution.py:530
  24.3 9.6 %collective-permute-start.4 = (bf16[32,40,128]{2,1,0:T(8,128)(2,1)S(1)}, bf16[32,40,128]{2,1,0:T(8,128)(2,1)S(1)}, u32[]{:S(2)}, u32[]{:S(2)}) collective-permute-start(bf16[32,40,128]{2,1,0:T(8,128)(2,1)S(1)} %get-tuple-element.52), channel_id=1, source_target_pairs={{0,128},{128,0},{1,129},{129,1},{2,130},{130,2},{3,131},{131,3},{4... | collective-permute-start | bytes 983048 | tf_op jit(solution)/shard_map/ppermute | solution.py:620
  33.9 1.2 %collective-permute-done.4 = bf16[32,40,128]{2,1,0:T(8,128)(2,1)S(1)} collective-permute-done((bf16[32,40,128]{2,1,0:T(8,128)(2,1)S(1)}, bf16[32,40,128]{2,1,0:T(8,128)(2,1)S(1)}, u32[]{:S(2)}, u32[]{:S(2)}) %collective-permute-start.4) | collective-permute-done | bytes 327712 | tf_op jit(solution)/shard_map/ppermute | solution.py:620
  35.1 0.1 reduce_sum.34
  35.2 17.2 %all_to_all.15 = bf16[32,40,128]{2,1,0:T(8,128)(2,1)S(1)} all-to-all(bf16[32,40,128]{2,1,0:T(8,128)(2,1)S(1)} %reduce_sum.34), channel_id=1, replica_groups=mesh['zone'=2,'core'=2,'row'=4,'col'=32] {'col'}, dimensions={0} | all-to-all | bytes 655360 | tf_op jit(solution)/shard_map/all_to_all | solution.py:607
  52.4 0.1 reduce_sum.35
  52.5 17.7 %all_to_all.16 = bf16[8,40,128]{2,1,0:T(8,128)(2,1)S(1)} all-to-all(bf16[8,40,128]{2,1,0:T(8,128)(2,1)S(1)} %broadcast_in_dim.8), channel_id=1, replica_groups=mesh['zone'=2,'core'=2,'row'=4,'col'=32] {'zone','row'}, dimensions={0} | all-to-all | bytes 163840 | tf_op jit(solution)/shard_map/all_to_all | solution.py:607
  70.2 0.8 broadcast_in_dim.9
  70.9 7.6 %all-to-all-start.2 = ((bf16[32,40,128]{2,1,0:T(8,128)(2,1)}), bf16[32,40,128]{2,1,0:T(8,128)(2,1)S(1)}, u32[]{:S(2)}, u32[]{:S(2)}) async-start(bf16[32,40,128]{2,1,0:T(8,128)(2,1)} %broadcast_in_dim.9), calls=%async_computation.2 | async-start | bytes 655360 | tf_op jit(solution)/shard_map/all_to_all | solution.py:607
  78.6 0.7 copy.30
  79.3 0.7 copy.29
  80.0 8.5 %all-to-all-done.2.mine_ref = bf16[32,40,128]{2,1,0:T(8,128)(2,1)S(1)} async-done(((bf16[32,40,128]{2,1,0:T(8,128)(2,1)}), bf16[32,40,128]{2,1,0:T(8,128)(2,1)S(1)}, u32[]{:S(2)}, u32[]{:S(2)}) %all-to-all-start.2) | async-done | bytes 327712 | tf_op jit(solution)/shard_map/all_to_all | solution.py:607
  88.5 6.3 %collective-permute-start.5 = (bf16[32,40,128]{2,1,0:T(8,128)(2,1)S(1)}, bf16[32,40,128]{2,1,0:T(8,128)(2,1)S(1)}, u32[]{:S(2)}, u32[]{:S(2)}) collective-permute-start(bf16[32,40,128]{2,1,0:T(8,128)(2,1)S(1)} %all-to-all-done.2.mine_ref), channel_id=1, source_target_pairs={{0,128},{128,0},{1,129},{129,1},{2,130},{130,2},{3,131},{131,3},{4... | collective-permute-start | bytes 983048 | tf_op jit(solution)/shard_map/ppermute | solution.py:569
  94.8 2.6 %mine.1 = (f32[256,768]{1,0:T(8,128)}, f32[256,256]{1,0:T(8,128)}, f32[256,256]{1,0:T(8,128)}) custom-call(s32[5]{0:T(128)S(1)} %stack.22.place_ref, bf16[32,40,128]{2,1,0:T(8,128)(2,1)S(1)} %all-to-all-done.2.mine_ref), custom_call_target="tpu_custom_call" | custom-call | flops 200000000 | bytes 1500000 | tf_op jit(solution)/shard_map/mine/pallas_call | solution.py:582
  97.4 0.0 collective-permute-done.5.other_ref
  97.4 1.4 %other.1 = (f32[256,768]{1,0:T(8,128)}, f32[256,256]{1,0:T(8,128)}) custom-call(s32[5]{0:T(128)S(1)} %stack.22.place_ref, bf16[32,40,128]{2,1,0:T(8,128)(2,1)S(1)} %collective-permute-done.5.other_ref, f32[256,768]{1,0:T(8,128)} %get-tuple-element.58.qkv_in, f32[256,256]{1,0:T(8,128)} %get-tuple-element.59.output_in), custom_call_target="tpu_custom_call", output_to_operand_aliasing={{0}: (2, {}), {1}: (3, {})} | custom-call | flops 200000000 | bytes 1000000 | tf_op jit(solution)/shard_map/other/pallas_call | solution.py:592
  (15 shorter events, 0.3 us)
Async XLA Ops:
  0.6 8.6 %copy-start = (bf16[256,256]{1,0:T(8,128)(2,1)S(1)}, bf16[256,256]{1,0:T(8,128)(2,1)}, u32[]{:S(2)}) copy-start(bf16[256,256]{1,0:T(8,128)(2,1)} %param.11) | copy-start | bytes 393220
  1.5 6.9 %copy-start.3 = (bf16[1,32,8,256]{3,2,1,0:T(8,128)(2,1)S(1)}, bf16[1,32,8,256]{3,2,1,0:T(8,128)(2,1)}, u32[]{:S(2)}) copy-start(bf16[1,32,8,256]{3,2,1,0:T(8,128)(2,1)} %param.8) | copy-start | bytes 393220
  1.5 6.9 %copy-start.4 = (bf16[1,32,8,256]{3,2,1,0:T(8,128)(2,1)S(1)}, bf16[1,32,8,256]{3,2,1,0:T(8,128)(2,1)}, u32[]{:S(2)}) copy-start(bf16[1,32,8,256]{3,2,1,0:T(8,128)(2,1)} %param.6) | copy-start | bytes 393220
  1.5 8.0 %collective-permute-start.1 = (bf16[16,8,256]{2,1,0:T(8,128)(2,1)S(1)}, bf16[16,8,256]{2,1,0:T(8,128)(2,1)S(1)}, u32[]{:S(2)}, u32[]{:S(2)}) collective-permute-start(bf16[16,8,256]{2,1,0:T(8,128)(2,1)S(1)} %pad_maximum_fusion.4), channel_id=1, source_target_pairs={{32,0},{64,32},{96,64},{33,1},{65,33},{97,65},{34,2},{66,34},{98,6... | collective-permute-start | bytes 196616 | tf_op jit(solution)/shard_map/ppermute | solution.py:37
  3.0 6.8 %collective-permute-start = (bf16[16,8,256]{2,1,0:T(8,128)(2,1)S(1)}, bf16[16,8,256]{2,1,0:T(8,128)(2,1)S(1)}, u32[]{:S(2)}, u32[]{:S(2)}) collective-permute-start(bf16[16,8,256]{2,1,0:T(8,128)(2,1)S(1)} %pad_maximum_fusion.3), channel_id=1, source_target_pairs={{0,32},{32,64},{64,96},{1,33},{33,65},{65,97},{2,34},{34,66},{66,9... | collective-permute-start | bytes 196616 | tf_op jit(solution)/shard_map/ppermute | solution.py:36
  9.9 11.0 %collective-permute-start.2 = (bf16[9,48,256]{2,1,0:T(8,128)(2,1)S(1)}, bf16[9,48,256]{2,1,0:T(8,128)(2,1)S(1)}, u32[]{:S(2)}, u32[]{:S(2)}) collective-permute-start(bf16[9,48,256]{2,1,0:T(8,128)(2,1)S(1)} %pad_maximum_fusion.1), channel_id=1, source_target_pairs={{1,0},{2,1},{3,2},{4,3},{5,4},{6,5},{7,6},{8,7},{9,8},{10,9},{11,1... | collective-permute-start | bytes 663560 | tf_op jit(solution)/shard_map/ppermute | solution.py:37
  11.2 4.2 %copy-start.1 = (bf16[256,768]{1,0:T(8,128)(2,1)S(1)}, bf16[256,768]{1,0:T(8,128)(2,1)}, u32[]{:S(2)}) copy-start(bf16[256,768]{1,0:T(8,128)(2,1)} %qkv_ref.5) | copy-start | bytes 1179652
  11.2 4.2 %copy-start.2 = (bf16[256,256]{1,0:T(8,128)(2,1)S(1)}, bf16[256,256]{1,0:T(8,128)(2,1)}, u32[]{:S(2)}) copy-start(bf16[256,256]{1,0:T(8,128)(2,1)} %out_ref.5) | copy-start | bytes 393220
  11.2 7.0 %collective-permute-start.3 = (bf16[9,48,256]{2,1,0:T(8,128)(2,1)S(1)}, bf16[9,48,256]{2,1,0:T(8,128)(2,1)S(1)}, u32[]{:S(2)}, u32[]{:S(2)}) collective-permute-start(bf16[9,48,256]{2,1,0:T(8,128)(2,1)S(1)} %pad_maximum_fusion.2), channel_id=1, source_target_pairs={{0,1},{1,2},{2,3},{3,4},{4,5},{5,6},{6,7},{7,8},{8,9},{9,10},{10,1... | collective-permute-start | bytes 663560 | tf_op jit(solution)/shard_map/ppermute | solution.py:36
  24.3 10.8 %collective-permute-start.4 = (bf16[32,40,128]{2,1,0:T(8,128)(2,1)S(1)}, bf16[32,40,128]{2,1,0:T(8,128)(2,1)S(1)}, u32[]{:S(2)}, u32[]{:S(2)}) collective-permute-start(bf16[32,40,128]{2,1,0:T(8,128)(2,1)S(1)} %get-tuple-element.52), channel_id=1, source_target_pairs={{0,128},{128,0},{1,129},{129,1},{2,130},{130,2},{3,131},{131,3},{4... | collective-permute-start | bytes 983048 | tf_op jit(solution)/shard_map/ppermute | solution.py:620
  70.9 17.5 %all-to-all-start.2 = ((bf16[32,40,128]{2,1,0:T(8,128)(2,1)}), bf16[32,40,128]{2,1,0:T(8,128)(2,1)S(1)}, u32[]{:S(2)}, u32[]{:S(2)}) async-start(bf16[32,40,128]{2,1,0:T(8,128)(2,1)} %broadcast_in_dim.9), calls=%async_computation.2 | async-start | bytes 655360 | tf_op jit(solution)/shard_map/all_to_all | solution.py:607
  88.5 8.9 %collective-permute-start.5 = (bf16[32,40,128]{2,1,0:T(8,128)(2,1)S(1)}, bf16[32,40,128]{2,1,0:T(8,128)(2,1)S(1)}, u32[]{:S(2)}, u32[]{:S(2)}) collective-permute-start(bf16[32,40,128]{2,1,0:T(8,128)(2,1)S(1)} %all-to-all-done.2.mine_ref), channel_id=1, source_target_pairs={{0,128},{128,0},{1,129},{129,1},{2,130},{130,2},{3,131},{131,3},{4... | collective-permute-start | bytes 983048 | tf_op jit(solution)/shard_map/ppermute | solution.py:569

commit v8 on v7

--- a/solution.py
+++ b/solution.py
@@ -376,73 +376,71 @@
     across = 4 * width // LANES
     line = lax.broadcasted_iota(jnp.int32, (SLOT, LANES), 0)
     lane = lax.broadcasted_iota(jnp.int32, (SLOT, LANES), 1)
+    low_half, high_half = grad_adaptive[:, :LANES], grad_adaptive[:, LANES:]
+    adaptives = jnp.where(line == image, low_half, jnp.where(line == SLOT // 2 + image, high_half, 0.0))
     high = (step_value // 32).astype(jnp.float32)
     low = (step_value % 32).astype(jnp.float32)
+    steps = jnp.where(line == image, jnp.where(lane == 0, high, jnp.where(lane == 1, low, 0.0)), 0.0)
     for ref, which in ((mine_ref, core), (other_ref, 1 - core)):
         part = whole_ref[pl.ds(pl.multiple_of(which * half, half), half), :].astype(jnp.bfloat16)
-        for block in range(ref.shape[0]):
+        for block in range(half // LINES * across):
             top = block // across * LINES
             first = block % across * LANES
-            ref[block, :LINES] = part[top : top + LINES, first : first + LANES]
-            if block < width // LANES:
-                side = jnp.where(line == image, grad_adaptive[:, block * LANES : (block + 1) * LANES], 0.0)
-                if block == 0:
-                    there = line == SLOT // 2 + image
-                    side = jnp.where(there & (lane == 0), high, side)
-                    side = jnp.where(there & (lane == 1), low, side)
-                ref[block, LINES:] = side.astype(jnp.bfloat16)
-            else:
-                ref[block, LINES:] = jnp.zeros((SLOT, LANES), jnp.bfloat16)
-
-
-def half_gradients(which, half_ref, qkv_ref, output_ref, qkv_half, output_half, sems):
-    width = output_ref.shape[0]
+            ref[pl.ds(block_line(block), LINES), :] = part[top : top + LINES, first : first + LANES]
+            if block % 2 == 0:
+                side = adaptives if block == 0 else steps if block == 2 else jnp.zeros((SLOT, LANES), jnp.float32)
+                ref[pl.ds(block_line(block) + LINES, SLOT), :] = side.astype(jnp.bfloat16)
+
+
+def block_line(block):
+    return (2 * LINES + SLOT) * (block // 2) + (LINES + SLOT) * (block % 2)
+
+
+def finish_kernel(senders, place_ref, mine_ref, other_ref, qkv_ref, output_ref, time_ref, qkv, output, time, sems):
+    images, share = senders
+    width = output.shape[0]
     half = width // CORES
     across = 4 * width // LANES
-    for block in range(half_ref.shape[0]):
-        top = block // across * LINES
-        first = block % across * LANES
-        values = half_ref[block, :LINES].astype(jnp.float32)
-        if first < 3 * width:
-            qkv_half[top : top + LINES, first : first + LANES] = values
-        else:
-            output_half[top : top + LINES, first - 3 * width : first - 3 * width + LANES] = values
-    there = pl.ds(pl.multiple_of(which * half, half), half)
-    copies = (
-        pltpu.make_async_copy(qkv_half, qkv_ref.at[there], sems.at[0]),
-        pltpu.make_async_copy(output_half, output_ref.at[there], sems.at[1]),
-    )
-    for copy in copies:
-        copy.start()
-    return copies
-
-
-def mine_kernel(senders, place_ref, mine_ref, qkv_ref, output_ref, time_ref, qkv_half, output_half, sems):
-    images, share = senders
-    width = output_ref.shape[0]
-    copies = half_gradients(place_ref[3], mine_ref, qkv_ref, output_ref, qkv_half, output_half, sems)
-    sides = [mine_ref[block, LINES:].astype(jnp.float32) for block in range(width // LANES)]
-    adaptives = jnp.concatenate(sides, axis=1)
-    adaptives = jnp.where(lax.broadcasted_iota(jnp.int32, adaptives.shape, 0) < images, adaptives, 0.0)
+    core = place_ref[3]
+    copies = []
+
+    def send(source, target):
+        copies.append(pltpu.make_async_copy(source, target, sems.at[len(copies)]))
+        copies[-1].start()
+
+    for ref, which in ((mine_ref, core), (other_ref, 1 - core)):
+        for band in range(half // LINES):
+            there = pl.ds(pl.multiple_of(which * half + band * LINES, LINES), LINES)
+            for place in range(across):
+                values = ref[pl.ds(block_line(band * across + place), LINES), :].astype(jnp.float32)
+                first = place * LANES
+                if first < 3 * width:
+                    qkv[there, first : first + LANES] = values
+                else:
+                    output[there, first - 3 * width : first - 3 * width + LANES] = values
+            send(qkv.at[there], qkv_ref.at[there])
+        there = pl.ds(pl.multiple_of(which * half, half), half)
+        send(output.at[there], output_ref.at[there])
+    side = mine_ref[LINES : LINES + SLOT, :].astype(jnp.float32)
+    half_slot = SLOT // 2
+    adaptives = jnp.concatenate([side, jnp.concatenate([side[half_slot:], side[:half_slot]], axis=0)], axis=1)
+    line = lax.broadcasted_iota(jnp.int32, (SLOT, 1), 0)
+    adaptives = jnp.where(line < images, adaptives, 0.0)
+    steps = mine_ref[pl.ds(block_line(2) + LINES, SLOT), :].astype(jnp.float32)
+    steps = (steps[:, 0:1] * 32.0 + steps[:, 1:2]) / share
     ladder = lax.broadcasted_iota(jnp.int32, (1, CF // 2), 1).astype(jnp.float32)
     frequency = jnp.exp(ladder * (-math.log(1000.0) / (CF // 2)))
-    steps = (sides[0][:, 0:1] * 32.0 + sides[0][:, 1:2]) / share
-    steps = jnp.concatenate([steps[SLOT // 2 :], steps[: SLOT // 2] * 0.0], axis=0)
     angle = steps * frequency
     features = jnp.concatenate([jnp.cos(angle), jnp.sin(angle)], axis=1)
-    time_ref[...] = lax.dot_general(
+    time[...] = lax.dot_general(
         features,
         adaptives,
         (((0,), (0,)), ((), ())),
         precision=lax.Precision.HIGHEST,
         preferred_element_type=jnp.float32,
     )
+    send(time, time_ref)
     for copy in copies:
-        copy.wait()
-
-
-def other_kernel(place_ref, other_ref, qkv_in, output_in, qkv_ref, output_ref, qkv_half, output_half, sems):
-    for copy in half_gradients(1 - place_ref[3], other_ref, qkv_ref, output_ref, qkv_half, output_half, sems):
         copy.wait()
 
 
@@ -526,7 +524,7 @@
         name="left",
     )(place, left, adaptive, qkv_weight, output_weight, *own, mask, grad_key, grad_value)
     pieces = width // CORES // LINES * (4 * width // LANES)
-    chunks = jax.ShapeDtypeStruct((pieces, LINES + SLOT, LANES), jnp.bfloat16)
+    chunks = jax.ShapeDtypeStruct((pieces * (LINES + SLOT // 2), LANES), jnp.bfloat16)
     result, grad_tokens, mine, other = pl.pallas_call(
         functools.partial(right_kernel, starts[middle + 1 :], total_cols),
         out_shape=(block, block, chunks, chunks),
@@ -561,45 +559,24 @@
         grad_query,
         *from_left,
     )
-    result = lying(result.transpose(1, 0, 2))
-    grad_tokens = lying(grad_tokens.transpose(1, 0, 2))
-
+    result = result.transpose(1, 0, 2)
+    grad_tokens = grad_tokens.transpose(1, 0, 2)
     mine = summed(mine, other)
-    mine, result, grad_tokens = lax.optimization_barrier((mine, result, grad_tokens))
     other = lax.ppermute(mine, "core", PARTNER)
     anywhere = pl.BlockSpec(memory_space=pl.ANY)
-    gradients = (
-        jax.ShapeDtypeStruct((width, 3 * width), jnp.float32),
-        jax.ShapeDtypeStruct((width, width), jnp.float32),
-    )
-    halves = [
-        pltpu.VMEM((width // CORES, 3 * width), jnp.float32),
-        pltpu.VMEM((width // CORES, width), jnp.float32),
-        pltpu.SemaphoreType.DMA((2,)),
-    ]
-    small = pltpu.CompilerParams(vmem_limit_bytes=8 * 2**20)
+    gradients = ((width, 3 * width), (width, width), (CF, width))
     senders = (lax.axis_size("zone") * CORES, lax.axis_size("row") * lax.axis_size("col"))
     total_qkv, total_output, total_time = pl.pallas_call(
-        functools.partial(mine_kernel, senders),
-        out_shape=gradients + (jax.ShapeDtypeStruct((CF, width), jnp.float32),),
-        in_specs=[smem, vmem],
-        out_specs=(anywhere, anywhere, vmem),
-        scratch_shapes=halves,
-        compiler_params=small,
-        cost_estimate=pl.CostEstimate(flops=200_000_000, bytes_accessed=1_500_000, transcendentals=2_000),
-        name="mine",
-    )(place, mine)
-    total_qkv, total_output = pl.pallas_call(
-        other_kernel,
-        out_shape=gradients,
-        in_specs=[smem, vmem, anywhere, anywhere],
-        out_specs=(anywhere, anywhere),
-        scratch_shapes=halves,
-        input_output_aliases={2: 0, 3: 1},
-        compiler_params=small,
-        cost_estimate=pl.CostEstimate(flops=200_000_000, bytes_accessed=1_000_000, transcendentals=0),
-        name="other",
-    )(place, other, total_qkv, total_output)
+        functools.partial(finish_kernel, senders),
+        out_shape=tuple(jax.ShapeDtypeStruct(shape, jnp.float32) for shape in gradients),
+        in_specs=[smem, vmem, vmem],
+        out_specs=(anywhere,) * 3,
+        scratch_shapes=[pltpu.VMEM(shape, jnp.float32) for shape in gradients]
+        + [pltpu.SemaphoreType.DMA((CORES * (width // CORES // LINES + 1) + 1,))],
+        compiler_params=pltpu.CompilerParams(vmem_limit_bytes=16 * 2**20),
+        cost_estimate=pl.CostEstimate(flops=200_000_000, bytes_accessed=2_000_000, transcendentals=2_000),
+        name="finish",
+    )(place, mine, other)
     return (result[None], grad_tokens[None], total_qkv, total_output, total_time)
 
 
@@ -618,9 +595,11 @@
 
 def summed(mine, other):
     mine = total(jnp.stack([mine, lax.ppermute(other, "core", PARTNER)]))
-    piece = total(swap(mine, "col"))
+    parts = lax.axis_size("col")
+    pieces = mine.reshape(parts, mine.shape[0] // parts // 4, 4, LANES)
+    piece = total(swap(pieces, "col"))
     piece = total(swap(copied(piece, ("zone", "row")), ("zone", "row")))
-    return swap(copied(piece, "col"), "col")
+    return swap(copied(piece, "col"), "col").reshape(mine.shape)
 
 
 def solution(mesh):

time: 99.2 us -> 97.7 us (0.985)
  blocking collectives: 34.8 us -> 51.1 us
  waiting for transfers between devices: 10.6 us -> 2.1 us
  starting transfers between devices: 35.8 us -> 29 us
  Pallas kernels: 12.1 us -> 10.3 us
    all_to_all x2 -> x3, blocking collectives: 34.8 us -> 51.1 us  [swap(): return lax.all_to_all(pieces, axes, 0, 0, tiled=True)]
    all_to_all x1 -> x0, waiting for transfers between devices: 8.46 us -> none  [swap(): return lax.all_to_all(pieces, axes, 0, 0, tiled=True)]
    all_to_all x1 -> x0, starting transfers between devices: 7.6 us -> none  [swap(): return lax.all_to_all(pieces, axes, 0, 0, tiled=True)]
    pallas_call x2 -> x1, Pallas kernels: 3.96 us -> 2.16 us  [on_device(): pl.pallas_call(functools.partial(finish_kernel, senders), out_shape=tuple...]
    unnamed x10 -> x12, local copies, waits for them, and re-layouts: 0.03 us -> 1.5 us
    pallas_call x2 -> x0, local copies, waits for them, and re-layouts: 1.46 us -> none  [on_device(): pl.pallas_call(functools.partial(right_kernel, starts[middle + 1:], total...]
  transfers between devices with their start and end apart: 7 -> 6, of which waited for: 4 -> 3; matrix products, arithmetic and copies ran while one was open for 2% -> 2% of each run, Pallas kernels for 7% -> 5%
where the time goes in v8:
time: 97.7 us; the launch traced here: 97.3 us
  blocking collectives  51.1 us (52%)
  starting transfers between devices  29 us (30%)
  Pallas kernels  10.3 us (11%)
  local copies, waits for them, and re-layouts  2.73 us (3%)
  waiting for transfers between devices  2.1 us (2%)
  between operations  1.55 us (2%)
    all_to_all x3, blocking collectives, swap(): return lax.all_to_all(pieces, axes, 0, 0, tiled=True)  51.1 us
    ppermute x2, starting transfers between devices, exchange(): from_previous = lax.ppermute(to_next, axis, forward)  9.58 us
    ppermute x1, starting transfers between devices, summed(): mine = total(jnp.stack([mine, lax.ppermute(other, 'core', PARTNER)]))  9.56 us
    ppermute x1, starting transfers between devices, on_device(): other = lax.ppermute(mine, 'core', PARTNER)  7.16 us
    pallas_call x1, Pallas kernels, on_device(): pl.pallas_call(functools.partial(right_kernel, starts[middle + 1:], total...  3.41 us
    ppermute x2, starting transfers between devices, exchange(): from_next = lax.ppermute(to_previous, axis, backward)  2.72 us
    pallas_call x1, Pallas kernels, on_device(): pl.pallas_call(functools.partial(left_kernel, starts[:middle], total_cols...  2.62 us
    pallas_call x1, Pallas kernels, on_device(): pl.pallas_call(functools.partial(finish_kernel, senders), out_shape=tuple...  2.16 us
  transfers between devices with their start and end apart: 6, of which 3 were waited for; matrix products, arithmetic and copies ran while one was open for 2% of the time, Pallas kernels for 5%

profile of v8, /device:TPU:1, one launch (start us, length us, event | category | flops | bytes accessed | tf_op | source)
XLA Modules:
  0.0 97.3 jit_solution(16224287579326849753)
XLA Ops:
  0.6 0.0 copy-start
  0.6 0.9 slice_bitcast_fusion.2
  1.5 0.0 copy-start.3
  1.5 0.0 copy-start.4
  1.5 1.4 %collective-permute-start.1 = (bf16[16,8,256]{2,1,0:T(8,128)(2,1)S(1)}, bf16[16,8,256]{2,1,0:T(8,128)(2,1)S(1)}, u32[]{:S(2)}, u32[]{:S(2)}) collective-permute-start(bf16[16,8,256]{2,1,0:T(8,128)(2,1)S(1)} %pad_maximum_fusion.4), channel_id=1, source_target_pairs={{32,0},{64,32},{96,64},{33,1},{65,33},{97,65},{34,2},{66,34},{98,6... | collective-permute-start | bytes 196616 | tf_op jit(solution)/shard_map/ppermute | solution.py:37
  3.0 5.4 %collective-permute-start = (bf16[16,8,256]{2,1,0:T(8,128)(2,1)S(1)}, bf16[16,8,256]{2,1,0:T(8,128)(2,1)S(1)}, u32[]{:S(2)}, u32[]{:S(2)}) collective-permute-start(bf16[16,8,256]{2,1,0:T(8,128)(2,1)S(1)} %pad_maximum_fusion.3), channel_id=1, source_target_pairs={{0,32},{32,64},{64,96},{1,33},{33,65},{65,97},{2,34},{34,66},{66,9... | collective-permute-start | bytes 196616 | tf_op jit(solution)/shard_map/ppermute | solution.py:36
  8.4 0.0 copy-done.3
  8.5 0.0 copy-done.4
  8.5 0.1 copy_bitcast_fusion
  9.2 0.0 copy-done
  9.3 0.1 fusion.5
  9.4 0.1 stack.22.place_ref
  9.5 0.0 collective-permute-done.1
  9.6 0.2 collective-permute-done
  9.9 1.3 %collective-permute-start.2 = (bf16[9,48,256]{2,1,0:T(8,128)(2,1)S(1)}, bf16[9,48,256]{2,1,0:T(8,128)(2,1)S(1)}, u32[]{:S(2)}, u32[]{:S(2)}) collective-permute-start(bf16[9,48,256]{2,1,0:T(8,128)(2,1)S(1)} %pad_maximum_fusion.1), channel_id=1, source_target_pairs={{1,0},{2,1},{3,2},{4,3},{5,4},{6,5},{7,6},{8,7},{9,8},{10,9},{11,1... | collective-permute-start | bytes 663560 | tf_op jit(solution)/shard_map/ppermute | solution.py:37
  11.2 0.0 copy-start.1
  11.2 0.0 copy-start.2
  11.2 4.1 %collective-permute-start.3 = (bf16[9,48,256]{2,1,0:T(8,128)(2,1)S(1)}, bf16[9,48,256]{2,1,0:T(8,128)(2,1)S(1)}, u32[]{:S(2)}, u32[]{:S(2)}) collective-permute-start(bf16[9,48,256]{2,1,0:T(8,128)(2,1)S(1)} %pad_maximum_fusion.2), channel_id=1, source_target_pairs={{0,1},{1,2},{2,3},{3,4},{4,5},{5,6},{6,7},{7,8},{8,9},{9,10},{10,1... | collective-permute-start | bytes 663560 | tf_op jit(solution)/shard_map/ppermute | solution.py:36
  15.4 0.0 copy-done.1
  15.4 0.0 copy-done.2
  15.4 2.1 %own.1 = (bf16[8,48,256]{2,1,0:T(8,128)(2,1)S(1)}, bf16[8,48,256]{2,1,0:T(8,128)(2,1)S(1)}, bf16[8,48,256]{2,1,0:T(8,128)(2,1)S(1)}, bf16[8,48,256]{2,1,0:T(8,12...) custom-call(s32[5]{0:T(128)S(1)} %stack.22.place_ref, ...), custom_call_target="tpu_custom_call" | custom-call | flops 1000000000 | bytes 4000000 | tf_op jit(solution)/shard_map/own/pallas_call | solution.py:498
  17.5 0.7 collective-permute-done.3.side_ref
  18.2 2.6 %left.1 = (bf16[3,32,256]{2,1,0:T(8,128)(2,1)S(1)}, f32[3,32,256]{2,1,0:T(8,128)S(1)}, f32[8,32,256]{2,1,0:T(8,128)S(1)}, f32[8,32,256]{2,1,0:T(8,128)S(1)}) custom-call(s32[5]{0:T(128)S(1)} %stack.22.place_ref, bf16[9,48,256]{2,1,0:T(8,128)(2,1)S(1)} %collective-permute-done.3.side_ref, f32[1,256]{1,0:T(1,128)S(1)} %bitcast.51, ...), custom_call_target="tpu_custom_call" | custom-call | flops 2000000000 | bytes 2000000 | tf_op jit(solution)/shard_map/left/pallas_call | solution.py:516
  20.9 0.0 collective-permute-done.2.side_ref
  20.9 3.4 %right.1 = (bf16[8,32,256]{2,1,0:T(8,128)(2,1)S(1)}, bf16[8,32,256]{2,1,0:T(8,128)(2,1)S(1)}, bf16[1152,128]{1,0:T(8,128)(2,1)S(1)}, bf16[1152,128]{1,0:T(8,128)(2,1)S(1)}) custom-call(s32[5]{0:T(128)S(1)} %stack.22.place_ref, bf16[8,48,256]{2,1,0:T(8,128)(2,1)S(1)} %get-tuple-element.73.tok_ref, bf16[8,48,256]{2,1,0:T(8,128)(2,1)S(1)} %get-tuple-element.72.cot_ref, ...), custom_call_target="tpu_custom_call" | custom-call | flops 3000000000 | bytes 3000000 | tf_op jit(solution)/shard_map/right/pallas_call | solution.py:528
  24.3 9.6 %collective-permute-start.4 = (bf16[1152,128]{1,0:T(8,128)(2,1)S(1)}, bf16[1152,128]{1,0:T(8,128)(2,1)S(1)}, u32[]{:S(2)}, u32[]{:S(2)}) collective-permute-start(bf16[1152,128]{1,0:T(8,128)(2,1)S(1)} %get-tuple-element.49), channel_id=1, source_target_pairs={{0,128},{128,0},{1,129},{129,1},{2,130},{130,2},{3,131},{131,3},{4... | collective-permute-start | bytes 884744 | tf_op jit(solution)/shard_map/ppermute | solution.py:597
  33.9 1.2 %collective-permute-done.4 = bf16[1152,128]{1,0:T(8,128)(2,1)S(1)} collective-permute-done((bf16[1152,128]{1,0:T(8,128)(2,1)S(1)}, bf16[1152,128]{1,0:T(8,128)(2,1)S(1)}, u32[]{:S(2)}, u32[]{:S(2)}) %collective-permute-start.4) | collective-permute-done | bytes 294944 | tf_op jit(solution)/shard_map/ppermute | solution.py:597
  35.0 0.1 reduce_sum.34
  35.1 16.9 %all_to_all.15 = bf16[32,9,4,128]{3,2,1,0:T(4,128)(2,1)S(1)} all-to-all(bf16[32,9,4,128]{3,2,1,0:T(4,128)(2,1)S(1)} %bitcast.53), channel_id=1, replica_groups=mesh['zone'=2,'core'=2,'row'=4,'col'=32] {'col'}, dimensions={0} | all-to-all | bytes 589824 | tf_op jit(solution)/shard_map/all_to_all | solution.py:584
  52.0 0.1 reduce_sum.35
  52.2 17.6 %all_to_all.16 = bf16[8,9,4,128]{3,2,1,0:T(4,128)(2,1)S(1)} all-to-all(bf16[8,9,4,128]{3,2,1,0:T(4,128)(2,1)S(1)} %broadcast_in_dim.10), channel_id=1, replica_groups=mesh['zone'=2,'core'=2,'row'=4,'col'=32] {'zone','row'}, dimensions={0} | all-to-all | bytes 147456 | tf_op jit(solution)/shard_map/all_to_all | solution.py:584
  69.8 0.1 broadcast_in_dim.22
  69.9 16.6 %all_to_all.17 = bf16[32,9,4,128]{3,2,1,0:T(4,128)(2,1)S(1)} all-to-all(bf16[32,9,4,128]{3,2,1,0:T(4,128)(2,1)S(1)} %broadcast_in_dim.22), channel_id=1, replica_groups=mesh['zone'=2,'core'=2,'row'=4,'col'=32] {'col'}, dimensions={0} | all-to-all | bytes 589824 | tf_op jit(solution)/shard_map/all_to_all | solution.py:584
  86.5 7.2 %collective-permute-start.5 = (bf16[1152,128]{1,0:T(8,128)(2,1)S(1)}, bf16[1152,128]{1,0:T(8,128)(2,1)S(1)}, u32[]{:S(2)}, u32[]{:S(2)}) collective-permute-start(bf16[1152,128]{1,0:T(8,128)(2,1)S(1)} %bitcast.46), channel_id=1, source_target_pairs={{0,128},{128,0},{1,129},{129,1},{2,130},{130,2},{3,131},{131,3},{4... | collective-permute-start | bytes 884744 | tf_op jit(solution)/shard_map/ppermute | solution.py:565
  93.7 0.7 copy.28
  94.4 0.7 copy.29
  95.2 0.0 collective-permute-done.5.other_ref
  95.2 2.2 %finish.1 = (f32[256,768]{1,0:T(8,128)}, f32[256,256]{1,0:T(8,128)}, f32[256,256]{1,0:T(8,128)}) custom-call(s32[5]{0:T(128)S(1)} %stack.22.place_ref, bf16[1152,128]{1,0:T(8,128)(2,1)S(1)} %bitcast.47, bf16[1152,128]{1,0:T(8,128)(2,1)S(1)} %collective-permute-done.5.other_ref), custom_call_target="tpu_custom_call" | custom-call | flops 200000000 | bytes 2000000 | tf_op jit(solution)/shard_map/finish/pallas_call | solution.py:569
  (15 shorter events, 0.3 us)
Async XLA Ops:
  0.6 8.6 %copy-start = (bf16[256,256]{1,0:T(8,128)(2,1)S(1)}, bf16[256,256]{1,0:T(8,128)(2,1)}, u32[]{:S(2)}) copy-start(bf16[256,256]{1,0:T(8,128)(2,1)} %param.11) | copy-start | bytes 393220
  1.5 6.9 %copy-start.3 = (bf16[1,32,8,256]{3,2,1,0:T(8,128)(2,1)S(1)}, bf16[1,32,8,256]{3,2,1,0:T(8,128)(2,1)}, u32[]{:S(2)}) copy-start(bf16[1,32,8,256]{3,2,1,0:T(8,128)(2,1)} %param.8) | copy-start | bytes 393220
  1.5 6.9 %copy-start.4 = (bf16[1,32,8,256]{3,2,1,0:T(8,128)(2,1)S(1)}, bf16[1,32,8,256]{3,2,1,0:T(8,128)(2,1)}, u32[]{:S(2)}) copy-start(bf16[1,32,8,256]{3,2,1,0:T(8,128)(2,1)} %param.6) | copy-start | bytes 393220
  1.5 8.0 %collective-permute-start.1 = (bf16[16,8,256]{2,1,0:T(8,128)(2,1)S(1)}, bf16[16,8,256]{2,1,0:T(8,128)(2,1)S(1)}, u32[]{:S(2)}, u32[]{:S(2)}) collective-permute-start(bf16[16,8,256]{2,1,0:T(8,128)(2,1)S(1)} %pad_maximum_fusion.4), channel_id=1, source_target_pairs={{32,0},{64,32},{96,64},{33,1},{65,33},{97,65},{34,2},{66,34},{98,6... | collective-permute-start | bytes 196616 | tf_op jit(solution)/shard_map/ppermute | solution.py:37
  3.0 6.8 %collective-permute-start = (bf16[16,8,256]{2,1,0:T(8,128)(2,1)S(1)}, bf16[16,8,256]{2,1,0:T(8,128)(2,1)S(1)}, u32[]{:S(2)}, u32[]{:S(2)}) collective-permute-start(bf16[16,8,256]{2,1,0:T(8,128)(2,1)S(1)} %pad_maximum_fusion.3), channel_id=1, source_target_pairs={{0,32},{32,64},{64,96},{1,33},{33,65},{65,97},{2,34},{34,66},{66,9... | collective-permute-start | bytes 196616 | tf_op jit(solution)/shard_map/ppermute | solution.py:36
  9.9 11.0 %collective-permute-start.2 = (bf16[9,48,256]{2,1,0:T(8,128)(2,1)S(1)}, bf16[9,48,256]{2,1,0:T(8,128)(2,1)S(1)}, u32[]{:S(2)}, u32[]{:S(2)}) collective-permute-start(bf16[9,48,256]{2,1,0:T(8,128)(2,1)S(1)} %pad_maximum_fusion.1), channel_id=1, source_target_pairs={{1,0},{2,1},{3,2},{4,3},{5,4},{6,5},{7,6},{8,7},{9,8},{10,9},{11,1... | collective-permute-start | bytes 663560 | tf_op jit(solution)/shard_map/ppermute | solution.py:37
  11.2 4.2 %copy-start.1 = (bf16[256,768]{1,0:T(8,128)(2,1)S(1)}, bf16[256,768]{1,0:T(8,128)(2,1)}, u32[]{:S(2)}) copy-start(bf16[256,768]{1,0:T(8,128)(2,1)} %qkv_ref.5) | copy-start | bytes 1179652
  11.2 4.2 %copy-start.2 = (bf16[256,256]{1,0:T(8,128)(2,1)S(1)}, bf16[256,256]{1,0:T(8,128)(2,1)}, u32[]{:S(2)}) copy-start(bf16[256,256]{1,0:T(8,128)(2,1)} %out_ref.5) | copy-start | bytes 393220
  11.2 7.0 %collective-permute-start.3 = (bf16[9,48,256]{2,1,0:T(8,128)(2,1)S(1)}, bf16[9,48,256]{2,1,0:T(8,128)(2,1)S(1)}, u32[]{:S(2)}, u32[]{:S(2)}) collective-permute-start(bf16[9,48,256]{2,1,0:T(8,128)(2,1)S(1)} %pad_maximum_fusion.2), channel_id=1, source_target_pairs={{0,1},{1,2},{2,3},{3,4},{4,5},{5,6},{6,7},{7,8},{8,9},{9,10},{10,1... | collective-permute-start | bytes 663560 | tf_op jit(solution)/shard_map/ppermute | solution.py:36
  24.3 10.8 %collective-permute-start.4 = (bf16[1152,128]{1,0:T(8,128)(2,1)S(1)}, bf16[1152,128]{1,0:T(8,128)(2,1)S(1)}, u32[]{:S(2)}, u32[]{:S(2)}) collective-permute-start(bf16[1152,128]{1,0:T(8,128)(2,1)S(1)} %get-tuple-element.49), channel_id=1, source_target_pairs={{0,128},{128,0},{1,129},{129,1},{2,130},{130,2},{3,131},{131,3},{4... | collective-permute-start | bytes 884744 | tf_op jit(solution)/shard_map/ppermute | solution.py:597
  86.5 8.6 %collective-permute-start.5 = (bf16[1152,128]{1,0:T(8,128)(2,1)S(1)}, bf16[1152,128]{1,0:T(8,128)(2,1)S(1)}, u32[]{:S(2)}, u32[]{:S(2)}) collective-permute-start(bf16[1152,128]{1,0:T(8,128)(2,1)S(1)} %bitcast.46), channel_id=1, source_target_pairs={{0,128},{128,0},{1,129},{129,1},{2,130},{130,2},{3,131},{131,3},{4... | collective-permute-start | bytes 884744 | tf_op jit(solution)/shard_map/ppermute | solution.py:565

commit v9 on v8

--- a/solution.py
+++ b/solution.py
@@ -119,7 +119,7 @@
     return attended, grad_query, nn(kept(grad_score), queries).reshape(shape), nn(kept(weights), grads).reshape(shape)
 
 
-def own_kernel(
+def early_kernel(
     total_rows,
     place_ref,
     tok_ref,
@@ -136,25 +136,18 @@
     query_inv_ref,
     key_raw_ref,
     key_inv_ref,
-    attended_ref,
-    grad_query_ref,
-    grad_key_ref,
-    grad_value_ref,
 ):
-    cols, rows, width = tok_ref.shape
-    lanes = mask_ref.shape[2]
-    height = rows - 2 * EDGE
+    shape = tok_ref.shape
+    cols, height, width = shape
+    _, rows, lanes = mask_ref.shape
     row_first = place_ref[0]
-    pixels = tok_ref[...].astype(jnp.float32).reshape(cols * rows, width)
+    pixels = tok_ref[...].astype(jnp.float32).reshape(cols * height, width)
     _, _, query, key, value, raw = projected(pixels, adaptive_ref[...], qkv_ref, average_matrix(width))
-    query = query.astype(jnp.bfloat16)
-    key = key.astype(jnp.bfloat16)
-    value = value.astype(jnp.bfloat16)
-    grad = nt(cot_ref[...].reshape(cols * rows, width), out_ref[...]).astype(jnp.bfloat16)
+    grad = nt(cot_ref[...].reshape(cols * height, width), out_ref[...])
     for ref, values in ((query_ref, query), (key_ref, key), (value_ref, value), (grad_ref, grad)):
-        ref[...] = values.reshape(cols, rows, width)
+        ref[...] = values.astype(jnp.bfloat16).reshape(shape)
     for ref, values in zip((query_raw_ref, query_inv_ref, key_raw_ref, key_inv_ref), raw):
-        ref[...] = values.reshape(cols, rows, width)[:, :height]
+        ref[...] = values.reshape(shape)
 
     def row_at(position):
         halo = jnp.where(position < height + EDGE, position - height - EDGE, position - EDGE)
@@ -170,12 +163,46 @@
     image_row = jnp.broadcast_to(row_first + key_row, row_gap.shape)
     near_row = (row_gap >= -RADIUS) & (row_gap <= RADIUS) & (image_row >= 0) & (image_row < total_rows)
     near_col = (col_gap >= 0) & (col_gap <= REACH)
-    mask = jnp.where(near_row, 1.0, 0.0) * jnp.where(near_col, 1.0, 0.0)
-    mask_ref[...] = mask
-
-    pair = slice(RADIUS * rows, (RADIUS + SPAN) * rows)
-    queries, grads = spread(query[pair]), spread(grad[pair])
-    weights, grad_score = soften(nt(key, queries), nt(value, grads), mask.reshape(cols * rows, lanes))
+    mask_ref[...] = jnp.where(near_row, 1.0, 0.0) * jnp.where(near_col, 1.0, 0.0)
+
+
+def own_kernel(
+    tok_ref,
+    cot_ref,
+    adaptive_ref,
+    qkv_ref,
+    out_ref,
+    early_query_ref,
+    early_key_ref,
+    early_value_ref,
+    early_grad_ref,
+    mask_ref,
+    query_ref,
+    key_ref,
+    value_ref,
+    grad_ref,
+    attended_ref,
+    grad_query_ref,
+    grad_key_ref,
+    grad_value_ref,
+):
+    cols, rows, width = tok_ref.shape
+    lanes = mask_ref.shape[2]
+    height = rows - 2 * EDGE
+    pixels = tok_ref[:, height:].astype(jnp.float32).reshape(cols * 2 * EDGE, width)
+    _, _, query, key, value, _ = projected(pixels, adaptive_ref[...], qkv_ref, average_matrix(width))
+    grad = nt(cot_ref[:, height:].reshape(cols * 2 * EDGE, width), out_ref[...])
+    early = (early_query_ref, early_key_ref, early_value_ref, early_grad_ref)
+    blocks = (query_ref, key_ref, value_ref, grad_ref)
+    for ref, source, values in zip(blocks, early, (query, key, value, grad)):
+        ref[:, :height] = source[...]
+        ref[:, height:] = values.astype(jnp.bfloat16).reshape(cols, 2 * EDGE, width)
+
+    key, value = (ref[...].reshape(cols * rows, width) for ref in (key_ref, value_ref))
+    pair = pl.ds(RADIUS, SPAN)
+    queries, grads = (spread(ref[pair].reshape(SPAN * rows, width)) for ref in (query_ref, grad_ref))
+    mask = mask_ref[...].reshape(cols * rows, lanes)
+    weights, grad_score = soften(nt(key, queries), nt(value, grads), mask)
     attended_ref[...], grad_query_ref[...], grad_key_ref[...], grad_value_ref[...] = combined(
         weights, grad_score, key, value, queries, grads, rows, height, True, 0, cols
     )
@@ -472,6 +499,7 @@
     above, below = (rows_.transpose(1, 0, 2, 3).reshape(2 * cols, EDGE, width) for rows_ in (above, below))
     both = jnp.concatenate([both, above, below], axis=1)
     tok, cot = both[:cols], both[cols:]
+    early_tok, early_cot = tokens[0].transpose(1, 0, 2), cotangent[0].transpose(1, 0, 2)
     to_next = jnp.concatenate([tok[cols - REACH :], cot[cols - RADIUS :]], axis=0)
     to_previous = jnp.concatenate([tok[:REACH], cot[:RADIUS]], axis=0)
     left, right = exchange(to_next, to_previous, "col")
@@ -495,16 +523,24 @@
         jax.ShapeDtypeStruct((SPAN, height, width), jnp.bfloat16),
         jax.ShapeDtypeStruct((SPAN, height, width), jnp.float32),
     )
-    prepared = pl.pallas_call(
-        functools.partial(own_kernel, total_rows),
-        out_shape=(tall,) * 4 + (masked,) + (exact,) * 4 + pair + (exact,) * 2,
+    *early, mask, query_raw, query_inv, key_raw, key_inv = pl.pallas_call(
+        functools.partial(early_kernel, total_rows),
+        out_shape=(block,) * 4 + (masked,) + (exact,) * 4,
         in_specs=[smem] + [vmem] * 5,
-        out_specs=(vmem,) * 13,
+        out_specs=(vmem,) * 9,
         compiler_params=limits,
-        cost_estimate=pl.CostEstimate(flops=1_000_000_000, bytes_accessed=4_000_000, transcendentals=200_000),
+        cost_estimate=pl.CostEstimate(flops=700_000_000, bytes_accessed=3_000_000, transcendentals=200_000),
+        name="early",
+    )(place, early_tok, early_cot, adaptive, qkv_weight, output_weight)
+    *own, attended, grad_query, grad_key, grad_value = pl.pallas_call(
+        own_kernel,
+        out_shape=(tall,) * 4 + pair + (exact,) * 2,
+        in_specs=[vmem] * 10,
+        out_specs=(vmem,) * 8,
+        compiler_params=limits,
+        cost_estimate=pl.CostEstimate(flops=1_000_000_000, bytes_accessed=3_000_000, transcendentals=200_000),
         name="own",
-    )(place, tok, cot, adaptive, qkv_weight, output_weight)
-    *own, mask, query_raw, query_inv, key_raw, key_inv, attended, grad_query, grad_key, grad_value = prepared
+    )(tok, cot, adaptive, qkv_weight, output_weight, *early, mask)
     starts = tuple(range(0, cols + REACH, SPAN))
     middle = starts.index(REACH)
     third = (cols - SPAN) // 2

time: 97.7 us -> 97.8 us (level)
    pallas_call x1 -> x2, Pallas kernels: 2.09 us -> 2.62 us  [the longest x1 1.42 us: on_device(): pl.pallas_call(own_kernel, out_shape=(tall,) * 4 + pair + (exact,) * 2, i...]
  transfers between devices with their start and end apart: 6 -> 6, of which waited for: 3 -> 2; matrix products, arithmetic and copies ran while one was open for 2% -> 2% of each run, Pallas kernels for 5% -> 5%
where the time goes in v9:
time: 97.8 us; the launch traced here: 97.4 us
  blocking collectives  50.6 us (52%)
  starting transfers between devices  28.4 us (29%)
  Pallas kernels  10.9 us (11%)
  local copies, waits for them, and re-layouts  2.72 us (3%)
  waiting for transfers between devices  2.59 us (3%)
  between operations  1.6 us (2%)
    all_to_all x3, blocking collectives, swap(): return lax.all_to_all(pieces, axes, 0, 0, tiled=True)  50.6 us
    ppermute x2, starting transfers between devices, exchange(): from_previous = lax.ppermute(to_next, axis, forward)  9.58 us
    ppermute x1, starting transfers between devices, summed(): mine = total(jnp.stack([mine, lax.ppermute(other, 'core', PARTNER)]))  8.99 us
    ppermute x1, starting transfers between devices, on_device(): other = lax.ppermute(mine, 'core', PARTNER)  7.16 us
    pallas_call x1, Pallas kernels, on_device(): pl.pallas_call(functools.partial(right_kernel, starts[middle + 1:], total...  3.44 us
    ppermute x2, starting transfers between devices, exchange(): from_next = lax.ppermute(to_previous, axis, backward)  2.72 us
    pallas_call x1, Pallas kernels, on_device(): pl.pallas_call(functools.partial(left_kernel, starts[:middle], total_cols...  2.65 us
    pallas_call x1, Pallas kernels, on_device(): pl.pallas_call(functools.partial(finish_kernel, senders), out_shape=tuple...  2.17 us
  transfers between devices with their start and end apart: 6, of which 2 were waited for; matrix products, arithmetic and copies ran while one was open for 2% of the time, Pallas kernels for 5%

profile of v9, /device:TPU:1, one launch (start us, length us, event | category | flops | bytes accessed | tf_op | source)
XLA Modules:
  0.0 97.4 jit_solution(13287445787483725461)
XLA Ops:
  0.6 0.0 copy-start
  0.6 0.9 slice_bitcast_fusion.2
  1.5 0.0 copy-start.3
  1.5 0.0 copy-start.4
  1.5 1.4 %collective-permute-start.1 = (bf16[16,8,256]{2,1,0:T(8,128)(2,1)S(1)}, bf16[16,8,256]{2,1,0:T(8,128)(2,1)S(1)}, u32[]{:S(2)}, u32[]{:S(2)}) collective-permute-start(bf16[16,8,256]{2,1,0:T(8,128)(2,1)S(1)} %pad_maximum_fusion.4), channel_id=1, source_target_pairs={{32,0},{64,32},{96,64},{33,1},{65,33},{97,65},{34,2},{66,34},{98,6... | collective-permute-start | bytes 196616 | tf_op jit(solution)/shard_map/ppermute | solution.py:37
  3.0 0.0 copy-start.1
  3.0 5.6 %collective-permute-start = (bf16[16,8,256]{2,1,0:T(8,128)(2,1)S(1)}, bf16[16,8,256]{2,1,0:T(8,128)(2,1)S(1)}, u32[]{:S(2)}, u32[]{:S(2)}) collective-permute-start(bf16[16,8,256]{2,1,0:T(8,128)(2,1)S(1)} %pad_maximum_fusion.3), channel_id=1, source_target_pairs={{0,32},{32,64},{64,96},{1,33},{33,65},{65,97},{2,34},{34,66},{66,9... | collective-permute-start | bytes 196616 | tf_op jit(solution)/shard_map/ppermute | solution.py:36
  8.6 0.0 copy-done.3
  8.6 0.0 copy-done.4
  8.6 0.1 copy_bitcast_fusion
  8.7 0.0 copy-start.2
  9.4 0.0 copy-done
  9.5 0.1 fusion.5
  9.6 0.1 stack.22.place_ref
  9.7 0.0 copy-done.1
  9.7 0.0 copy-done.2
  9.7 1.2 %early.1 = (bf16[8,32,256]{2,1,0:T(8,128)(2,1)S(1)}, bf16[8,32,256]{2,1,0:T(8,128)(2,1)S(1)}, bf16[8,32,256]{2,1,0:T(8,128)(2,1)S(1)}, bf16[8,32,256]{2,1,0:T(8,...) custom-call(s32[5]{0:T(128)S(1)} %stack.22.place_ref, ...), custom_call_target="tpu_custom_call" | custom-call | flops 700000000 | bytes 3000000 | tf_op jit(solution)/shard_map/early/pallas_call | solution.py:526
  10.9 0.0 collective-permute-done.1
  11.0 0.0 collective-permute-done
  11.1 1.3 %collective-permute-start.2 = (bf16[9,48,256]{2,1,0:T(8,128)(2,1)S(1)}, bf16[9,48,256]{2,1,0:T(8,128)(2,1)S(1)}, u32[]{:S(2)}, u32[]{:S(2)}) collective-permute-start(bf16[9,48,256]{2,1,0:T(8,128)(2,1)S(1)} %pad_maximum_fusion.1), channel_id=1, source_target_pairs={{1,0},{2,1},{3,2},{4,3},{5,4},{6,5},{7,6},{8,7},{9,8},{10,9},{11,1... | collective-permute-start | bytes 663560 | tf_op jit(solution)/shard_map/ppermute | solution.py:37
  12.4 4.0 %collective-permute-start.3 = (bf16[9,48,256]{2,1,0:T(8,128)(2,1)S(1)}, bf16[9,48,256]{2,1,0:T(8,128)(2,1)S(1)}, u32[]{:S(2)}, u32[]{:S(2)}) collective-permute-start(bf16[9,48,256]{2,1,0:T(8,128)(2,1)S(1)} %pad_maximum_fusion.2), channel_id=1, source_target_pairs={{0,1},{1,2},{2,3},{3,4},{4,5},{5,6},{6,7},{7,8},{8,9},{9,10},{10,1... | collective-permute-start | bytes 663560 | tf_op jit(solution)/shard_map/ppermute | solution.py:36
  16.5 1.4 %own.1 = (bf16[8,48,256]{2,1,0:T(8,128)(2,1)S(1)}, bf16[8,48,256]{2,1,0:T(8,128)(2,1)S(1)}, bf16[8,48,256]{2,1,0:T(8,128)(2,1)S(1)}, bf16[8,48,256]{2,1,0:T(8,12...) custom-call(bf16[8,48,256]{2,1,0:T(8,128)(2,1)S(1)} %get-tuple-eleme, ...), custom_call_target="tpu_custom_call" | custom-call | flops 1000000000 | bytes 3000000 | tf_op jit(solution)/shard_map/own/pallas_call | solution.py:535
  17.9 1.4 %collective-permute-done.3.side_ref = bf16[9,48,256]{2,1,0:T(8,128)(2,1)S(1)} collective-permute-done((bf16[9,48,256]{2,1,0:T(8,128)(2,1)S(1)}, bf16[9,48,256]{2,1,0:T(8,128)(2,1)S(1)}, u32[]{:S(2)}, u32[]{:S(2)}) %collective-permute-start.3) | collective-permute-done | bytes 221216 | tf_op jit(solution)/shard_map/ppermute | solution.py:36
  19.3 2.7 %left.1 = (bf16[3,32,256]{2,1,0:T(8,128)(2,1)S(1)}, f32[3,32,256]{2,1,0:T(8,128)S(1)}, f32[8,32,256]{2,1,0:T(8,128)S(1)}, f32[8,32,256]{2,1,0:T(8,128)S(1)}) custom-call(s32[5]{0:T(128)S(1)} %stack.22.place_ref, bf16[9,48,256]{2,1,0:T(8,128)(2,1)S(1)} %collective-permute-done.3.side_ref, f32[1,256]{1,0:T(1,128)S(1)} %bitcast.52, ...), custom_call_target="tpu_custom_call" | custom-call | flops 2000000000 | bytes 2000000 | tf_op jit(solution)/shard_map/left/pallas_call | solution.py:552
  22.0 0.0 collective-permute-done.2.side_ref
  22.0 3.4 %right.1 = (bf16[8,32,256]{2,1,0:T(8,128)(2,1)S(1)}, bf16[8,32,256]{2,1,0:T(8,128)(2,1)S(1)}, bf16[1152,128]{1,0:T(8,128)(2,1)S(1)}, bf16[1152,128]{1,0:T(8,128)(2,1)S(1)}) custom-call(s32[5]{0:T(128)S(1)} %stack.22.place_ref, bf16[8,48,256]{2,1,0:T(8,128)(2,1)S(1)} %get-tuple-element.81.tok_ref, bf16[8,48,256]{2,1,0:T(8,128)(2,1)S(1)} %get-tuple-element.80.cot_ref, ...), custom_call_target="tpu_custom_call" | custom-call | flops 3000000000 | bytes 3000000 | tf_op jit(solution)/shard_map/right/pallas_call | solution.py:564
  25.4 9.0 %collective-permute-start.4 = (bf16[1152,128]{1,0:T(8,128)(2,1)S(1)}, bf16[1152,128]{1,0:T(8,128)(2,1)S(1)}, u32[]{:S(2)}, u32[]{:S(2)}) collective-permute-start(bf16[1152,128]{1,0:T(8,128)(2,1)S(1)} %get-tuple-element.57), channel_id=1, source_target_pairs={{0,128},{128,0},{1,129},{129,1},{2,130},{130,2},{3,131},{131,3},{4... | collective-permute-start | bytes 884744 | tf_op jit(solution)/shard_map/ppermute | solution.py:633
  34.4 1.2 %collective-permute-done.4 = bf16[1152,128]{1,0:T(8,128)(2,1)S(1)} collective-permute-done((bf16[1152,128]{1,0:T(8,128)(2,1)S(1)}, bf16[1152,128]{1,0:T(8,128)(2,1)S(1)}, u32[]{:S(2)}, u32[]{:S(2)}) %collective-permute-start.4) | collective-permute-done | bytes 294944 | tf_op jit(solution)/shard_map/ppermute | solution.py:633
  35.6 0.1 reduce_sum.34
  35.7 17.5 %all_to_all.15 = bf16[32,9,4,128]{3,2,1,0:T(4,128)(2,1)S(1)} all-to-all(bf16[32,9,4,128]{3,2,1,0:T(4,128)(2,1)S(1)} %bitcast.54), channel_id=1, replica_groups=mesh['zone'=2,'core'=2,'row'=4,'col'=32] {'col'}, dimensions={0} | all-to-all | bytes 589824 | tf_op jit(solution)/shard_map/all_to_all | solution.py:620
  53.2 0.1 reduce_sum.35
  53.3 16.5 %all_to_all.16 = bf16[8,9,4,128]{3,2,1,0:T(4,128)(2,1)S(1)} all-to-all(bf16[8,9,4,128]{3,2,1,0:T(4,128)(2,1)S(1)} %broadcast_in_dim.10), channel_id=1, replica_groups=mesh['zone'=2,'core'=2,'row'=4,'col'=32] {'zone','row'}, dimensions={0} | all-to-all | bytes 147456 | tf_op jit(solution)/shard_map/all_to_all | solution.py:620
  69.9 0.1 broadcast_in_dim.22
  70.0 16.6 %all_to_all.17 = bf16[32,9,4,128]{3,2,1,0:T(4,128)(2,1)S(1)} all-to-all(bf16[32,9,4,128]{3,2,1,0:T(4,128)(2,1)S(1)} %broadcast_in_dim.22), channel_id=1, replica_groups=mesh['zone'=2,'core'=2,'row'=4,'col'=32] {'col'}, dimensions={0} | all-to-all | bytes 589824 | tf_op jit(solution)/shard_map/all_to_all | solution.py:620
  86.6 7.2 %collective-permute-start.5 = (bf16[1152,128]{1,0:T(8,128)(2,1)S(1)}, bf16[1152,128]{1,0:T(8,128)(2,1)S(1)}, u32[]{:S(2)}, u32[]{:S(2)}) collective-permute-start(bf16[1152,128]{1,0:T(8,128)(2,1)S(1)} %bitcast.46), channel_id=1, source_target_pairs={{0,128},{128,0},{1,129},{129,1},{2,130},{130,2},{3,131},{131,3},{4... | collective-permute-start | bytes 884744 | tf_op jit(solution)/shard_map/ppermute | solution.py:601
  93.8 0.7 copy.28
  94.5 0.7 copy.29
  95.2 0.0 collective-permute-done.5.other_ref
  95.2 2.2 %finish.1 = (f32[256,768]{1,0:T(8,128)}, f32[256,256]{1,0:T(8,128)}, f32[256,256]{1,0:T(8,128)}) custom-call(s32[5]{0:T(128)S(1)} %stack.22.place_ref, bf16[1152,128]{1,0:T(8,128)(2,1)S(1)} %bitcast.47, bf16[1152,128]{1,0:T(8,128)(2,1)S(1)} %collective-permute-done.5.other_ref), custom_call_target="tpu_custom_call" | custom-call | flops 200000000 | bytes 2000000 | tf_op jit(solution)/shard_map/finish/pallas_call | solution.py:605
  (15 shorter events, 0.3 us)
Async XLA Ops:
  0.6 8.8 %copy-start = (bf16[256,256]{1,0:T(8,128)(2,1)S(1)}, bf16[256,256]{1,0:T(8,128)(2,1)}, u32[]{:S(2)}) copy-start(bf16[256,256]{1,0:T(8,128)(2,1)} %param.11) | copy-start | bytes 393220
  1.5 7.1 %copy-start.3 = (bf16[1,32,8,256]{3,2,1,0:T(8,128)(2,1)S(1)}, bf16[1,32,8,256]{3,2,1,0:T(8,128)(2,1)}, u32[]{:S(2)}) copy-start(bf16[1,32,8,256]{3,2,1,0:T(8,128)(2,1)} %param.8) | copy-start | bytes 393220
  1.5 7.1 %copy-start.4 = (bf16[1,32,8,256]{3,2,1,0:T(8,128)(2,1)S(1)}, bf16[1,32,8,256]{3,2,1,0:T(8,128)(2,1)}, u32[]{:S(2)}) copy-start(bf16[1,32,8,256]{3,2,1,0:T(8,128)(2,1)} %param.6) | copy-start | bytes 393220
  1.5 9.4 %collective-permute-start.1 = (bf16[16,8,256]{2,1,0:T(8,128)(2,1)S(1)}, bf16[16,8,256]{2,1,0:T(8,128)(2,1)S(1)}, u32[]{:S(2)}, u32[]{:S(2)}) collective-permute-start(bf16[16,8,256]{2,1,0:T(8,128)(2,1)S(1)} %pad_maximum_fusion.4), channel_id=1, source_target_pairs={{32,0},{64,32},{96,64},{33,1},{65,33},{97,65},{34,2},{66,34},{98,6... | collective-permute-start | bytes 196616 | tf_op jit(solution)/shard_map/ppermute | solution.py:37
  3.0 6.7 %copy-start.1 = (bf16[256,768]{1,0:T(8,128)(2,1)S(1)}, bf16[256,768]{1,0:T(8,128)(2,1)}, u32[]{:S(2)}) copy-start(bf16[256,768]{1,0:T(8,128)(2,1)} %qkv_ref.7) | copy-start | bytes 1179652
  3.0 8.0 %collective-permute-start = (bf16[16,8,256]{2,1,0:T(8,128)(2,1)S(1)}, bf16[16,8,256]{2,1,0:T(8,128)(2,1)S(1)}, u32[]{:S(2)}, u32[]{:S(2)}) collective-permute-start(bf16[16,8,256]{2,1,0:T(8,128)(2,1)S(1)} %pad_maximum_fusion.3), channel_id=1, source_target_pairs={{0,32},{32,64},{64,96},{1,33},{33,65},{65,97},{2,34},{34,66},{66,9... | collective-permute-start | bytes 196616 | tf_op jit(solution)/shard_map/ppermute | solution.py:36
  8.7 1.1 %copy-start.2 = (bf16[256,256]{1,0:T(8,128)(2,1)S(1)}, bf16[256,256]{1,0:T(8,128)(2,1)}, u32[]{:S(2)}) copy-start(bf16[256,256]{1,0:T(8,128)(2,1)} %out_ref.7) | copy-start | bytes 393220
  11.1 10.8 %collective-permute-start.2 = (bf16[9,48,256]{2,1,0:T(8,128)(2,1)S(1)}, bf16[9,48,256]{2,1,0:T(8,128)(2,1)S(1)}, u32[]{:S(2)}, u32[]{:S(2)}) collective-permute-start(bf16[9,48,256]{2,1,0:T(8,128)(2,1)S(1)} %pad_maximum_fusion.1), channel_id=1, source_target_pairs={{1,0},{2,1},{3,2},{4,3},{5,4},{6,5},{7,6},{8,7},{9,8},{10,9},{11,1... | collective-permute-start | bytes 663560 | tf_op jit(solution)/shard_map/ppermute | solution.py:37
  12.4 6.9 %collective-permute-start.3 = (bf16[9,48,256]{2,1,0:T(8,128)(2,1)S(1)}, bf16[9,48,256]{2,1,0:T(8,128)(2,1)S(1)}, u32[]{:S(2)}, u32[]{:S(2)}) collective-permute-start(bf16[9,48,256]{2,1,0:T(8,128)(2,1)S(1)} %pad_maximum_fusion.2), channel_id=1, source_target_pairs={{0,1},{1,2},{2,3},{3,4},{4,5},{5,6},{6,7},{7,8},{8,9},{9,10},{10,1... | collective-permute-start | bytes 663560 | tf_op jit(solution)/shard_map/ppermute | solution.py:36
  25.4 10.2 %collective-permute-start.4 = (bf16[1152,128]{1,0:T(8,128)(2,1)S(1)}, bf16[1152,128]{1,0:T(8,128)(2,1)S(1)}, u32[]{:S(2)}, u32[]{:S(2)}) collective-permute-start(bf16[1152,128]{1,0:T(8,128)(2,1)S(1)} %get-tuple-element.57), channel_id=1, source_target_pairs={{0,128},{128,0},{1,129},{129,1},{2,130},{130,2},{3,131},{131,3},{4... | collective-permute-start | bytes 884744 | tf_op jit(solution)/shard_map/ppermute | solution.py:633
  86.6 8.6 %collective-permute-start.5 = (bf16[1152,128]{1,0:T(8,128)(2,1)S(1)}, bf16[1152,128]{1,0:T(8,128)(2,1)S(1)}, u32[]{:S(2)}, u32[]{:S(2)}) collective-permute-start(bf16[1152,128]{1,0:T(8,128)(2,1)S(1)} %bitcast.46), channel_id=1, source_target_pairs={{0,128},{128,0},{1,129},{129,1},{2,130},{130,2},{3,131},{131,3},{4... | collective-permute-start | bytes 884744 | tf_op jit(solution)/shard_map/ppermute | solution.py:601

commit v10 on v8

--- a/solution.py
+++ b/solution.py
@@ -203,9 +203,18 @@
     col_first = place_ref[1]
     left = starts[0] == 0
     pixels = side_ref[:REACH].astype(jnp.float32).reshape(REACH * rows, width)
-    _, _, query, key, value, _ = projected(pixels, adaptive_ref[...], qkv_ref, average_matrix(width))
-    for ref, values in zip(side, (query, key, value)):
+    average = average_matrix(width)
+    _, normed = normalized(pixels, adaptive_ref[...])
+    project = nn(normed, qkv_ref[:, width:])
+    key_raw = project[:, :width]
+    key = key_raw * lax.rsqrt(head_mean(key_raw * key_raw, average) + epsilon)
+    for ref, values in zip(side[1:3], (key, project[:, width:])):
         ref[...] = values.astype(jnp.bfloat16).reshape(REACH, rows, width)
+    asking = slice((REACH - RADIUS) * rows, REACH * rows) if left else slice(0, RADIUS * rows)
+    query_raw = nn(normed[asking], qkv_ref[:, :width])
+    query_inv = lax.rsqrt(head_mean(query_raw * query_raw, average) + epsilon)
+    query = query_raw * query_inv * (score_scale / HEAD_DIM)
+    side[0][...] = query.astype(jnp.bfloat16).reshape(RADIUS, rows, width)
     grad = nt(side_ref[REACH:].reshape(RADIUS * rows, width), out_ref[...])
     side[3][...] = grad.astype(jnp.bfloat16).reshape(RADIUS, rows, width)
 
@@ -512,7 +521,8 @@
         jax.ShapeDtypeStruct((third, height, width), jnp.bfloat16),
         jax.ShapeDtypeStruct((third, height, width), jnp.float32),
     )
-    side = [pltpu.VMEM((REACH, rows, width), jnp.bfloat16)] * 3 + [pltpu.VMEM((RADIUS, rows, width), jnp.bfloat16)]
+    near, far = (pltpu.VMEM((count, rows, width), jnp.bfloat16) for count in (RADIUS, REACH))
+    side = [near, far, far, near]
     from_left = pl.pallas_call(
         functools.partial(left_kernel, starts[:middle], total_cols),
         out_shape=part + (exact,) * 2,

time: 97.7 us -> 97.6 us (level)
  no operation moved by 1% of the time
where the time goes in v10:
time: 97.6 us; the launch traced here: 97.2 us
  blocking collectives  51.1 us (52%)
  starting transfers between devices  29 us (30%)
  Pallas kernels  10.1 us (10%)
  local copies, waits for them, and re-layouts  2.73 us (3%)
  waiting for transfers between devices  2.1 us (2%)
  between operations  1.55 us (2%)
    all_to_all x3, blocking collectives, swap(): return lax.all_to_all(pieces, axes, 0, 0, tiled=True)  51.1 us
    ppermute x2, starting transfers between devices, exchange(): from_previous = lax.ppermute(to_next, axis, forward)  9.58 us
    ppermute x1, starting transfers between devices, summed(): mine = total(jnp.stack([mine, lax.ppermute(other, 'core', PARTNER)]))  9.56 us
    ppermute x1, starting transfers between devices, on_device(): other = lax.ppermute(mine, 'core', PARTNER)  7.16 us
    pallas_call x1, Pallas kernels, on_device(): pl.pallas_call(functools.partial(right_kernel, starts[middle + 1:], total...  3.27 us
    ppermute x2, starting transfers between devices, exchange(): from_next = lax.ppermute(to_previous, axis, backward)  2.72 us
    pallas_call x1, Pallas kernels, on_device(): pl.pallas_call(functools.partial(left_kernel, starts[:middle], total_cols...  2.61 us
    pallas_call x1, Pallas kernels, on_device(): pl.pallas_call(functools.partial(finish_kernel, senders), out_shape=tuple...  2.17 us
  transfers between devices with their start and end apart: 6, of which 3 were waited for; matrix products, arithmetic and copies ran while one was open for 2% of the time, Pallas kernels for 5%

profile of v10, /device:TPU:1, one launch (start us, length us, event | category | flops | bytes accessed | tf_op | source)
XLA Modules:
  0.0 97.2 jit_solution(4002605596785384423)
XLA Ops:
  0.6 0.0 copy-start
  0.6 0.9 slice_bitcast_fusion.2
  1.5 0.0 copy-start.3
  1.5 0.0 copy-start.4
  1.5 1.4 %collective-permute-start.1 = (bf16[16,8,256]{2,1,0:T(8,128)(2,1)S(1)}, bf16[16,8,256]{2,1,0:T(8,128)(2,1)S(1)}, u32[]{:S(2)}, u32[]{:S(2)}) collective-permute-start(bf16[16,8,256]{2,1,0:T(8,128)(2,1)S(1)} %pad_maximum_fusion.4), channel_id=1, source_target_pairs={{32,0},{64,32},{96,64},{33,1},{65,33},{97,65},{34,2},{66,34},{98,6... | collective-permute-start | bytes 196616 | tf_op jit(solution)/shard_map/ppermute | solution.py:37
  3.0 5.4 %collective-permute-start = (bf16[16,8,256]{2,1,0:T(8,128)(2,1)S(1)}, bf16[16,8,256]{2,1,0:T(8,128)(2,1)S(1)}, u32[]{:S(2)}, u32[]{:S(2)}) collective-permute-start(bf16[16,8,256]{2,1,0:T(8,128)(2,1)S(1)} %pad_maximum_fusion.3), channel_id=1, source_target_pairs={{0,32},{32,64},{64,96},{1,33},{33,65},{65,97},{2,34},{34,66},{66,9... | collective-permute-start | bytes 196616 | tf_op jit(solution)/shard_map/ppermute | solution.py:36
  8.4 0.0 copy-done.3
  8.5 0.0 copy-done.4
  8.5 0.1 copy_bitcast_fusion
  9.2 0.0 copy-done
  9.3 0.1 fusion.5
  9.4 0.1 stack.22.place_ref
  9.5 0.0 collective-permute-done.1
  9.6 0.2 collective-permute-done
  9.9 1.3 %collective-permute-start.2 = (bf16[9,48,256]{2,1,0:T(8,128)(2,1)S(1)}, bf16[9,48,256]{2,1,0:T(8,128)(2,1)S(1)}, u32[]{:S(2)}, u32[]{:S(2)}) collective-permute-start(bf16[9,48,256]{2,1,0:T(8,128)(2,1)S(1)} %pad_maximum_fusion.1), channel_id=1, source_target_pairs={{1,0},{2,1},{3,2},{4,3},{5,4},{6,5},{7,6},{8,7},{9,8},{10,9},{11,1... | collective-permute-start | bytes 663560 | tf_op jit(solution)/shard_map/ppermute | solution.py:37
  11.2 0.0 copy-start.1
  11.2 0.0 copy-start.2
  11.2 4.1 %collective-permute-start.3 = (bf16[9,48,256]{2,1,0:T(8,128)(2,1)S(1)}, bf16[9,48,256]{2,1,0:T(8,128)(2,1)S(1)}, u32[]{:S(2)}, u32[]{:S(2)}) collective-permute-start(bf16[9,48,256]{2,1,0:T(8,128)(2,1)S(1)} %pad_maximum_fusion.2), channel_id=1, source_target_pairs={{0,1},{1,2},{2,3},{3,4},{4,5},{5,6},{6,7},{7,8},{8,9},{9,10},{10,1... | collective-permute-start | bytes 663560 | tf_op jit(solution)/shard_map/ppermute | solution.py:36
  15.4 0.0 copy-done.1
  15.4 0.0 copy-done.2
  15.4 2.1 %own.1 = (bf16[8,48,256]{2,1,0:T(8,128)(2,1)S(1)}, bf16[8,48,256]{2,1,0:T(8,128)(2,1)S(1)}, bf16[8,48,256]{2,1,0:T(8,128)(2,1)S(1)}, bf16[8,48,256]{2,1,0:T(8,12...) custom-call(s32[5]{0:T(128)S(1)} %stack.22.place_ref, ...), custom_call_target="tpu_custom_call" | custom-call | flops 1000000000 | bytes 4000000 | tf_op jit(solution)/shard_map/own/pallas_call | solution.py:507
  17.5 0.7 collective-permute-done.3.side_ref
  18.2 2.6 %left.1 = (bf16[3,32,256]{2,1,0:T(8,128)(2,1)S(1)}, f32[3,32,256]{2,1,0:T(8,128)S(1)}, f32[8,32,256]{2,1,0:T(8,128)S(1)}, f32[8,32,256]{2,1,0:T(8,128)S(1)}) custom-call(s32[5]{0:T(128)S(1)} %stack.22.place_ref, bf16[9,48,256]{2,1,0:T(8,128)(2,1)S(1)} %collective-permute-done.3.side_ref, f32[1,256]{1,0:T(1,128)S(1)} %bitcast.51, ...), custom_call_target="tpu_custom_call" | custom-call | flops 2000000000 | bytes 2000000 | tf_op jit(solution)/shard_map/left/pallas_call | solution.py:526
  20.9 0.0 collective-permute-done.2.side_ref
  20.9 3.3 %right.1 = (bf16[8,32,256]{2,1,0:T(8,128)(2,1)S(1)}, bf16[8,32,256]{2,1,0:T(8,128)(2,1)S(1)}, bf16[1152,128]{1,0:T(8,128)(2,1)S(1)}, bf16[1152,128]{1,0:T(8,128)(2,1)S(1)}) custom-call(s32[5]{0:T(128)S(1)} %stack.22.place_ref, bf16[8,48,256]{2,1,0:T(8,128)(2,1)S(1)} %get-tuple-element.73.tok_ref, bf16[8,48,256]{2,1,0:T(8,128)(2,1)S(1)} %get-tuple-element.72.cot_ref, ...), custom_call_target="tpu_custom_call" | custom-call | flops 3000000000 | bytes 3000000 | tf_op jit(solution)/shard_map/right/pallas_call | solution.py:538
  24.1 9.6 %collective-permute-start.4 = (bf16[1152,128]{1,0:T(8,128)(2,1)S(1)}, bf16[1152,128]{1,0:T(8,128)(2,1)S(1)}, u32[]{:S(2)}, u32[]{:S(2)}) collective-permute-start(bf16[1152,128]{1,0:T(8,128)(2,1)S(1)} %get-tuple-element.49), channel_id=1, source_target_pairs={{0,128},{128,0},{1,129},{129,1},{2,130},{130,2},{3,131},{131,3},{4... | collective-permute-start | bytes 884744 | tf_op jit(solution)/shard_map/ppermute | solution.py:607
  33.7 1.2 %collective-permute-done.4 = bf16[1152,128]{1,0:T(8,128)(2,1)S(1)} collective-permute-done((bf16[1152,128]{1,0:T(8,128)(2,1)S(1)}, bf16[1152,128]{1,0:T(8,128)(2,1)S(1)}, u32[]{:S(2)}, u32[]{:S(2)}) %collective-permute-start.4) | collective-permute-done | bytes 294944 | tf_op jit(solution)/shard_map/ppermute | solution.py:607
  34.9 0.1 reduce_sum.34
  35.0 16.9 %all_to_all.15 = bf16[32,9,4,128]{3,2,1,0:T(4,128)(2,1)S(1)} all-to-all(bf16[32,9,4,128]{3,2,1,0:T(4,128)(2,1)S(1)} %bitcast.53), channel_id=1, replica_groups=mesh['zone'=2,'core'=2,'row'=4,'col'=32] {'col'}, dimensions={0} | all-to-all | bytes 589824 | tf_op jit(solution)/shard_map/all_to_all | solution.py:594
  51.9 0.1 reduce_sum.35
  52.0 17.6 %all_to_all.16 = bf16[8,9,4,128]{3,2,1,0:T(4,128)(2,1)S(1)} all-to-all(bf16[8,9,4,128]{3,2,1,0:T(4,128)(2,1)S(1)} %broadcast_in_dim.10), channel_id=1, replica_groups=mesh['zone'=2,'core'=2,'row'=4,'col'=32] {'zone','row'}, dimensions={0} | all-to-all | bytes 147456 | tf_op jit(solution)/shard_map/all_to_all | solution.py:594
  69.7 0.1 broadcast_in_dim.22
  69.7 16.6 %all_to_all.17 = bf16[32,9,4,128]{3,2,1,0:T(4,128)(2,1)S(1)} all-to-all(bf16[32,9,4,128]{3,2,1,0:T(4,128)(2,1)S(1)} %broadcast_in_dim.22), channel_id=1, replica_groups=mesh['zone'=2,'core'=2,'row'=4,'col'=32] {'col'}, dimensions={0} | all-to-all | bytes 589824 | tf_op jit(solution)/shard_map/all_to_all | solution.py:594
  86.4 7.2 %collective-permute-start.5 = (bf16[1152,128]{1,0:T(8,128)(2,1)S(1)}, bf16[1152,128]{1,0:T(8,128)(2,1)S(1)}, u32[]{:S(2)}, u32[]{:S(2)}) collective-permute-start(bf16[1152,128]{1,0:T(8,128)(2,1)S(1)} %bitcast.46), channel_id=1, source_target_pairs={{0,128},{128,0},{1,129},{129,1},{2,130},{130,2},{3,131},{131,3},{4... | collective-permute-start | bytes 884744 | tf_op jit(solution)/shard_map/ppermute | solution.py:575
  93.6 0.7 copy.28
  94.3 0.7 copy.29
  95.0 0.0 collective-permute-done.5.other_ref
  95.0 2.2 %finish.1 = (f32[256,768]{1,0:T(8,128)}, f32[256,256]{1,0:T(8,128)}, f32[256,256]{1,0:T(8,128)}) custom-call(s32[5]{0:T(128)S(1)} %stack.22.place_ref, bf16[1152,128]{1,0:T(8,128)(2,1)S(1)} %bitcast.47, bf16[1152,128]{1,0:T(8,128)(2,1)S(1)} %collective-permute-done.5.other_ref), custom_call_target="tpu_custom_call" | custom-call | flops 200000000 | bytes 2000000 | tf_op jit(solution)/shard_map/finish/pallas_call | solution.py:579
  (15 shorter events, 0.3 us)
Async XLA Ops:
  0.6 8.6 %copy-start = (bf16[256,256]{1,0:T(8,128)(2,1)S(1)}, bf16[256,256]{1,0:T(8,128)(2,1)}, u32[]{:S(2)}) copy-start(bf16[256,256]{1,0:T(8,128)(2,1)} %param.11) | copy-start | bytes 393220
  1.5 6.9 %copy-start.3 = (bf16[1,32,8,256]{3,2,1,0:T(8,128)(2,1)S(1)}, bf16[1,32,8,256]{3,2,1,0:T(8,128)(2,1)}, u32[]{:S(2)}) copy-start(bf16[1,32,8,256]{3,2,1,0:T(8,128)(2,1)} %param.8) | copy-start | bytes 393220
  1.5 6.9 %copy-start.4 = (bf16[1,32,8,256]{3,2,1,0:T(8,128)(2,1)S(1)}, bf16[1,32,8,256]{3,2,1,0:T(8,128)(2,1)}, u32[]{:S(2)}) copy-start(bf16[1,32,8,256]{3,2,1,0:T(8,128)(2,1)} %param.6) | copy-start | bytes 393220
  1.5 8.0 %collective-permute-start.1 = (bf16[16,8,256]{2,1,0:T(8,128)(2,1)S(1)}, bf16[16,8,256]{2,1,0:T(8,128)(2,1)S(1)}, u32[]{:S(2)}, u32[]{:S(2)}) collective-permute-start(bf16[16,8,256]{2,1,0:T(8,128)(2,1)S(1)} %pad_maximum_fusion.4), channel_id=1, source_target_pairs={{32,0},{64,32},{96,64},{33,1},{65,33},{97,65},{34,2},{66,34},{98,6... | collective-permute-start | bytes 196616 | tf_op jit(solution)/shard_map/ppermute | solution.py:37
  3.0 6.8 %collective-permute-start = (bf16[16,8,256]{2,1,0:T(8,128)(2,1)S(1)}, bf16[16,8,256]{2,1,0:T(8,128)(2,1)S(1)}, u32[]{:S(2)}, u32[]{:S(2)}) collective-permute-start(bf16[16,8,256]{2,1,0:T(8,128)(2,1)S(1)} %pad_maximum_fusion.3), channel_id=1, source_target_pairs={{0,32},{32,64},{64,96},{1,33},{33,65},{65,97},{2,34},{34,66},{66,9... | collective-permute-start | bytes 196616 | tf_op jit(solution)/shard_map/ppermute | solution.py:36
  9.9 11.0 %collective-permute-start.2 = (bf16[9,48,256]{2,1,0:T(8,128)(2,1)S(1)}, bf16[9,48,256]{2,1,0:T(8,128)(2,1)S(1)}, u32[]{:S(2)}, u32[]{:S(2)}) collective-permute-start(bf16[9,48,256]{2,1,0:T(8,128)(2,1)S(1)} %pad_maximum_fusion.1), channel_id=1, source_target_pairs={{1,0},{2,1},{3,2},{4,3},{5,4},{6,5},{7,6},{8,7},{9,8},{10,9},{11,1... | collective-permute-start | bytes 663560 | tf_op jit(solution)/shard_map/ppermute | solution.py:37
  11.2 4.2 %copy-start.1 = (bf16[256,768]{1,0:T(8,128)(2,1)S(1)}, bf16[256,768]{1,0:T(8,128)(2,1)}, u32[]{:S(2)}) copy-start(bf16[256,768]{1,0:T(8,128)(2,1)} %qkv_ref.5) | copy-start | bytes 1179652
  11.2 4.2 %copy-start.2 = (bf16[256,256]{1,0:T(8,128)(2,1)S(1)}, bf16[256,256]{1,0:T(8,128)(2,1)}, u32[]{:S(2)}) copy-start(bf16[256,256]{1,0:T(8,128)(2,1)} %out_ref.5) | copy-start | bytes 393220
  11.2 7.0 %collective-permute-start.3 = (bf16[9,48,256]{2,1,0:T(8,128)(2,1)S(1)}, bf16[9,48,256]{2,1,0:T(8,128)(2,1)S(1)}, u32[]{:S(2)}, u32[]{:S(2)}) collective-permute-start(bf16[9,48,256]{2,1,0:T(8,128)(2,1)S(1)} %pad_maximum_fusion.2), channel_id=1, source_target_pairs={{0,1},{1,2},{2,3},{3,4},{4,5},{5,6},{6,7},{7,8},{8,9},{9,10},{10,1... | collective-permute-start | bytes 663560 | tf_op jit(solution)/shard_map/ppermute | solution.py:36
  24.1 10.8 %collective-permute-start.4 = (bf16[1152,128]{1,0:T(8,128)(2,1)S(1)}, bf16[1152,128]{1,0:T(8,128)(2,1)S(1)}, u32[]{:S(2)}, u32[]{:S(2)}) collective-permute-start(bf16[1152,128]{1,0:T(8,128)(2,1)S(1)} %get-tuple-element.49), channel_id=1, source_target_pairs={{0,128},{128,0},{1,129},{129,1},{2,130},{130,2},{3,131},{131,3},{4... | collective-permute-start | bytes 884744 | tf_op jit(solution)/shard_map/ppermute | solution.py:607
  86.4 8.6 %collective-permute-start.5 = (bf16[1152,128]{1,0:T(8,128)(2,1)S(1)}, bf16[1152,128]{1,0:T(8,128)(2,1)S(1)}, u32[]{:S(2)}, u32[]{:S(2)}) collective-permute-start(bf16[1152,128]{1,0:T(8,128)(2,1)S(1)} %bitcast.46), channel_id=1, source_target_pairs={{0,128},{128,0},{1,129},{129,1},{2,130},{130,2},{3,131},{131,3},{4... | collective-permute-start | bytes 884744 | tf_op jit(solution)/shard_map/ppermute | solution.py:575

commit v11 on v10

--- a/solution.py
+++ b/solution.py
@@ -460,6 +460,19 @@
 LANES = 128
 
 
+def edge_kernel(tok_ref, cot_ref, last_ref, first_ref, sems):
+    height = tok_ref.shape[0]
+    copies = []
+    for target, low in ((last_ref, height - EDGE), (first_ref, 0)):
+        for half, source in enumerate((tok_ref, cot_ref)):
+            there = target.at[pl.ds(half * EDGE, EDGE)]
+            copies.append(pltpu.make_async_copy(source.at[pl.ds(low, EDGE)], there, sems.at[len(copies)]))
+    for copy in copies:
+        copy.start()
+    for copy in copies:
+        copy.wait()
+
+
 def lying(values):
     return with_layout_constraint(values, Layout(major_to_minor=(0, 1, 2)))
 
@@ -472,11 +485,19 @@
     total_cols = cols * lax.axis_size("col")
     rows = height + 2 * EDGE
 
-    def edge_rows(low, high):
-        return lying(jnp.concatenate([tokens[0, low:high], cotangent[0, low:high]], axis=0))
-
+    message = jax.ShapeDtypeStruct((2 * EDGE, cols, width), jnp.bfloat16)
+    last_rows, first_rows = pl.pallas_call(
+        edge_kernel,
+        out_shape=(message,) * 2,
+        in_specs=[pl.BlockSpec(memory_space=pl.ANY)] * 2,
+        out_specs=(pl.BlockSpec(memory_space=pltpu.VMEM),) * 2,
+        scratch_shapes=[pltpu.SemaphoreType.DMA((4,))],
+        compiler_params=pltpu.CompilerParams(vmem_limit_bytes=8 * 2**20),
+        cost_estimate=pl.CostEstimate(flops=0, bytes_accessed=300_000, transcendentals=0),
+        name="edges",
+    )(tokens[0], cotangent[0])
     both = jnp.concatenate([tokens[0].transpose(1, 0, 2), cotangent[0].transpose(1, 0, 2)], axis=0)
-    above, below = exchange(edge_rows(height - EDGE, height), edge_rows(0, EDGE), "row")
+    above, below = exchange(lying(last_rows), lying(first_rows), "row")
     above, below = (lying(rows_).transpose(1, 0, 2).reshape(cols, 2, EDGE, width) for rows_ in (above, below))
     above, below = (rows_.transpose(1, 0, 2, 3).reshape(2 * cols, EDGE, width) for rows_ in (above, below))
     both = jnp.concatenate([both, above, below], axis=1)

time: 97.6 us -> 99.5 us (1.019)
  starting transfers between devices: 29 us -> 25.6 us
  waiting for transfers between devices: 2.1 us -> 5.14 us
  blocking collectives: 51.1 us -> 52.3 us
    ppermute x2, waiting for transfers between devices: 0.01 us -> 3.25 us  [exchange(): from_next = lax.ppermute(to_previous, axis, backward)]
    ppermute x1, starting transfers between devices: 9.56 us -> 6.87 us  [summed(): mine = total(jnp.stack([mine, lax.ppermute(other, 'core', PARTNER)]))]
    unnamed x12 -> x16, local copies, waits for them, and re-layouts: 1.5 us -> 3.33 us
    all_to_all x3, blocking collectives: 51.1 us -> 52.3 us  [swap(): return lax.all_to_all(pieces, axes, 0, 0, tiled=True)]
where the time goes in v11:
time: 99.5 us; the launch traced here: 99.1 us
  blocking collectives  52.3 us (53%)
  starting transfers between devices  25.6 us (26%)
  Pallas kernels  10.3 us (10%)
  waiting for transfers between devices  5.14 us (5%)
  local copies, waits for them, and re-layouts  3.71 us (4%)
  between operations  1.53 us (2%)
    all_to_all x3, blocking collectives, swap(): return lax.all_to_all(pieces, axes, 0, 0, tiled=True)  52.3 us
    ppermute x2, starting transfers between devices, exchange(): from_previous = lax.ppermute(to_next, axis, forward)  8.95 us
    ppermute x1, starting transfers between devices, on_device(): other = lax.ppermute(mine, 'core', PARTNER)  7.16 us
    ppermute x1, starting transfers between devices, summed(): mine = total(jnp.stack([mine, lax.ppermute(other, 'core', PARTNER)]))  6.87 us
    unnamed x16, local copies, waits for them, and re-layouts  3.33 us
    pallas_call x1, Pallas kernels, on_device(): pl.pallas_call(functools.partial(right_kernel, starts[middle + 1:], total...  3.27 us
    ppermute x2, waiting for transfers between devices, exchange(): from_next = lax.ppermute(to_previous, axis, backward)  3.25 us
    pallas_call x1, Pallas kernels, on_device(): pl.pallas_call(functools.partial(left_kernel, starts[:middle], total_cols...  2.62 us
  transfers between devices with their start and end apart: 6, of which 3 were waited for; matrix products, arithmetic and copies ran while one was open for 2% of the time, Pallas kernels for 5%

profile of v11, /device:TPU:1, one launch (start us, length us, event | category | flops | bytes accessed | tf_op | source)
XLA Modules:
  0.0 99.1 jit_solution(14108044057701790796)
XLA Ops:
  0.6 0.0 copy-start
  0.6 0.0 copy-start.1
  0.7 0.9 copy-done.1
  1.6 0.0 copy-start.3
  1.6 0.9 copy-done.3
  2.5 0.0 copy-start.2
  2.5 0.0 copy-start.4
  2.5 0.2 edges.1
  2.7 4.8 %collective-permute-start = (bf16[16,8,256]{2,1,0:T(8,128)(2,1)S(1)}, bf16[16,8,256]{2,1,0:T(8,128)(2,1)S(1)}, u32[]{:S(2)}, u32[]{:S(2)}) collective-permute-start(bf16[16,8,256]{2,1,0:T(8,128)(2,1)S(1)} %get-tuple-element.31), channel_id=1, source_target_pairs={{0,32},{32,64},{64,96},{1,33},{33,65},{65,97},{2,34},{34,66},{66,9... | collective-permute-start | bytes 196616 | tf_op jit(solution)/shard_map/ppermute | solution.py:36
  7.5 1.3 %collective-permute-start.1 = (bf16[16,8,256]{2,1,0:T(8,128)(2,1)S(1)}, bf16[16,8,256]{2,1,0:T(8,128)(2,1)S(1)}, u32[]{:S(2)}, u32[]{:S(2)}) collective-permute-start(bf16[16,8,256]{2,1,0:T(8,128)(2,1)S(1)} %get-tuple-element.32), channel_id=1, source_target_pairs={{32,0},{64,32},{96,64},{33,1},{65,33},{97,65},{34,2},{66,34},{98,6... | collective-permute-start | bytes 196616 | tf_op jit(solution)/shard_map/ppermute | solution.py:37
  8.8 0.0 copy-done.2
  8.8 0.0 copy-done.4
  8.8 0.1 copy_bitcast_fusion
  9.6 0.0 copy-done
  9.6 0.1 fusion.5
  9.8 0.1 stack.22.place_ref
  9.9 0.0 collective-permute-done
  9.9 3.2 %collective-permute-done.1 = bf16[16,8,256]{2,1,0:T(8,128)(2,1)S(1)} collective-permute-done((bf16[16,8,256]{2,1,0:T(8,128)(2,1)S(1)}, bf16[16,8,256]{2,1,0:T(8,128)(2,1)S(1)}, u32[]{:S(2)}, u32[]{:S(2)}) %collective-permute-start.1) | collective-permute-done | bytes 65568 | tf_op jit(solution)/shard_map/ppermute | solution.py:37
  13.3 1.3 %collective-permute-start.2 = (bf16[9,48,256]{2,1,0:T(8,128)(2,1)S(1)}, bf16[9,48,256]{2,1,0:T(8,128)(2,1)S(1)}, u32[]{:S(2)}, u32[]{:S(2)}) collective-permute-start(bf16[9,48,256]{2,1,0:T(8,128)(2,1)S(1)} %pad_maximum_fusion.1), channel_id=1, source_target_pairs={{1,0},{2,1},{3,2},{4,3},{5,4},{6,5},{7,6},{8,7},{9,8},{10,9},{11,1... | collective-permute-start | bytes 663560 | tf_op jit(solution)/shard_map/ppermute | solution.py:37
  14.6 0.0 copy-start.5
  14.7 0.0 copy-start.6
  14.7 4.1 %collective-permute-start.3 = (bf16[9,48,256]{2,1,0:T(8,128)(2,1)S(1)}, bf16[9,48,256]{2,1,0:T(8,128)(2,1)S(1)}, u32[]{:S(2)}, u32[]{:S(2)}) collective-permute-start(bf16[9,48,256]{2,1,0:T(8,128)(2,1)S(1)} %pad_maximum_fusion.2), channel_id=1, source_target_pairs={{0,1},{1,2},{2,3},{3,4},{4,5},{5,6},{6,7},{7,8},{8,9},{9,10},{10,1... | collective-permute-start | bytes 663560 | tf_op jit(solution)/shard_map/ppermute | solution.py:36
  18.8 0.0 copy-done.5
  18.8 0.0 copy-done.6
  18.9 2.1 %own.1 = (bf16[8,48,256]{2,1,0:T(8,128)(2,1)S(1)}, bf16[8,48,256]{2,1,0:T(8,128)(2,1)S(1)}, bf16[8,48,256]{2,1,0:T(8,128)(2,1)S(1)}, bf16[8,48,256]{2,1,0:T(8,12...) custom-call(s32[5]{0:T(128)S(1)} %stack.22.place_ref, ...), custom_call_target="tpu_custom_call" | custom-call | flops 1000000000 | bytes 4000000 | tf_op jit(solution)/shard_map/own/pallas_call | solution.py:528
  20.9 0.7 collective-permute-done.3.side_ref
  21.6 2.6 %left.1 = (bf16[3,32,256]{2,1,0:T(8,128)(2,1)S(1)}, f32[3,32,256]{2,1,0:T(8,128)S(1)}, f32[8,32,256]{2,1,0:T(8,128)S(1)}, f32[8,32,256]{2,1,0:T(8,128)S(1)}) custom-call(s32[5]{0:T(128)S(1)} %stack.22.place_ref, bf16[9,48,256]{2,1,0:T(8,128)(2,1)S(1)} %collective-permute-done.3.side_ref, f32[1,256]{1,0:T(1,128)S(1)} %bitcast.47, ...), custom_call_target="tpu_custom_call" | custom-call | flops 2000000000 | bytes 2000000 | tf_op jit(solution)/shard_map/left/pallas_call | solution.py:547
  24.3 0.0 collective-permute-done.2.side_ref
  24.3 3.3 %right.1 = (bf16[8,32,256]{2,1,0:T(8,128)(2,1)S(1)}, bf16[8,32,256]{2,1,0:T(8,128)(2,1)S(1)}, bf16[1152,128]{1,0:T(8,128)(2,1)S(1)}, bf16[1152,128]{1,0:T(8,128)(2,1)S(1)}) custom-call(s32[5]{0:T(128)S(1)} %stack.22.place_ref, bf16[8,48,256]{2,1,0:T(8,128)(2,1)S(1)} %get-tuple-element.77.tok_ref, bf16[8,48,256]{2,1,0:T(8,128)(2,1)S(1)} %get-tuple-element.76.cot_ref, ...), custom_call_target="tpu_custom_call" | custom-call | flops 3000000000 | bytes 3000000 | tf_op jit(solution)/shard_map/right/pallas_call | solution.py:559
  27.6 6.9 %collective-permute-start.4 = (bf16[1152,128]{1,0:T(8,128)(2,1)S(1)}, bf16[1152,128]{1,0:T(8,128)(2,1)S(1)}, u32[]{:S(2)}, u32[]{:S(2)}) collective-permute-start(bf16[1152,128]{1,0:T(8,128)(2,1)S(1)} %get-tuple-element.53), channel_id=1, source_target_pairs={{0,128},{128,0},{1,129},{129,1},{2,130},{130,2},{3,131},{131,3},{4... | collective-permute-start | bytes 884744 | tf_op jit(solution)/shard_map/ppermute | solution.py:628
  34.4 1.2 %collective-permute-done.4 = bf16[1152,128]{1,0:T(8,128)(2,1)S(1)} collective-permute-done((bf16[1152,128]{1,0:T(8,128)(2,1)S(1)}, bf16[1152,128]{1,0:T(8,128)(2,1)S(1)}, u32[]{:S(2)}, u32[]{:S(2)}) %collective-permute-start.4) | collective-permute-done | bytes 294944 | tf_op jit(solution)/shard_map/ppermute | solution.py:628
  35.6 0.1 reduce_sum.34
  35.7 19.8 %all_to_all.15 = bf16[32,9,4,128]{3,2,1,0:T(4,128)(2,1)S(1)} all-to-all(bf16[32,9,4,128]{3,2,1,0:T(4,128)(2,1)S(1)} %bitcast.49), channel_id=1, replica_groups=mesh['zone'=2,'core'=2,'row'=4,'col'=32] {'col'}, dimensions={0} | all-to-all | bytes 589824 | tf_op jit(solution)/shard_map/all_to_all | solution.py:615
  55.5 0.1 reduce_sum.35
  55.6 15.9 %all_to_all.16 = bf16[8,9,4,128]{3,2,1,0:T(4,128)(2,1)S(1)} all-to-all(bf16[8,9,4,128]{3,2,1,0:T(4,128)(2,1)S(1)} %broadcast_in_dim.10), channel_id=1, replica_groups=mesh['zone'=2,'core'=2,'row'=4,'col'=32] {'zone','row'}, dimensions={0} | all-to-all | bytes 147456 | tf_op jit(solution)/shard_map/all_to_all | solution.py:615
  71.6 0.1 broadcast_in_dim.22
  71.7 16.6 %all_to_all.17 = bf16[32,9,4,128]{3,2,1,0:T(4,128)(2,1)S(1)} all-to-all(bf16[32,9,4,128]{3,2,1,0:T(4,128)(2,1)S(1)} %broadcast_in_dim.22), channel_id=1, replica_groups=mesh['zone'=2,'core'=2,'row'=4,'col'=32] {'col'}, dimensions={0} | all-to-all | bytes 589824 | tf_op jit(solution)/shard_map/all_to_all | solution.py:615
  88.3 7.2 %collective-permute-start.5 = (bf16[1152,128]{1,0:T(8,128)(2,1)S(1)}, bf16[1152,128]{1,0:T(8,128)(2,1)S(1)}, u32[]{:S(2)}, u32[]{:S(2)}) collective-permute-start(bf16[1152,128]{1,0:T(8,128)(2,1)S(1)} %bitcast.42), channel_id=1, source_target_pairs={{0,128},{128,0},{1,129},{129,1},{2,130},{130,2},{3,131},{131,3},{4... | collective-permute-start | bytes 884744 | tf_op jit(solution)/shard_map/ppermute | solution.py:596
  95.5 0.7 copy.34
  96.2 0.7 copy.35
  96.9 0.0 collective-permute-done.5.other_ref
  96.9 2.2 %finish.1 = (f32[256,768]{1,0:T(8,128)}, f32[256,256]{1,0:T(8,128)}, f32[256,256]{1,0:T(8,128)}) custom-call(s32[5]{0:T(128)S(1)} %stack.22.place_ref, bf16[1152,128]{1,0:T(8,128)(2,1)S(1)} %bitcast.43, bf16[1152,128]{1,0:T(8,128)(2,1)S(1)} %collective-permute-done.5.other_ref), custom_call_target="tpu_custom_call" | custom-call | flops 200000000 | bytes 2000000 | tf_op jit(solution)/shard_map/finish/pallas_call | solution.py:600
  (13 shorter events, 0.3 us)
Async XLA Ops:
  0.6 9.0 %copy-start = (bf16[256,256]{1,0:T(8,128)(2,1)S(1)}, bf16[256,256]{1,0:T(8,128)(2,1)}, u32[]{:S(2)}) copy-start(bf16[256,256]{1,0:T(8,128)(2,1)} %param.11) | copy-start | bytes 393220
  0.6 0.9 copy-start.1
  1.6 0.9 copy-start.3
  2.5 6.3 %copy-start.2 = (bf16[1,32,8,256]{3,2,1,0:T(8,128)(2,1)S(1)}, bf16[1,32,8,256]{3,2,1,0:T(8,128)(2,1)}, u32[]{:S(2)}) copy-start(bf16[1,32,8,256]{3,2,1,0:T(8,128)(2,1)} %param.6) | copy-start | bytes 393220
  2.5 6.3 %copy-start.4 = (bf16[1,32,8,256]{3,2,1,0:T(8,128)(2,1)S(1)}, bf16[1,32,8,256]{3,2,1,0:T(8,128)(2,1)}, u32[]{:S(2)}) copy-start(bf16[1,32,8,256]{3,2,1,0:T(8,128)(2,1)} %param.8) | copy-start | bytes 393220
  2.7 7.2 %collective-permute-start = (bf16[16,8,256]{2,1,0:T(8,128)(2,1)S(1)}, bf16[16,8,256]{2,1,0:T(8,128)(2,1)S(1)}, u32[]{:S(2)}, u32[]{:S(2)}) collective-permute-start(bf16[16,8,256]{2,1,0:T(8,128)(2,1)S(1)} %get-tuple-element.31), channel_id=1, source_target_pairs={{0,32},{32,64},{64,96},{1,33},{33,65},{65,97},{2,34},{34,66},{66,9... | collective-permute-start | bytes 196616 | tf_op jit(solution)/shard_map/ppermute | solution.py:36
  7.5 5.6 %collective-permute-start.1 = (bf16[16,8,256]{2,1,0:T(8,128)(2,1)S(1)}, bf16[16,8,256]{2,1,0:T(8,128)(2,1)S(1)}, u32[]{:S(2)}, u32[]{:S(2)}) collective-permute-start(bf16[16,8,256]{2,1,0:T(8,128)(2,1)S(1)} %get-tuple-element.32), channel_id=1, source_target_pairs={{32,0},{64,32},{96,64},{33,1},{65,33},{97,65},{34,2},{66,34},{98,6... | collective-permute-start | bytes 196616 | tf_op jit(solution)/shard_map/ppermute | solution.py:37
  13.3 11.0 %collective-permute-start.2 = (bf16[9,48,256]{2,1,0:T(8,128)(2,1)S(1)}, bf16[9,48,256]{2,1,0:T(8,128)(2,1)S(1)}, u32[]{:S(2)}, u32[]{:S(2)}) collective-permute-start(bf16[9,48,256]{2,1,0:T(8,128)(2,1)S(1)} %pad_maximum_fusion.1), channel_id=1, source_target_pairs={{1,0},{2,1},{3,2},{4,3},{5,4},{6,5},{7,6},{8,7},{9,8},{10,9},{11,1... | collective-permute-start | bytes 663560 | tf_op jit(solution)/shard_map/ppermute | solution.py:37
  14.6 4.2 %copy-start.5 = (bf16[256,768]{1,0:T(8,128)(2,1)S(1)}, bf16[256,768]{1,0:T(8,128)(2,1)}, u32[]{:S(2)}) copy-start(bf16[256,768]{1,0:T(8,128)(2,1)} %qkv_ref.5) | copy-start | bytes 1179652
  14.7 4.2 %copy-start.6 = (bf16[256,256]{1,0:T(8,128)(2,1)S(1)}, bf16[256,256]{1,0:T(8,128)(2,1)}, u32[]{:S(2)}) copy-start(bf16[256,256]{1,0:T(8,128)(2,1)} %out_ref.5) | copy-start | bytes 393220
  14.7 7.0 %collective-permute-start.3 = (bf16[9,48,256]{2,1,0:T(8,128)(2,1)S(1)}, bf16[9,48,256]{2,1,0:T(8,128)(2,1)S(1)}, u32[]{:S(2)}, u32[]{:S(2)}) collective-permute-start(bf16[9,48,256]{2,1,0:T(8,128)(2,1)S(1)} %pad_maximum_fusion.2), channel_id=1, source_target_pairs={{0,1},{1,2},{2,3},{3,4},{4,5},{5,6},{6,7},{7,8},{8,9},{9,10},{10,1... | collective-permute-start | bytes 663560 | tf_op jit(solution)/shard_map/ppermute | solution.py:36
  27.6 8.1 %collective-permute-start.4 = (bf16[1152,128]{1,0:T(8,128)(2,1)S(1)}, bf16[1152,128]{1,0:T(8,128)(2,1)S(1)}, u32[]{:S(2)}, u32[]{:S(2)}) collective-permute-start(bf16[1152,128]{1,0:T(8,128)(2,1)S(1)} %get-tuple-element.53), channel_id=1, source_target_pairs={{0,128},{128,0},{1,129},{129,1},{2,130},{130,2},{3,131},{131,3},{4... | collective-permute-start | bytes 884744 | tf_op jit(solution)/shard_map/ppermute | solution.py:628
  88.3 8.6 %collective-permute-start.5 = (bf16[1152,128]{1,0:T(8,128)(2,1)S(1)}, bf16[1152,128]{1,0:T(8,128)(2,1)S(1)}, u32[]{:S(2)}, u32[]{:S(2)}) collective-permute-start(bf16[1152,128]{1,0:T(8,128)(2,1)S(1)} %bitcast.42), channel_id=1, source_target_pairs={{0,128},{128,0},{1,129},{129,1},{2,130},{130,2},{3,131},{131,3},{4... | collective-permute-start | bytes 884744 | tf_op jit(solution)/shard_map/ppermute | solution.py:596
